TPU v7x, 32 devices: a whole 2x2x4 slice. The times are simulated.
32 devices in a mesh: fsdp: 8 (over y, x, core), tp: 4 (over z).
Axes of the slice: x: 2, y: 2, z: 4, core: 2. Of those that a mesh axis runs over, the one named last changes fastest.
Arguments:
- tokens: bfloat16 [8192, 768], P(('fsdp', 'tp')), may hold values from -6 to 6
- segment_ids: int32 [8, 1024], P('fsdp'), may hold values from 0 to 7, never falling along the last dimension, each value on 1 to 384 neighbouring positions
- patch_pos: int32 [2, 8192], P(None, ('fsdp', 'tp')), may hold values from 0 to 63
- row_table: bfloat16 [64, 768], P(None, ('fsdp', 'tp')), may hold values from -3 to 3
- col_table: bfloat16 [64, 768], P(None, ('fsdp', 'tp')), may hold values from -3 to 3
- ln_gain: bfloat16 [2, 2, 768], P(None, None, ('fsdp', 'tp')), may hold values from 0.5 to 1.5
- ln_bias: bfloat16 [2, 2, 768], P(None, None, ('fsdp', 'tp')), may hold values from -1.796875 to 1.796875
- qkv_bias: bfloat16 [2, 3, 768], P(None, None, ('fsdp', 'tp')), may hold values from -1.796875 to 1.796875
- qk_gain: bfloat16 [2, 2, 768], P(None, None, ('fsdp', 'tp')), may hold values from 0.5 to 1.5
- query_bias: bfloat16 [2, 768], P(None, ('fsdp', 'tp')), may hold values from -3 to 3
- out_bias: bfloat16 [2, 768], P(None, ('fsdp', 'tp')), may hold values from -1.796875 to 1.796875
- fc1_bias: bfloat16 [2, 3072], P(None, ('fsdp', 'tp')), may hold values from -1.796875 to 1.796875
- fc2_bias: bfloat16 [2, 768], P(None, ('fsdp', 'tp')), may hold values from -1.796875 to 1.796875
- w_qkv: bfloat16 [2, 768, 3, 768], P(None, 'fsdp', None, 'tp'), may hold values from -0.21875 to 0.21875
- w_out: bfloat16 [2, 768, 768], P(None, 'tp', 'fsdp'), may hold values from -1.75 to 1.75
- w_fc1: bfloat16 [2, 768, 3072], P(None, 'fsdp', 'tp'), may hold values from -0.21875 to 0.21875
- w_fc2: bfloat16 [2, 3072, 768], P(None, 'tp', 'fsdp'), may hold values from -0.109375 to 0.109375
- cotangent: float32 [8192, 768], P(('fsdp', 'tp')), may hold values from -6 to 6
Outputs:
- activations: float32 [8192, 768], P(('fsdp', 'tp'))
- token_grad: float32 [8192, 768], P(('fsdp', 'tp'))
- row_table_grad: float32 [64, 768], P(None, ('fsdp', 'tp'))
- col_table_grad: float32 [64, 768], P(None, ('fsdp', 'tp'))
- ln_gain_grad: float32 [2, 2, 768], P(None, None, ('fsdp', 'tp'))
- ln_bias_grad: float32 [2, 2, 768], P(None, None, ('fsdp', 'tp'))
- qkv_bias_grad: float32 [2, 3, 768], P(None, None, ('fsdp', 'tp'))
- qk_gain_grad: float32 [2, 2, 768], P(None, None, ('fsdp', 'tp'))
- query_bias_grad: float32 [2, 768], P(None, ('fsdp', 'tp'))
- out_bias_grad: float32 [2, 768], P(None, ('fsdp', 'tp'))
- fc1_bias_grad: float32 [2, 3072], P(None, ('fsdp', 'tp'))
- fc2_bias_grad: float32 [2, 768], P(None, ('fsdp', 'tp'))
- w_qkv_grad: float32 [2, 768, 3, 768], P(None, 'fsdp', None, 'tp')
- w_out_grad: float32 [2, 768, 768], P(None, 'tp', 'fsdp')
- w_fc1_grad: float32 [2, 768, 3072], P(None, 'fsdp', 'tp')
- w_fc2_grad: float32 [2, 3072, 768], P(None, 'tp', 'fsdp')
Inputs may be any that keep to these rules, and one draw needn't show every extreme that they name: `segment_ids`: each row is one sequence; ids never fall along it and every id from 0 to 7 appears in one run of 1 to 384 tokens; some image has exactly 384.
All inputs are finite; a program needn't handle non-finite values.
Results may differ from a plain program's by a relative error of at most 0.019.
Values may be sent and summed in bfloat16 or wider, within the bound.
A program may use at most 192 MiB of HBM per device.

v0:
```python
import jax
import jax.numpy as jnp
from jax import lax
from jax.sharding import PartitionSpec as P

HD = 64


epsilon = 1e-06
negative_fill = -1e30
highest = lax.Precision.HIGHEST
root_half = 0.7071067811865476
inv_root_two_pi = 0.3989422804014327


def norm_rows(value):
    centered = value - jnp.mean(value, axis=-1, keepdims=True)
    scale_inv = lax.rsqrt(jnp.mean(centered * centered, axis=-1, keepdims=True) + epsilon)
    return (centered * scale_inv, scale_inv)


def norm_back(grad_hat, normed, scale_inv):
    return scale_inv * (
        grad_hat
        - jnp.mean(grad_hat, axis=-1, keepdims=True)
        - normed * jnp.mean(grad_hat * normed, axis=-1, keepdims=True)
    )


def gelu_exact(value):
    return 0.5 * value * (1.0 + lax.erf(value * root_half))


def gelu_slope(value):
    return (
        0.5 * (1.0 + lax.erf(value * root_half))
        + value * jnp.exp(-0.5 * value * value) * inv_root_two_pi
    )


def split_blocks(length):
    block = min(512, length)
    return (block, length // block)


def block_scores(query_block, key_seq, query_seg, key_seg):
    scores = jnp.einsum(
        "qhd,khd->hqk", query_block, key_seq, preferred_element_type=jnp.float32
    ) * HD ** (-0.5)
    same_image = query_seg[:, None] == key_seg[None, :]
    return jnp.where(same_image[None], scores, negative_fill)


def fetch_block(index, count, block, query_blocks, keys, values, segments):
    seq_index = index // count
    start = index % count * block
    key_seq = lax.dynamic_index_in_dim(keys, seq_index, 0, keepdims=False)
    value_seq = lax.dynamic_index_in_dim(values, seq_index, 0, keepdims=False)
    seg_seq = lax.dynamic_index_in_dim(segments, seq_index, 0, keepdims=False)
    query_seg = lax.dynamic_slice_in_dim(seg_seq, start, block)
    query_block = lax.dynamic_index_in_dim(query_blocks, index, 0, keepdims=False)
    return (query_block, key_seq, value_seq, query_seg, seg_seq)


def attend(queries, keys, values, segments):
    seqs, length, heads, width = queries.shape
    block, count = split_blocks(length)
    query_blocks = queries.reshape(seqs * count, block, heads, width)

    def one_block(index):
        query_block, key_seq, value_seq, query_seg, seg_seq = fetch_block(
            index, count, block, query_blocks, keys, values, segments
        )
        scores = block_scores(query_block, key_seq, query_seg, seg_seq)
        top = jnp.max(scores, axis=-1, keepdims=True)
        weights = jnp.exp(scores - top)
        total = jnp.sum(weights, axis=-1, keepdims=True)
        probs = (weights / total).astype(jnp.bfloat16)
        mixed = jnp.einsum("hqk,khd->qhd", probs, value_seq, preferred_element_type=jnp.float32)
        return (mixed.astype(jnp.bfloat16), (top + jnp.log(total))[..., 0])

    mixed, log_norm = lax.map(one_block, jnp.arange(seqs * count, dtype=jnp.int32))
    return (mixed.reshape(seqs, length, heads, width), log_norm)


def attend_back(queries, keys, values, segments, log_norm, grad_mixed):
    seqs, length, heads, width = queries.shape
    block, count = split_blocks(length)
    query_blocks = queries.reshape(seqs * count, block, heads, width)
    grad_blocks = grad_mixed.reshape(seqs * count, block, heads, width)

    def one_block(index):
        query_block, key_seq, value_seq, query_seg, seg_seq = fetch_block(
            index, count, block, query_blocks, keys, values, segments
        )
        grad_block = lax.dynamic_index_in_dim(grad_blocks, index, 0, keepdims=False)
        norm_block = lax.dynamic_index_in_dim(log_norm, index, 0, keepdims=False)
        scores = block_scores(query_block, key_seq, query_seg, seg_seq)
        probs = jnp.exp(scores - norm_block[..., None])
        grad_values = jnp.einsum(
            "hqk,qhd->khd",
            probs.astype(jnp.bfloat16),
            grad_block,
            preferred_element_type=jnp.float32,
        )
        grad_probs = jnp.einsum(
            "qhd,khd->hqk", grad_block, value_seq, preferred_element_type=jnp.float32
        )
        grad_scores = (
            probs * (grad_probs - jnp.sum(probs * grad_probs, axis=-1, keepdims=True))
        ).astype(jnp.bfloat16)
        grad_query = jnp.einsum(
            "hqk,khd->qhd", grad_scores, key_seq, preferred_element_type=jnp.float32
        ) * HD ** (-0.5)
        grad_keys = jnp.einsum(
            "hqk,qhd->khd", grad_scores, query_block, preferred_element_type=jnp.float32
        ) * HD ** (-0.5)
        return (grad_query, grad_keys, grad_values)

    grad_query, grad_keys, grad_values = lax.map(
        one_block, jnp.arange(seqs * count, dtype=jnp.int32)
    )
    grad_query = grad_query.reshape(seqs * length, heads, width)
    grad_keys = jnp.sum(grad_keys.reshape(seqs, count, length, heads, width), axis=1).reshape(
        seqs * length, heads, width
    )
    grad_values = jnp.sum(grad_values.reshape(seqs, count, length, heads, width), axis=1).reshape(
        seqs * length, heads, width
    )
    return (grad_query, grad_keys, grad_values)


def gather_rows(rows):
    return lax.all_gather(rows, "tp", axis=0, tiled=True)


def gather_grads(rows):
    return lax.all_gather(rows, "tp", axis=0, tiled=True)


def sum_branch(left, right, own_rows):

    def term(start, count):
        return jnp.dot(left, right, preferred_element_type=jnp.float32)

    return lax.psum_scatter(
        term(jnp.int32(0), own_rows * lax.axis_size("tp")).astype(jnp.bfloat16),
        "tp",
        scatter_dimension=0,
        tiled=True,
    ).astype(jnp.float32)


def sum_inputs(left, right, own_rows):

    def term(start, count):
        return lax.dot_general(
            left, right, (((1,), (1,)), ((), ())), preferred_element_type=jnp.float32
        )

    return lax.psum_scatter(
        term(jnp.int32(0), own_rows * lax.axis_size("tp")).astype(jnp.bfloat16),
        "tp",
        scatter_dimension=0,
        tiled=True,
    ).astype(jnp.float32)


def place_slice(local, full_width, offset):
    padded = jnp.zeros(local.shape[:-1] + (full_width,), jnp.float32)
    return lax.dynamic_update_slice_in_dim(padded, local, offset, local.ndim - 1)


def body(
    tokens,
    segment_ids,
    patch_pos,
    row_table,
    col_table,
    ln_gain,
    ln_bias,
    qkv_bias,
    qk_gain,
    query_bias,
    out_bias,
    fc1_bias,
    fc2_bias,
    w_qkv,
    w_out,
    w_fc1,
    w_fc2,
    cotangent,
):
    small = (
        lax.all_gather(row_table, ("fsdp", "tp"), axis=1, tiled=True),
        lax.all_gather(col_table, ("fsdp", "tp"), axis=1, tiled=True),
        lax.all_gather(ln_gain, ("fsdp", "tp"), axis=2, tiled=True),
        lax.all_gather(ln_bias, ("fsdp", "tp"), axis=2, tiled=True),
        lax.all_gather(qkv_bias, ("fsdp", "tp"), axis=2, tiled=True),
        lax.all_gather(qk_gain, ("fsdp", "tp"), axis=2, tiled=True),
        lax.all_gather(query_bias, ("fsdp", "tp"), axis=1, tiled=True),
        lax.all_gather(out_bias, ("fsdp", "tp"), axis=1, tiled=True),
        lax.all_gather(fc1_bias, ("fsdp", "tp"), axis=1, tiled=True),
        lax.all_gather(fc2_bias, ("fsdp", "tp"), axis=1, tiled=True),
    )
    rows_full = small[0]
    cols_full = small[1]
    (
        gains,
        shifts,
        proj_full,
        head_gain_full,
        head_shift_full,
        out_shift,
        hidden_full,
        last_shift,
    ) = [item.astype(jnp.float32) for item in small[2:]]
    layers = w_qkv.shape[0]
    model_width = gains.shape[2]
    hidden_width = hidden_full.shape[1]
    head_cols = w_qkv.shape[3]
    hidden_cols = w_fc1.shape[2]
    heads = head_cols // HD
    tp_index = lax.axis_index("tp")
    head_start = tp_index * head_cols
    hidden_start = tp_index * hidden_cols
    proj_bias = lax.dynamic_slice_in_dim(proj_full, head_start, head_cols, 2)
    head_gain = lax.dynamic_slice_in_dim(head_gain_full, head_start, head_cols, 2)
    head_shift = lax.dynamic_slice_in_dim(head_shift_full, head_start, head_cols, 1)
    hidden_shift = lax.dynamic_slice_in_dim(hidden_full, hidden_start, hidden_cols, 1)
    own_rows = tokens.shape[0]
    seqs = segment_ids.shape[0]
    grid_ids = jnp.arange(rows_full.shape[0], dtype=jnp.int32)
    row_hot = patch_pos[0][:, None] == grid_ids[None, :]
    col_hot = patch_pos[1][:, None] == grid_ids[None, :]
    residual = (
        tokens.astype(jnp.float32)
        + jnp.dot(row_hot.astype(jnp.bfloat16), rows_full, preferred_element_type=jnp.float32)
        + jnp.dot(col_hot.astype(jnp.bfloat16), cols_full, preferred_element_type=jnp.float32)
    )
    saved = []
    for layer in range(layers):
        weights = (
            lax.all_gather(w_qkv[layer], "fsdp", axis=0, tiled=True),
            lax.all_gather(w_out[layer], "fsdp", axis=1, tiled=True),
            lax.all_gather(w_fc1[layer], "fsdp", axis=0, tiled=True),
            lax.all_gather(w_fc2[layer], "fsdp", axis=1, tiled=True),
        )
        w_proj, w_mix, w_up, w_down = weights
        whole = None
        attn_hat, attn_scale = norm_rows(residual)
        attn_in = gather_rows((attn_hat * gains[layer, 0] + shifts[layer, 0]).astype(jnp.bfloat16))
        group = attn_in.shape[0]
        shape_four = (seqs, group // seqs, heads, HD)
        proj = (
            jnp.einsum("gd,dcf->gcf", attn_in, w_proj, preferred_element_type=jnp.float32)
            + proj_bias[layer][None]
        )
        query_hat, query_scale = norm_rows(proj[:, 0].reshape(group, heads, HD))
        key_hat, key_scale = norm_rows(proj[:, 1].reshape(group, heads, HD))
        queries = (
            (
                query_hat * head_gain[layer, 0].reshape(heads, HD)
                + head_shift[layer].reshape(heads, HD)
            )
            .astype(jnp.bfloat16)
            .reshape(shape_four)
        )
        keys = (
            (key_hat * head_gain[layer, 1].reshape(heads, HD))
            .astype(jnp.bfloat16)
            .reshape(shape_four)
        )
        values = proj[:, 2].astype(jnp.bfloat16).reshape(shape_four)
        mixed, log_norm = attend(queries, keys, values, segment_ids)
        mixed = mixed.reshape(group, head_cols)
        attn_out = sum_branch(mixed, w_mix, own_rows)
        middle = residual + attn_out + out_shift[layer]
        mlp_hat, mlp_scale = norm_rows(middle)
        mlp_in = gather_rows((mlp_hat * gains[layer, 1] + shifts[layer, 1]).astype(jnp.bfloat16))
        hidden = jnp.dot(mlp_in, w_up, preferred_element_type=jnp.float32) + hidden_shift[layer]
        activated = gelu_exact(hidden).astype(jnp.bfloat16)
        mlp_out = sum_branch(activated, w_down, own_rows)
        residual = middle + mlp_out + last_shift[layer]
        saved.append(
            (
                weights,
                whole,
                attn_hat,
                attn_scale,
                attn_in,
                query_hat,
                query_scale,
                key_hat,
                key_scale,
                queries,
                keys,
                values,
                log_norm,
                mixed,
                mlp_hat,
                mlp_scale,
                mlp_in,
                hidden,
                activated,
            )
        )
    grad = cotangent
    gain_grads, shift_grads, proj_shift_grads, head_gain_grads, head_shift_grads = (
        [],
        [],
        [],
        [],
        [],
    )
    out_shift_grads, hidden_shift_grads, last_shift_grads = ([], [], [])
    w_proj_grads, w_mix_grads, w_up_grads, w_down_grads = ([], [], [], [])
    for layer in reversed(range(layers)):
        (
            weights,
            whole,
            attn_hat,
            attn_scale,
            attn_in,
            query_hat,
            query_scale,
            key_hat,
            key_scale,
            queries,
            keys,
            values,
            log_norm,
            mixed,
            mlp_hat,
            mlp_scale,
            mlp_in,
            hidden,
            activated,
        ) = saved[layer]
        weights = (
            lax.all_gather(w_qkv[layer], "fsdp", axis=0, tiled=True),
            lax.all_gather(w_out[layer], "fsdp", axis=1, tiled=True),
            lax.all_gather(w_fc1[layer], "fsdp", axis=0, tiled=True),
            lax.all_gather(w_fc2[layer], "fsdp", axis=1, tiled=True),
        )
        w_proj, w_mix, w_up, w_down = weights
        whole = None
        group = attn_in.shape[0]
        shape_four = (seqs, group // seqs, heads, HD)
        down_grad = grad.astype(jnp.bfloat16)
        last_shift_grads.append(jnp.sum(down_grad, axis=0, dtype=jnp.float32))
        down_all = gather_grads(down_grad)
        w_down_grad = jnp.einsum(
            "gf,gd->fd", activated, down_all, preferred_element_type=jnp.float32
        )
        hidden_grad = (
            jnp.einsum("gd,fd->gf", down_all, w_down, preferred_element_type=jnp.float32)
            * gelu_slope(hidden)
        ).astype(jnp.bfloat16)
        hidden_shift_grads.append(
            place_slice(jnp.sum(hidden_grad, axis=0, dtype=jnp.float32), hidden_width, hidden_start)
        )
        w_up_grad = jnp.einsum("gd,gf->df", mlp_in, hidden_grad, preferred_element_type=jnp.float32)
        mlp_grad = sum_inputs(hidden_grad, w_up, own_rows)
        mlp_gain_grad = jnp.sum(mlp_grad * mlp_hat, axis=0)
        mlp_shift_grad = jnp.sum(mlp_grad, axis=0)
        grad_mid = grad + norm_back(mlp_grad * gains[layer, 1], mlp_hat, mlp_scale)
        mix_grad = grad_mid.astype(jnp.bfloat16)
        out_shift_grads.append(jnp.sum(mix_grad, axis=0, dtype=jnp.float32))
        mix_all = gather_grads(mix_grad)
        w_mix_grad = jnp.einsum("ge,gd->ed", mixed, mix_all, preferred_element_type=jnp.float32)
        grad_mixed = (
            jnp.einsum("gd,ed->ge", mix_all, w_mix, preferred_element_type=jnp.float32)
            .astype(jnp.bfloat16)
            .reshape(shape_four)
        )
        grad_query, grad_keys, grad_values = attend_back(
            queries, keys, values, segment_ids, log_norm, grad_mixed
        )
        query_gain = head_gain[layer, 0].reshape(heads, HD)
        key_gain = head_gain[layer, 1].reshape(heads, HD)
        query_gain_grad = jnp.sum(grad_query * query_hat, axis=0).reshape(head_cols)
        key_gain_grad = jnp.sum(grad_keys * key_hat, axis=0).reshape(head_cols)
        head_gain_grads.append(
            place_slice(
                jnp.stack([query_gain_grad, key_gain_grad], axis=0), model_width, head_start
            )
        )
        head_shift_grads.append(
            place_slice(jnp.sum(grad_query, axis=0).reshape(head_cols), model_width, head_start)
        )
        proj_grad = jnp.stack(
            [
                norm_back(grad_query * query_gain, query_hat, query_scale).reshape(
                    group, head_cols
                ),
                norm_back(grad_keys * key_gain, key_hat, key_scale).reshape(group, head_cols),
                grad_values.reshape(group, head_cols),
            ],
            axis=1,
        ).astype(jnp.bfloat16)
        proj_shift_grads.append(
            place_slice(jnp.sum(proj_grad, axis=0, dtype=jnp.float32), model_width, head_start)
        )
        w_proj_grad = jnp.einsum(
            "gd,gcf->dcf", attn_in, proj_grad, preferred_element_type=jnp.float32
        )
        attn_grad = sum_inputs(
            proj_grad.reshape(group, 3 * head_cols),
            w_proj.reshape(w_proj.shape[0], 3 * head_cols),
            own_rows,
        )
        attn_gain_grad = jnp.sum(attn_grad * attn_hat, axis=0)
        attn_shift_grad = jnp.sum(attn_grad, axis=0)
        grad = grad_mid + norm_back(attn_grad * gains[layer, 0], attn_hat, attn_scale)
        gain_grads.append(jnp.stack([attn_gain_grad, mlp_gain_grad], axis=0))
        shift_grads.append(jnp.stack([attn_shift_grad, mlp_shift_grad], axis=0))
        owned = (
            lax.psum_scatter(w_proj_grad, "fsdp", scatter_dimension=0, tiled=True),
            lax.psum_scatter(w_mix_grad, "fsdp", scatter_dimension=1, tiled=True),
            lax.psum_scatter(w_up_grad, "fsdp", scatter_dimension=0, tiled=True),
            lax.psum_scatter(w_down_grad, "fsdp", scatter_dimension=1, tiled=True),
        )
        w_proj_grads.append(owned[0])
        w_mix_grads.append(owned[1])
        w_up_grads.append(owned[2])
        w_down_grads.append(owned[3])

    def stacked(items):
        return jnp.stack(items[::-1], axis=0)

    row_grad = jnp.einsum("tg,td->gd", row_hot.astype(jnp.float32), grad, precision=highest)
    col_grad = jnp.einsum("tg,td->gd", col_hot.astype(jnp.float32), grad, precision=highest)
    owned_small = (
        lax.psum_scatter(row_grad, ("fsdp", "tp"), scatter_dimension=1, tiled=True),
        lax.psum_scatter(col_grad, ("fsdp", "tp"), scatter_dimension=1, tiled=True),
        lax.psum_scatter(stacked(gain_grads), ("fsdp", "tp"), scatter_dimension=2, tiled=True),
        lax.psum_scatter(stacked(shift_grads), ("fsdp", "tp"), scatter_dimension=2, tiled=True),
        lax.psum_scatter(
            stacked(proj_shift_grads), ("fsdp", "tp"), scatter_dimension=2, tiled=True
        ),
        lax.psum_scatter(stacked(head_gain_grads), ("fsdp", "tp"), scatter_dimension=2, tiled=True),
        lax.psum_scatter(
            stacked(head_shift_grads), ("fsdp", "tp"), scatter_dimension=1, tiled=True
        ),
        lax.psum_scatter(stacked(out_shift_grads), ("fsdp", "tp"), scatter_dimension=1, tiled=True),
        lax.psum_scatter(
            stacked(hidden_shift_grads), ("fsdp", "tp"), scatter_dimension=1, tiled=True
        ),
        lax.psum_scatter(
            stacked(last_shift_grads), ("fsdp", "tp"), scatter_dimension=1, tiled=True
        ),
    )
    return (
        residual,
        grad,
        owned_small[0],
        owned_small[1],
        owned_small[2],
        owned_small[3],
        owned_small[4],
        owned_small[5],
        owned_small[6],
        owned_small[7],
        owned_small[8],
        owned_small[9],
        stacked(w_proj_grads),
        stacked(w_mix_grads),
        stacked(w_up_grads),
        stacked(w_down_grads),
    )


def solution(mesh):
    in_specs = (
        P(("fsdp", "tp"), None),
        P("fsdp", None),
        P(None, ("fsdp", "tp")),
        P(None, ("fsdp", "tp")),
        P(None, ("fsdp", "tp")),
        P(None, None, ("fsdp", "tp")),
        P(None, None, ("fsdp", "tp")),
        P(None, None, ("fsdp", "tp")),
        P(None, None, ("fsdp", "tp")),
        P(None, ("fsdp", "tp")),
        P(None, ("fsdp", "tp")),
        P(None, ("fsdp", "tp")),
        P(None, ("fsdp", "tp")),
        P(None, "fsdp", None, "tp"),
        P(None, "tp", "fsdp"),
        P(None, "fsdp", "tp"),
        P(None, "tp", "fsdp"),
        P(("fsdp", "tp"), None),
    )
    out_specs = (
        P(("fsdp", "tp"), None),
        P(("fsdp", "tp"), None),
        P(None, ("fsdp", "tp")),
        P(None, ("fsdp", "tp")),
        P(None, None, ("fsdp", "tp")),
        P(None, None, ("fsdp", "tp")),
        P(None, None, ("fsdp", "tp")),
        P(None, None, ("fsdp", "tp")),
        P(None, ("fsdp", "tp")),
        P(None, ("fsdp", "tp")),
        P(None, ("fsdp", "tp")),
        P(None, ("fsdp", "tp")),
        P(None, "fsdp", None, "tp"),
        P(None, "tp", "fsdp"),
        P(None, "fsdp", "tp"),
        P(None, "tp", "fsdp"),
    )
    return jax.shard_map(body, mesh=mesh, in_specs=in_specs, out_specs=out_specs, check_vma=False)
```

profile of v0, /device:TPU:0, one launch (start us, length us, event | category | flops | bytes accessed | tf_op | source)
XLA Modules:
  0.0 2138.5 jit_solution(11170683279895438184)
XLA Ops:
  8.8 71.5 %all_gather.86 = bf16[64,768]{0,1:T(8,128)(2,1)S(1)} all-gather(bf16[64,24]{0,1:T(8,128)(2,1)} %param.29), channel_id=1, replica_groups=mesh['fsdp'=8,'tp'=4] {'fsdp','tp'}, dimensions={1}, use_global_device_ids=true | all-gather | bytes 101376 | tf_op jit(solution)/shard_map/all_gather | solution.py:195
  80.3 65.1 %all_gather.87 = bf16[64,768]{0,1:T(8,128)(2,1)S(1)} all-gather(bf16[64,24]{0,1:T(8,128)(2,1)} %param.30), channel_id=1, replica_groups=mesh['fsdp'=8,'tp'=4] {'fsdp','tp'}, dimensions={1}, use_global_device_ids=true | all-gather | bytes 101376 | tf_op jit(solution)/shard_map/all_gather | solution.py:196
  147.5 68.8 %all_gather.88 = bf16[2,2,768]{1,0,2:T(2,128)(2,1)S(1)} all-gather(bf16[2,2,24]{1,0,2:T(2,128)(2,1)S(1)} %copy.128), channel_id=1, replica_groups=mesh['fsdp'=8,'tp'=4] {'fsdp','tp'}, dimensions={2}, use_global_device_ids=true | all-gather | bytes 6336 | tf_op jit(solution)/shard_map/all_gather | solution.py:197
  216.6 9.7 slice_reduce_fusion.1
  226.5 67.2 %all_gather.89 = bf16[2,2,768]{1,0,2:T(2,128)(2,1)S(1)} all-gather(bf16[2,2,24]{1,0,2:T(2,128)(2,1)S(1)} %copy.129), channel_id=1, replica_groups=mesh['fsdp'=8,'tp'=4] {'fsdp','tp'}, dimensions={2}, use_global_device_ids=true | all-gather | bytes 6336 | tf_op jit(solution)/shard_map/all_gather | solution.py:198
  294.0 9.7 slice_reduce_fusion
  304.9 12.2 all-gather
  318.1 70.5 %all_gather.92 = bf16[2,3,768]{1,0,2:T(2,128)(2,1)S(1)} all-gather(bf16[2,3,24]{1,0,2:T(2,128)(2,1)S(1)} %copy.132), channel_id=1, replica_groups=mesh['fsdp'=8,'tp'=4] {'fsdp','tp'}, dimensions={2}, use_global_device_ids=true | all-gather | bytes 9504 | tf_op jit(solution)/shard_map/all_gather | solution.py:199
  389.1 67.0 %all_gather.93 = bf16[2,2,768]{1,0,2:T(2,128)(2,1)S(1)} all-gather(bf16[2,2,24]{1,0,2:T(2,128)(2,1)S(1)} %copy.135), channel_id=1, replica_groups=mesh['fsdp'=8,'tp'=4] {'fsdp','tp'}, dimensions={2}, use_global_device_ids=true | all-gather | bytes 6336 | tf_op jit(solution)/shard_map/all_gather | solution.py:200
  458.9 64.7 %all-gather.8 = bf16[32,24,2]{1,2,0:T(2,128)(2,1)S(1)} all-gather(bf16[1,24,2]{1,2,0:T(2,128)(2,1)S(1)} %bitcast.656), channel_id=1, replica_groups=mesh['fsdp'=8,'tp'=4] {'fsdp','tp'}, dimensions={0}, use_global_device_ids=true | all-gather | bytes 3168 | tf_op jit(solution)/shard_map/all_gather | solution.py:201
  524.9 9.4 all-gather.1
  543.5 19.3 while.60
  566.1 65.7 %all-gather.9 = bf16[32,24,2]{1,2,0:T(2,128)(2,1)S(1)} all-gather(bf16[1,24,2]{1,2,0:T(2,128)(2,1)S(1)} %bitcast.657), channel_id=1, replica_groups=mesh['fsdp'=8,'tp'=4] {'fsdp','tp'}, dimensions={0}, use_global_device_ids=true | all-gather | bytes 3168 | tf_op jit(solution)/shard_map/all_gather | solution.py:202
  635.4 64.0 %all-gather.10 = bf16[32,96,2]{1,2,0:T(2,128)(2,1)S(1)} all-gather(bf16[1,96,2]{1,2,0:T(2,128)(2,1)S(1)} %bitcast.658), channel_id=1, replica_groups=mesh['fsdp'=8,'tp'=4] {'fsdp','tp'}, dimensions={0}, use_global_device_ids=true | all-gather | bytes 12672 | tf_op jit(solution)/shard_map/all_gather | solution.py:203
  699.7 5.3 multiply_convert_fusion.3
  709.5 65.9 %all-gather.11 = bf16[32,24,2]{1,2,0:T(2,128)(2,1)S(1)} all-gather(bf16[1,24,2]{1,2,0:T(2,128)(2,1)S(1)} %bitcast.659), channel_id=1, replica_groups=mesh['fsdp'=8,'tp'=4] {'fsdp','tp'}, dimensions={0}, use_global_device_ids=true | all-gather | bytes 3168 | tf_op jit(solution)/shard_map/all_gather | solution.py:204
  778.4 12.6 all-gather.4
  793.5 9.3 all-gather.5
  804.4 8.0 all-gather.29.cloned.1.call-done
  820.2 19.3 while.61
  842.6 33.5 %reduce-scatter.41.cloned.1.call-done = bf16[256,768]{1,0:T(8,128)(2,1)} async-done(((bf16[1024,768]{1,0:T(8,128)(2,1)}), bf16[256,768]{1,0:T(8,128)(2,1)}) %reduce-scatter.41.cloned.1.call-update) | async-done | bytes 393232 | tf_op jit(solution)/shard_map/reduce_scatter | solution.py:146
  882.2 32.3 %all-gather.31.cloned.1.call-done = bf16[1024,768]{1,0:T(8,128)(2,1)} async-done(((bf16[256,768]{1,0:T(8,128)(2,1)}), bf16[1024,768]{1,0:T(8,128)(2,1)}) %all-gather.31.cloned.1.call-update) | async-done | bytes 1572880 | tf_op jit(solution)/shard_map/all_gather | solution.py:134
  914.6 5.4 multiply_convert_fusion.2
  920.0 19.7 all-gather.47.cloned.1.call-done
  939.7 39.0 %all-gather.33.cloned.1.call-done = bf16[1024,768]{1,0:T(8,128)(2,1)} async-done(((bf16[256,768]{1,0:T(8,128)(2,1)}), bf16[1024,768]{1,0:T(8,128)(2,1)}) %all-gather.33.cloned.1.call-update) | async-done | bytes 1572880 | tf_op jit(solution)/shard_map/all_gather | solution.py:138
  978.6 4.9 convert_reduce_fusion
  991.7 29.9 %reduce-scatter.45.cloned.1.call-done = bf16[256,768]{1,0:T(8,128)(2,1)} async-done(((bf16[1024,768]{1,0:T(8,128)(2,1)}), bf16[256,768]{1,0:T(8,128)(2,1)}) %reduce-scatter.45.cloned.1.call-update) | async-done | bytes 393232 | tf_op jit(solution)/shard_map/reduce_scatter | solution.py:161
  1023.6 34.4 %reduce-scatter.43.cloned.1.call-done = bf16[256,768]{1,0:T(8,128)(2,1)} async-done(((bf16[1024,768]{1,0:T(8,128)(2,1)}), bf16[256,768]{1,0:T(8,128)(2,1)}) %reduce-scatter.43.cloned.1.call-update) | async-done | bytes 393232 | tf_op jit(solution)/shard_map/reduce_scatter | solution.py:146
  1061.9 35.8 %all-gather.35.cloned.1.call-done = bf16[1024,768]{1,0:T(8,128)(2,1)} async-done(((bf16[256,768]{1,0:T(8,128)(2,1)}), bf16[1024,768]{1,0:T(8,128)(2,1)}) %all-gather.35.cloned.1.call-update) | async-done | bytes 1572880 | tf_op jit(solution)/shard_map/all_gather | solution.py:138
  1104.5 31.4 %while.62 = (s32[]{:T(128)}, f32[2,512,3,64]{1,3,2,0:T(8,128)}, f32[2,1024,3,64]{1,3,2,0:T(8,128)}, f32[2,1024,3,64]{1,3,2,0:T(8,128)}, s32[2]{0:T(128)S(1)}, /*...) while((s32[]{:T(128)}, f32[2,512,3,64]{1,3,2,0:T(8,128)}, ...), condition=%wide.region_33.34_spmd, body=%wide.region_31.33_spmd.sunk | while | flops 1031043584 | bytes 73720832 | solution.py:120
  1151.9 34.2 %reduce-scatter.47.cloned.1.call-done = bf16[256,768]{1,0:T(8,128)(2,1)} async-done(((bf16[1024,768]{1,0:T(8,128)(2,1)}), bf16[256,768]{1,0:T(8,128)(2,1)}) %reduce-scatter.47.cloned.1.call-update) | async-done | bytes 393232 | tf_op jit(solution)/shard_map/reduce_scatter | solution.py:161
  1190.9 35.9 %all-gather.37.cloned.1.call-done = bf16[1024,768]{1,0:T(8,128)(2,1)} async-done(((bf16[256,768]{1,0:T(8,128)(2,1)}), bf16[1024,768]{1,0:T(8,128)(2,1)}) %all-gather.37.cloned.1.call-update) | async-done | bytes 1572880 | tf_op jit(solution)/shard_map/all_gather | solution.py:138
  1226.8 4.9 convert_reduce_fusion.1
  1235.6 34.2 %reduce-scatter.49.cloned.1.call-done = bf16[256,768]{1,0:T(8,128)(2,1)} async-done(((bf16[1024,768]{1,0:T(8,128)(2,1)}), bf16[256,768]{1,0:T(8,128)(2,1)}) %reduce-scatter.49.cloned.1.call-update) | async-done | bytes 393232 | tf_op jit(solution)/shard_map/reduce_scatter | solution.py:161
  1299.4 11.5 all-gather.39.cloned.1.call-done
  1316.1 28.6 %while.63 = (s32[]{:T(128)}, f32[2,512,3,64]{1,3,2,0:T(8,128)S(1)}, f32[2,1024,3,64]{1,3,2,0:T(8,128)}, f32[2,1024,3,64]{1,3,2,0:T(8,128)}, s32[2]{0:T(128)S(1)}...) while((s32[]{:T(128)}, f32[2,512,3,64]{1,3,2,0:T(8,128)S(1)}, ...), condition=%wide.region_48.49_spmd, body=%wide.region_46.48_spmd.sunk | while | flops 1031043584 | bytes 65856428 | solution.py:120
  1372.7 77.4 %reduce-scatter.65.cloned.1.call-done = f32[96,2]{1,0:T(8,128)} async-done(((f32[3072,2]{1,0:T(8,128)}), f32[96,2]{1,0:T(8,128)}) %reduce-scatter.65.cloned.1.call-update) | async-done | bytes 784
  1452.2 42.7 %reduce-scatter.63.cloned.1.call-done = f32[768,96]{0,1:T(8,128)} async-done(((f32[768,768]{0,1:T(8,128)}), f32[768,96]{0,1:T(8,128)}) %reduce-scatter.63.cloned.1.call-update) | async-done | bytes 294928 | tf_op jit(solution)/shard_map/reduce_scatter | solution.py:422
  1494.9 46.1 %reduce-scatter.61.cloned.1.call-done = f32[768,96]{0,1:T(8,128)} async-done(((f32[768,768]{0,1:T(8,128)}), f32[768,96]{0,1:T(8,128)}) %reduce-scatter.61.cloned.1.call-update) | async-done | bytes 294928 | tf_op jit(solution)/shard_map/reduce_scatter | solution.py:422
  1542.8 43.8 %reduce-scatter.59.cloned.1.call-done = f32[96,768]{1,0:T(8,128)} async-done(((f32[768,768]{1,0:T(8,128)}), f32[96,768]{1,0:T(8,128)}) %reduce-scatter.59.cloned.1.call-update) | async-done | bytes 294928 | tf_op jit(solution)/shard_map/reduce_scatter | solution.py:421
  1586.7 46.1 %reduce-scatter.57.cloned.1.call-done = f32[96,768]{1,0:T(8,128)} async-done(((f32[768,768]{1,0:T(8,128)}), f32[96,768]{1,0:T(8,128)}) %reduce-scatter.57.cloned.1.call-update) | async-done | bytes 294928 | tf_op jit(solution)/shard_map/reduce_scatter | solution.py:421
  1637.5 34.0 %reduce-scatter.67.cloned.1.call-done = f32[96,192]{1,0:T(8,128)} async-done(((f32[768,192]{1,0:T(8,128)}), f32[96,192]{1,0:T(8,128)}) %reduce-scatter.67.cloned.1.call-update) | async-done | bytes 73744
  1673.2 35.8 %reduce-scatter.51.cloned.1.call-done = bf16[256,768]{1,0:T(8,128)(2,1)} async-done(((bf16[1024,768]{1,0:T(8,128)(2,1)}), bf16[256,768]{1,0:T(8,128)(2,1)}) %reduce-scatter.51.cloned.1.call-update) | async-done | bytes 393232 | tf_op jit(solution)/shard_map/reduce_scatter | solution.py:161
  1714.8 38.8 %reduce-scatter.55.cloned.1.call-done = f32[96,3,192]{2,0,1:T(8,128)} async-done(((f32[768,3,192]{2,0,1:T(8,128)}), f32[96,3,192]{2,0,1:T(8,128)}) %reduce-scatter.55.cloned.1.call-update) | async-done | bytes 221200 | tf_op jit(solution)/shard_map/reduce_scatter | solution.py:419
  1753.6 45.9 %reduce-scatter.53.cloned.1.call-done = f32[96,3,192]{2,0,1:T(8,128)} async-done(((f32[768,3,192]{2,0,1:T(8,128)}), f32[96,3,192]{2,0,1:T(8,128)}) %reduce-scatter.53.cloned.1.call-update) | async-done | bytes 221200 | tf_op jit(solution)/shard_map/reduce_scatter | solution.py:419
  1803.1 124.2 %all-reduce.12.cloned.1.call-done = (f32[2,2,768]{2,1,0:T(2,128)}, f32[2,2,768]{2,1,0:T(2,128)}, f32[2,3,768]{2,0,1:T(2,128)}, f32[2,2,768]{2,1,0:T(2,128)}, f32...) async-done(((f32[2,2,768]{2,1,0:T(2,128)}, f32[2,2,768]{2,1,0:T(2,128)}, f32[2,3,768]{2,0,1:T(2,128)}, f32[2,2,768]{2,1,0:T(2,128)}, f32[2,768]{1,0:T(2,128)}, ...) | async-done | bytes 73744
  1936.5 94.9 %reduce-scatter.73.cloned.1.call-done = f32[64,24]{0,1:T(8,128)} async-done(((f32[64,768]{0,1:T(8,128)}), f32[64,24]{0,1:T(8,128)}) %reduce-scatter.73.cloned.1.call-update) | async-done | bytes 6160
  2031.3 99.6 %reduce-scatter.71.cloned.1.call-done = f32[64,24]{0,1:T(8,128)} async-done(((f32[64,768]{0,1:T(8,128)}), f32[64,24]{0,1:T(8,128)}) %reduce-scatter.71.cloned.1.call-update) | async-done | bytes 6160
  (708 shorter events, 261.6 us)
Async XLA Ops:
  8.0 527.8 %all-gather.25.cloned.1.call-start = ((), (), s32[]{:S(2)}) async-start(), calls=%async_computation.19 | async-start | bytes 1966080 | tf_op jit(solution)/shard_map/all_gather | solution.py:134
  147.1 485.0 %copy-start.4 = (f32[256,768]{1,0:T(8,128)}, f32[256,768]{1,0:T(8,128)S(1)}, u32[]{:S(2)}) copy-start(f32[256,768]{1,0:T(8,128)S(1)} %get-tuple-element.802) | copy-start | bytes 2359300
  147.1 156.5 %copy-start.81 = (f32[256]{0:T(256)}, f32[256]{0:T(256)S(1)}, u32[]{:S(2)}) copy-start(f32[256]{0:T(256)S(1)} %broadcast_multiply_fusion.23) | copy-start | bytes 3076
  226.4 407.2 %copy-start.75 = (f32[768]{0:T(1024)}, f32[768]{0:T(1024)S(1)}, u32[]{:S(2)}) copy-start(f32[768]{0:T(1024)S(1)} %get-tuple-element.644) | copy-start | bytes 9220
  226.4 550.8 %copy-start.77 = (f32[768]{0:T(1024)}, f32[768]{0:T(1024)S(1)}, u32[]{:S(2)}) copy-start(f32[768]{0:T(1024)S(1)} %get-tuple-element.643) | copy-start | bytes 9220
  304.7 327.4 %reduce-scatter.37.cloned.1.call-start = ((), (), s32[]{:S(2)}) async-start(), calls=%async_computation.20 | async-start | bytes 1966080 | tf_op jit(solution)/shard_map/reduce_scatter | solution.py:146
  318.0 217.9 %copy-start.47 = (bf16[1,768,3,192]{1,3,2,0:T(8,128)(2,1)}, bf16[1,768,3,192]{1,3,2,0:T(8,128)(2,1)S(1)}, u32[]{:S(2)}) copy-start(bf16[1,768,3,192]{1,3,2,0:T(8,128)(2,1)S(1)} %copy.131) | copy-start | bytes 2654212
  318.0 206.1 %copy-start.72 = (bf16[2,192,96]{2,1,0:T(8,128)(2,1)S(1)}, bf16[2,192,96]{2,1,0:T(8,128)(2,1)}, u32[]{:S(2)}) copy-start(bf16[2,192,96]{2,1,0:T(8,128)(2,1)} %param.40) | copy-start | bytes 221188
  458.3 334.8 %copy-start.114 = (f32[192]{0:T(256)}, f32[192]{0:T(256)S(1)}, u32[]{:S(2)}) copy-start(f32[192]{0:T(256)S(1)} %get-tuple-element.658) | copy-start | bytes 2308
  458.3 334.9 %copy-start.116 = (f32[192]{0:T(256)}, f32[192]{0:T(256)S(1)}, u32[]{:S(2)}) copy-start(f32[192]{0:T(256)S(1)} %get-tuple-element.659) | copy-start | bytes 2308
  565.2 134.4 %all-gather.41.cloned.1.call-start = ((), (), s32[]{:S(2)}) async-start(), calls=%async_computation.41 | async-start | bytes 1327104 | tf_op jit(solution)/shard_map/all_gather | solution.py:246
  566.0 133.6 %all-gather.27.cloned.1.call-start = ((), (), s32[]{:S(2)}) async-start(), calls=%async_computation.21 | async-start | bytes 1966080 | tf_op jit(solution)/shard_map/all_gather | solution.py:134
  634.6 70.5 %all-gather.43.cloned.1.call-start = ((), (), s32[]{:S(2)}) async-start(), calls=%async_computation.42 | async-start | bytes 1327104 | tf_op jit(solution)/shard_map/all_gather | solution.py:247
  635.4 140.4 %reduce-scatter.39.cloned.1.call-start = ((), (), s32[]{:S(2)}) async-start(), calls=%async_computation.22 | async-start | bytes 1966080 | tf_op jit(solution)/shard_map/reduce_scatter | solution.py:146
  709.4 102.9 %all-gather.29.cloned.1.call-start = ((), (), s32[]{:S(2)}) async-start(), calls=%async_computation.23 | async-start | bytes 1966080 | tf_op jit(solution)/shard_map/all_gather | solution.py:134
  778.2 97.9 %reduce-scatter.41.cloned.1.call-start = ((), (), s32[]{:S(2)}) async-start(), calls=%async_computation.24 | async-start | bytes 1966080 | tf_op jit(solution)/shard_map/reduce_scatter | solution.py:146
  841.8 40.4 %all-gather.45.cloned.1.call-start = ((), (), s32[]{:S(2)}) async-start(), calls=%async_computation.43 | async-start | bytes 1327104 | tf_op jit(solution)/shard_map/all_gather | solution.py:246
  842.6 72.0 %all-gather.31.cloned.1.call-start = ((), (), s32[]{:S(2)}) async-start(), calls=%async_computation.25 | async-start | bytes 1966080 | tf_op jit(solution)/shard_map/all_gather | solution.py:134
  878.6 61.1 %all-gather.47.cloned.1.call-start = ((), (), s32[]{:S(2)}) async-start(), calls=%async_computation.44 | async-start | bytes 1327104 | tf_op jit(solution)/shard_map/all_gather | solution.py:247
  879.2 99.5 %all-gather.33.cloned.1.call-start = ((), (), s32[]{:S(2)}) async-start(), calls=%async_computation.27 | async-start | bytes 1966080 | tf_op jit(solution)/shard_map/all_gather | solution.py:138
  881.7 139.9 %reduce-scatter.45.cloned.1.call-start = ((), (), s32[]{:S(2)}) async-start(), calls=%async_computation.28 | async-start | bytes 1966080 | tf_op jit(solution)/shard_map/reduce_scatter | solution.py:161
  987.3 70.8 %reduce-scatter.43.cloned.1.call-start = ((), (), s32[]{:S(2)}) async-start(), calls=%async_computation.26 | async-start | bytes 1966080 | tf_op jit(solution)/shard_map/reduce_scatter | solution.py:146
  991.6 106.0 %all-gather.35.cloned.1.call-start = ((), (), s32[]{:S(2)}) async-start(), calls=%async_computation.29 | async-start | bytes 1966080 | tf_op jit(solution)/shard_map/all_gather | solution.py:138
  1061.7 124.4 %reduce-scatter.47.cloned.1.call-start = ((), (), s32[]{:S(2)}) async-start(), calls=%async_computation.30 | async-start | bytes 1966080 | tf_op jit(solution)/shard_map/reduce_scatter | solution.py:161
  1151.8 75.0 %all-gather.37.cloned.1.call-start = ((), (), s32[]{:S(2)}) async-start(), calls=%async_computation.31 | async-start | bytes 1966080 | tf_op jit(solution)/shard_map/all_gather | solution.py:138
  1190.8 79.0 %reduce-scatter.49.cloned.1.call-start = ((), (), s32[]{:S(2)}) async-start(), calls=%async_computation.32 | async-start | bytes 1966080 | tf_op jit(solution)/shard_map/reduce_scatter | solution.py:161
  1235.6 75.3 %all-gather.39.cloned.1.call-start = ((), (), s32[]{:S(2)}) async-start(), calls=%async_computation.33 | async-start | bytes 1966080 | tf_op jit(solution)/shard_map/all_gather | solution.py:138
  1274.8 96.2 %reduce-scatter.69.cloned.1.call-start = ((), (), s32[]{:S(2)}) async-start(), calls=%async_computation.47 | async-start | bytes 884736
  1278.0 172.1 %reduce-scatter.65.cloned.1.call-start = ((), (), s32[]{:S(2)}) async-start(), calls=%async_computation.45 | async-start | bytes 1622016
  1279.8 215.0 %reduce-scatter.63.cloned.1.call-start = ((), (), s32[]{:S(2)}) async-start(), calls=%async_computation.40 | async-start | bytes 2654208 | tf_op jit(solution)/shard_map/reduce_scatter | solution.py:422
  1284.9 256.1 %reduce-scatter.61.cloned.1.call-start = ((), (), s32[]{:S(2)}) async-start(), calls=%async_computation.39 | async-start | bytes 2654208 | tf_op jit(solution)/shard_map/reduce_scatter | solution.py:422
  1289.1 297.6 %reduce-scatter.59.cloned.1.call-start = ((), (), s32[]{:S(2)}) async-start(), calls=%async_computation.38 | async-start | bytes 2654208 | tf_op jit(solution)/shard_map/reduce_scatter | solution.py:421
  1294.9 337.8 %reduce-scatter.57.cloned.1.call-start = ((), (), s32[]{:S(2)}) async-start(), calls=%async_computation.37 | async-start | bytes 2654208 | tf_op jit(solution)/shard_map/reduce_scatter | solution.py:421
  1299.3 372.2 %reduce-scatter.67.cloned.1.call-start = ((), (), s32[]{:S(2)}) async-start(), calls=%async_computation.46 | async-start | bytes 884736
  1351.7 357.3 %reduce-scatter.51.cloned.1.call-start = ((), (), s32[]{:S(2)}) async-start(), calls=%async_computation.34 | async-start | bytes 1966080 | tf_op jit(solution)/shard_map/reduce_scatter | solution.py:161
  1360.5 393.1 %reduce-scatter.55.cloned.1.call-start = ((), (), s32[]{:S(2)}) async-start(), calls=%async_computation.36 | async-start | bytes 2654208 | tf_op jit(solution)/shard_map/reduce_scatter | solution.py:419
  1364.8 434.7 %reduce-scatter.53.cloned.1.call-start = ((), (), s32[]{:S(2)}) async-start(), calls=%async_computation.35 | async-start | bytes 2654208 | tf_op jit(solution)/shard_map/reduce_scatter | solution.py:419
  1369.3 265.3 %copy-start.125 = (f32[3,64]{1,0:T(4,128)S(1)}, f32[3,64]{1,0:T(4,128)}, u32[]{:S(2)}) copy-start(f32[3,64]{1,0:T(4,128)} %get-tuple-element.640) | copy-start | bytes 2308
  1369.3 265.4 %copy-start.124 = (f32[3,64]{1,0:T(4,128)S(1)}, f32[3,64]{1,0:T(4,128)}, u32[]{:S(2)}) copy-start(f32[3,64]{1,0:T(4,128)} %get-tuple-element.622) | copy-start | bytes 2308
  1369.3 557.9 %all-reduce.12.cloned.1.call-start = ((), (), s32[]{:S(2)}) async-start(), calls=%async_computation.50 | async-start | bytes 147456
  1370.3 338.7 %copy-start.5 = (f32[256,768]{1,0:T(8,128)S(1)}, f32[256,768]{1,0:T(8,128)}, u32[]{:S(2)}) copy-start(f32[256,768]{1,0:T(8,128)} %copy-done.4) | copy-start | bytes 2359300
  1370.3 338.7 %copy-start.74 = (f32[768]{0:T(1024)S(1)}, f32[768]{0:T(1024)}, u32[]{:S(2)}) copy-start(f32[768]{0:T(1024)} %copy-done.73) | copy-start | bytes 9220
  1370.4 338.7 %copy-start.82 = (f32[256]{0:T(256)S(1)}, f32[256]{0:T(256)}, u32[]{:S(2)}) copy-start(f32[256]{0:T(256)} %copy-done.81) | copy-start | bytes 3076
  1370.4 338.7 %copy-start.95 = (f32[256]{0:T(256)S(1)}, f32[256]{0:T(256)}, u32[]{:S(2)}) copy-start(f32[256]{0:T(256)} %copy-done.94) | copy-start | bytes 3076
  1542.8 169.0 %copy-start.35 = (f32[256,768]{1,0:T(8,128)S(1)}, f32[256,768]{1,0:T(8,128)}, u32[]{:S(2)}) copy-start(f32[256,768]{1,0:T(8,128)} %get-tuple-element.760) | copy-start | bytes 2359300
  1711.8 319.6 %reduce-scatter.73.cloned.1.call-start = ((), (), s32[]{:S(2)}) async-start(), calls=%async_computation.49 | async-start | bytes 405504
  1713.1 417.8 %copy-start.24 = (f32[256,768]{1,0:T(8,128)}, f32[256,768]{1,0:T(8,128)S(1)}, u32[]{:S(2)}) copy-start(f32[256,768]{1,0:T(8,128)S(1)} %fusion.136) | copy-start | bytes 2359300
  1714.8 416.2 %reduce-scatter.71.cloned.1.call-start = ((), (), s32[]{:S(2)}) async-start(), calls=%async_computation.48 | async-start | bytes 405504
  (138 other events, 3003.0 us)
Sparse Core Ops, SparseCore 0:
  304.8 37.5 all-gather.24
  565.3 33.5 reduce-scatter.36
  709.6 32.9 reduce-scatter.38
  841.9 34.1 reduce-scatter.40
  987.4 34.1 reduce-scatter.44
  1023.8 34.2 reduce-scatter.42
  1151.9 34.1 reduce-scatter.46
  1235.7 34.1 reduce-scatter.48
Sparse Core Ops, SparseCore 1:
  568.2 22.0 all-gather.40
  634.7 34.5 all-gather.26
  671.0 22.7 all-gather.42
  778.3 34.0 all-gather.28
  845.1 22.7 all-gather.44
  878.7 35.9 all-gather.30
  916.9 22.7 all-gather.46
  941.7 36.9 all-gather.32
  1061.8 35.9 all-gather.34
  1190.9 35.9 all-gather.36
  1274.9 35.9 all-gather.38
  1314.0 33.8 reduce-scatter.68
  1353.0 97.1 reduce-scatter.64
  1453.5 41.3 reduce-scatter.62
  1498.6 42.3 reduce-scatter.60
  1544.3 42.3 reduce-scatter.58
  1590.4 42.3 reduce-scatter.56
  1636.5 34.9 reduce-scatter.66
  1673.7 35.3 reduce-scatter.50
  1712.4 41.2 reduce-scatter.54
  1757.2 42.3 reduce-scatter.52
  1805.8 121.4 all-reduce.11
  1933.4 97.9 reduce-scatter.72
  2036.9 94.0 reduce-scatter.70
where the time goes:
time: 2150 us; the launch traced here: 2140 us
  waiting for transfers between devices  1080 us (50%)
  blocking collectives  714 us (33%)
  matrix products  132 us (6%)
  local copies, waits for them, and re-layouts  89.4 us (4%)
  other arithmetic  75.4 us (4%)
  loops' own time  26.8 us (1%)
    unnamed x38, waiting for transfers between devices  432 us
    reduce_scatter x4, waiting for transfers between devices, sum_inputs(): lax.psum_scatter(term(jnp.int32(0), own_rows * lax.axis_size('tp')).astyp...  134 us
    all_gather x4, waiting for transfers between devices, gather_grads(): return lax.all_gather(rows, 'tp', axis=0, tiled=True)  122 us
    reduce_scatter x2, waiting for transfers between devices, body(): lax.psum_scatter(w_up_grad, 'fsdp', scatter_dimension=0, tiled=True)  89.9 us
    reduce_scatter x2, waiting for transfers between devices, body(): lax.psum_scatter(w_down_grad, 'fsdp', scatter_dimension=1, tiled=True)  88.7 us
    reduce_scatter x2, waiting for transfers between devices, body(): lax.psum_scatter(w_proj_grad, 'fsdp', scatter_dimension=0, tiled=True)  84.7 us
    all_gather x1, blocking collectives, body(): lax.all_gather(row_table, ('fsdp', 'tp'), axis=1, tiled=True)  71.5 us
    all_gather x1, blocking collectives, body(): lax.all_gather(qkv_bias, ('fsdp', 'tp'), axis=2, tiled=True)  70.5 us
  transfers between devices with their start and end apart: 32, of which 24 were waited for; matrix products, arithmetic and copies ran while one was open for 6% of the time, Pallas kernels for 0%

commit v1 on v0

v1 whole, which is shorter than its diff:
```python
import functools

import jax
import jax.numpy as jnp
from jax import lax
from jax.experimental import pallas as pl
from jax.experimental.pallas import tpu as pltpu
from jax.sharding import PartitionSpec as P

HD = 64
PAIR = 128
REACH = 384
EPS = 1e-06
FILL = -1e30
ROOT_HALF = 0.7071067811865476
INV_ROOT_TWO_PI = 0.3989422804014327
HIGHEST = lax.Precision.HIGHEST
F32 = jnp.float32
BF16 = jnp.bfloat16
TILE = 512


def nn(left, right):
    return lax.dot_general(left, right, (((1,), (0,)), ((), ())), preferred_element_type=F32)


def nt(left, right):
    return lax.dot_general(left, right, (((1,), (1,)), ((), ())), preferred_element_type=F32)


def halves(array):
    middle = array.shape[1] // 2
    return array[:, :middle], array[:, middle:]


def row_norm(value):
    centered = value - jnp.mean(value, axis=-1, keepdims=True)
    scale = lax.rsqrt(jnp.mean(centered * centered, axis=-1, keepdims=True) + EPS)
    return centered * scale, scale


def row_norm_back(grad_hat, normed, scale):
    return scale * (
        grad_hat
        - jnp.mean(grad_hat, axis=-1, keepdims=True)
        - normed * jnp.mean(grad_hat * normed, axis=-1, keepdims=True)
    )


def head_mean(value):
    rows = lax.broadcasted_iota(jnp.int32, (PAIR, PAIR), 0) // HD
    cols = lax.broadcasted_iota(jnp.int32, (PAIR, PAIR), 1) // HD
    spread = jnp.where(rows == cols, 1.0 / HD, 0.0).astype(BF16)
    high = value.astype(BF16)
    low = (value - high.astype(F32)).astype(BF16)
    return nn(high, spread) + nn(low, spread)


def head_norm(value):
    centered = value - head_mean(value)
    scale = lax.rsqrt(head_mean(centered * centered) + EPS)
    return centered * scale, scale


def head_norm_back(grad_hat, normed, scale):
    return scale * (grad_hat - head_mean(grad_hat) - normed * head_mean(grad_hat * normed))


def attend_kernel(
    a_ref, own_ref, far_ref, bias_ref, q_gain_ref, k_gain_ref, q_shift_ref, seg_k_ref, seg_q_ref,
    qn_ref, kn_ref, v_ref, q_hat_ref, k_hat_ref, q_scale_ref, k_scale_ref, p_ref, o_ref, mask_ref,
):
    rows = qn_ref.shape[0]

    @pl.when(pl.program_id(0) == 0)
    def _():
        mask_ref[...] = jnp.where(seg_k_ref[...] == seg_q_ref[...], 0.0, FILL)

    near, distant = halves(a_ref[...])
    near_q, distant_q = halves(a_ref[REACH : REACH + rows, :])
    kv = nn(near, own_ref[:, PAIR:]) + nn(distant, far_ref[:, PAIR:]) + bias_ref[:, PAIR:]
    q = nn(near_q, own_ref[:, :PAIR]) + nn(distant_q, far_ref[:, :PAIR]) + bias_ref[:, :PAIR]
    q_hat, q_scale = head_norm(q)
    k_hat, k_scale = head_norm(kv[:, :PAIR])
    qn = (q_hat * q_gain_ref[...] + q_shift_ref[...]).astype(BF16)
    kn = (k_hat * k_gain_ref[...]).astype(BF16)
    v = kv[:, PAIR:].astype(BF16)
    qn_ref[...] = qn
    kn_ref[...] = kn
    v_ref[...] = v
    q_hat_ref[...] = q_hat.astype(BF16)
    k_hat_ref[...] = k_hat.astype(BF16)
    q_scale_ref[...] = q_scale.astype(BF16)
    k_scale_ref[...] = k_scale.astype(BF16)
    head_of = lax.broadcasted_iota(jnp.int32, (1, PAIR), 1) // HD
    v_t = v.T
    mixed = []
    for head in range(PAIR // HD):
        q_head = jnp.where(head_of == head, qn * HD ** (-0.5), 0.0).astype(BF16)
        scores = nt(kn, q_head) + mask_ref[...]
        weights = jnp.exp(scores - jnp.max(scores, axis=0, keepdims=True))
        total = jnp.sum(weights, axis=0, keepdims=True)
        probs = (weights * (1.0 / total)).astype(BF16)
        p_ref[head] = probs
        mixed.append(nn(v_t[head * HD : (head + 1) * HD], probs))
    o_ref[...] = jnp.concatenate(mixed, axis=0).T.astype(BF16)


def attend(a_win, w_own, w_far, bias, q_gain, k_gain, q_shift, seg_k, seg_q, rows):
    window, width = a_win.shape
    half = width // 2
    pairs = width // PAIR
    whole = lambda shape: pl.BlockSpec(shape, lambda p: (0,) * len(shape))
    col = lambda height, wide=PAIR: pl.BlockSpec((height, wide), lambda p: (0, p))
    outs = [
        (rows, width), (window, width), (window, width), (rows, width), (window, width), (rows, width), (window, width),
    ]
    return pl.pallas_call(
        attend_kernel,
        grid=(pairs,),
        in_specs=[
            whole((window, width)), col(half, 3 * PAIR), col(half, 3 * PAIR), col(1, 3 * PAIR), col(1), col(1), col(1),
            whole((window, 1)), whole((1, rows)),
        ],
        out_specs=[col(height) for height, _ in outs]
        + [pl.BlockSpec((2, window, rows), lambda p: (p, 0, 0)), col(rows)],
        out_shape=[jax.ShapeDtypeStruct(shape, BF16) for shape in outs]
        + [jax.ShapeDtypeStruct((2 * pairs, window, rows), BF16), jax.ShapeDtypeStruct((rows, width), BF16)],
        scratch_shapes=[pltpu.VMEM((window, rows), F32)],
        cost_estimate=pl.CostEstimate(
            flops=2 * window * width * width * 2 + 8 * window * rows * width * 4,
            bytes_accessed=20 * window * width,
            transcendentals=2 * pairs * window * rows,
        ),
        name="attend",
    )(a_win, w_own, w_far, bias, q_gain, k_gain, q_shift, seg_k, seg_q)


def mlp_kernel(
    o_ref, x_ref, mix_own_ref, mix_far_ref, out_shift_ref, gain_ref, shift_ref, up_own_ref, up_far_ref, up_shift_ref,
    down_own_ref, down_far_ref, last_shift_ref, next_gain_ref, next_shift_ref,
    mid_ref, m_ref, act_ref, slope_ref, x2_ref, a_ref, acc_ref,
):
    half = mix_own_ref.shape[0]
    step = pl.program_id(0)

    @pl.when(step == 0)
    def _():
        o = o_ref[...]
        mid_ref[:, :half] = x_ref[:, :half] + (nt(o, mix_own_ref[...]) + out_shift_ref[:, :half])
        mid_ref[:, half:] = x_ref[:, half:] + (nt(o, mix_far_ref[...]) + out_shift_ref[:, half:])
        hat, _ = row_norm(mid_ref[...])
        m_ref[...] = (hat * gain_ref[...] + shift_ref[...]).astype(BF16)
        acc_ref[...] = jnp.zeros_like(acc_ref)

    near, distant = halves(m_ref[...])
    hidden = nn(near, up_own_ref[...]) + nn(distant, up_far_ref[...]) + up_shift_ref[...]
    phi = 0.5 * (1.0 + lax.erf(hidden * ROOT_HALF))
    act = (hidden * phi).astype(BF16)
    act_ref[...] = act
    slope_ref[...] = (phi + hidden * jnp.exp(-0.5 * hidden * hidden) * INV_ROOT_TWO_PI).astype(BF16)
    acc_ref[:, :half] += nt(act, down_own_ref[...])
    acc_ref[:, half:] += nt(act, down_far_ref[...])

    @pl.when(step == pl.num_programs(0) - 1)
    def _():
        x2 = mid_ref[...] + (acc_ref[...] + last_shift_ref[...])
        x2_ref[...] = x2
        hat, _ = row_norm(x2)
        a_ref[...] = (hat * next_gain_ref[...] + next_shift_ref[...]).astype(BF16)


def mlp(o, x, attn_own, attn_far, out_shift, gain, shift, mlp_own, mlp_far, up_shift, last_shift, next_gain, next_shift):
    rows, width = x.shape
    half = width // 2
    hidden = up_shift.shape[1]
    steps = hidden // TILE
    whole = lambda shape: pl.BlockSpec(shape, lambda j: (0,) * len(shape))
    mix = pl.BlockSpec((half, width), lambda j: (0, 3))
    up = pl.BlockSpec((half, TILE), lambda j: (0, j))
    down = pl.BlockSpec((half, TILE), lambda j: (0, j + steps))
    row = whole((1, width))
    full = whole((rows, width))
    tall = pl.BlockSpec((rows, TILE), lambda j: (0, j))
    return pl.pallas_call(
        mlp_kernel,
        grid=(steps,),
        in_specs=[
            full, full, mix, mix, row, row, row, up, up, pl.BlockSpec((1, TILE), lambda j: (0, j)), down, down, row, row, row,
        ],
        out_specs=[full, full, tall, tall, full, full],
        out_shape=[
            jax.ShapeDtypeStruct((rows, width), F32),
            jax.ShapeDtypeStruct((rows, width), BF16),
            jax.ShapeDtypeStruct((rows, hidden), BF16),
            jax.ShapeDtypeStruct((rows, hidden), BF16),
            jax.ShapeDtypeStruct((rows, width), F32),
            jax.ShapeDtypeStruct((rows, width), BF16),
        ],
        scratch_shapes=[pltpu.VMEM((rows, width), F32)],
        cost_estimate=pl.CostEstimate(
            flops=2 * rows * width * (width + 2 * hidden),
            bytes_accessed=2 * width * (width + 2 * hidden),
            transcendentals=2 * rows * hidden,
        ),
        name="mlp",
    )(
        o, x, attn_own, attn_far, out_shift, gain, shift, mlp_own, mlp_far, up_shift, mlp_own, mlp_far, last_shift,
        next_gain, next_shift,
    )


def mlp_back_kernel(
    g_ref, down_own_ref, down_far_ref, slope_ref, up_own_ref, up_far_ref, mid_ref, gain_ref, mix_own_ref, mix_far_ref,
    gz_ref, gh_ref, up_shift_grad_ref, g1_ref, gr_ref, go_ref, small_ref, acc_ref,
):
    half = mix_own_ref.shape[0]
    step = pl.program_id(0)

    @pl.when(step == 0)
    def _():
        gz_ref[...] = g_ref[...].astype(BF16)
        acc_ref[...] = jnp.zeros_like(acc_ref)

    near, distant = halves(gz_ref[...])
    gh = ((nn(near, down_own_ref[...]) + nn(distant, down_far_ref[...])) * slope_ref[...].astype(F32)).astype(BF16)
    gh_ref[...] = gh
    up_shift_grad_ref[...] = jnp.sum(gh.astype(F32), axis=0, keepdims=True)
    acc_ref[:, :half] += nt(gh, up_own_ref[...])
    acc_ref[:, half:] += nt(gh, up_far_ref[...])

    @pl.when(step == pl.num_programs(0) - 1)
    def _():
        gm = acc_ref[...]
        hat, scale = row_norm(mid_ref[...])
        g1 = g_ref[...] + row_norm_back(gm * gain_ref[...], hat, scale)
        gr = g1.astype(BF16)
        g1_ref[...] = g1
        gr_ref[...] = gr
        small_ref[...] = jnp.zeros_like(small_ref)
        small_ref[0:1, :] = jnp.sum(gz_ref[...].astype(F32), axis=0, keepdims=True)
        small_ref[1:2, :] = jnp.sum(gr.astype(F32), axis=0, keepdims=True)
        small_ref[2:3, :] = jnp.sum(gm * hat, axis=0, keepdims=True)
        small_ref[3:4, :] = jnp.sum(gm, axis=0, keepdims=True)
        go_ref[...] = (nn(gr[:, :half], mix_own_ref[...]) + nn(gr[:, half:], mix_far_ref[...])).astype(BF16)


def mlp_back(grad, mlp_own, mlp_far, slope, mid, gain, attn_own, attn_far):
    rows, width = grad.shape
    half = width // 2
    hidden = slope.shape[1]
    steps = hidden // TILE
    whole = lambda shape: pl.BlockSpec(shape, lambda j: (0,) * len(shape))
    mix = pl.BlockSpec((half, width), lambda j: (0, 3))
    up = pl.BlockSpec((half, TILE), lambda j: (0, j))
    down = pl.BlockSpec((half, TILE), lambda j: (0, j + steps))
    full = whole((rows, width))
    tall = pl.BlockSpec((rows, TILE), lambda j: (0, j))
    return pl.pallas_call(
        mlp_back_kernel,
        grid=(steps,),
        in_specs=[full, down, down, tall, up, up, full, whole((1, width)), mix, mix],
        out_specs=[full, tall, pl.BlockSpec((1, TILE), lambda j: (0, j)), full, full, full, whole((8, width))],
        out_shape=[
            jax.ShapeDtypeStruct((rows, width), BF16),
            jax.ShapeDtypeStruct((rows, hidden), BF16),
            jax.ShapeDtypeStruct((1, hidden), F32),
            jax.ShapeDtypeStruct((rows, width), F32),
            jax.ShapeDtypeStruct((rows, width), BF16),
            jax.ShapeDtypeStruct((rows, width), BF16),
            jax.ShapeDtypeStruct((8, width), F32),
        ],
        scratch_shapes=[pltpu.VMEM((rows, width), F32)],
        cost_estimate=pl.CostEstimate(
            flops=2 * rows * width * (width + 2 * hidden),
            bytes_accessed=2 * width * (width + 2 * hidden),
            transcendentals=0,
        ),
        name="mlp_back",
    )(grad, mlp_own, mlp_far, slope, mlp_own, mlp_far, mid, gain, attn_own, attn_far)


def attend_back_kernel(
    go_ref, qn_ref, kn_ref, v_ref, q_hat_ref, k_hat_ref, q_scale_ref, k_scale_ref, p_ref, own_ref, far_ref, q_gain_ref,
    k_gain_ref, gq_ref, gkv_ref, mine_ref, left_ref, right_ref, small_ref, acc_ref,
):
    rows = go_ref.shape[0]
    half = own_ref.shape[0]
    step = pl.program_id(0)

    @pl.when(step == 0)
    def _():
        acc_ref[...] = jnp.zeros_like(acc_ref)

    head_of = lax.broadcasted_iota(jnp.int32, (1, PAIR), 1) // HD
    go, qn, kn, v = go_ref[...], qn_ref[...], kn_ref[...], v_ref[...]
    k_t = kn.T
    grad_q, grad_k, grad_v = [], 0.0, 0.0
    for head in range(PAIR // HD):
        go_head = jnp.where(head_of == head, go, 0.0).astype(BF16)
        q_head = jnp.where(head_of == head, qn * HD ** (-0.5), 0.0).astype(BF16)
        stored = p_ref[head]
        probs = stored.astype(F32)
        grad_probs = nt(v, go_head)
        delta = jnp.sum(probs * grad_probs, axis=0, keepdims=True)
        grad_scores = (probs * (grad_probs - delta)).astype(BF16)
        grad_v += nn(stored, go_head)
        grad_k += nn(grad_scores, q_head)
        grad_q.append(nn(k_t[head * HD : (head + 1) * HD], grad_scores))
    grad_q = jnp.concatenate(grad_q, axis=0).T * HD ** (-0.5)
    q_hat = q_hat_ref[...].astype(F32)
    k_hat = k_hat_ref[...].astype(F32)
    gq = head_norm_back(grad_q * q_gain_ref[...], q_hat, q_scale_ref[...].astype(F32)).astype(BF16)
    gk = head_norm_back(grad_k * k_gain_ref[...], k_hat, k_scale_ref[...].astype(F32)).astype(BF16)
    gv = grad_v.astype(BF16)
    gkv = jnp.concatenate([gk, gv], axis=1)
    gq_ref[...] = gq
    gkv_ref[...] = gkv
    small_ref[...] = jnp.zeros_like(small_ref)
    small_ref[0:1, :] = jnp.sum(grad_q * q_hat, axis=0, keepdims=True)
    small_ref[1:2, :] = jnp.sum(grad_k * k_hat, axis=0, keepdims=True)
    small_ref[2:3, :] = jnp.sum(grad_q, axis=0, keepdims=True)
    small_ref[3:4, :] = jnp.sum(gq.astype(F32), axis=0, keepdims=True)
    small_ref[4:5, :] = jnp.sum(gk.astype(F32), axis=0, keepdims=True)
    small_ref[5:6, :] = jnp.sum(gv.astype(F32), axis=0, keepdims=True)
    acc_ref[:, :half] += nt(gkv, own_ref[:, PAIR:])
    acc_ref[:, half:] += nt(gkv, far_ref[:, PAIR:])
    acc_ref[REACH : REACH + rows, :half] += nt(gq, own_ref[:, :PAIR])
    acc_ref[REACH : REACH + rows, half:] += nt(gq, far_ref[:, :PAIR])

    @pl.when(step == pl.num_programs(0) - 1)
    def _():
        left_ref[...] = acc_ref[:REACH, :].astype(BF16)
        mine_ref[...] = acc_ref[REACH : REACH + rows, :]
        right_ref[...] = acc_ref[REACH + rows :, :].astype(BF16)


def attend_back(go, qn, kn, v, q_hat, k_hat, q_scale, k_scale, probs, attn_own, attn_far, q_gain, k_gain):
    rows, width = go.shape
    window = kn.shape[0]
    half = width // 2
    pairs = width // PAIR
    whole = lambda shape: pl.BlockSpec(shape, lambda p: (0,) * len(shape))
    col = lambda height, wide=PAIR: pl.BlockSpec((height, wide), lambda p: (0, p))
    return pl.pallas_call(
        attend_back_kernel,
        grid=(pairs,),
        in_specs=[
            col(rows), col(rows), col(window), col(window), col(rows), col(window), col(rows), col(window),
            pl.BlockSpec((2, window, rows), lambda p: (p, 0, 0)), col(half, 3 * PAIR), col(half, 3 * PAIR), col(1), col(1),
        ],
        out_specs=[
            col(rows), col(window, 2 * PAIR), whole((rows, width)), whole((REACH, width)), whole((REACH, width)), col(8),
        ],
        out_shape=[
            jax.ShapeDtypeStruct((rows, width), BF16),
            jax.ShapeDtypeStruct((window, 2 * width), BF16),
            jax.ShapeDtypeStruct((rows, width), F32),
            jax.ShapeDtypeStruct((REACH, width), BF16),
            jax.ShapeDtypeStruct((REACH, width), BF16),
            jax.ShapeDtypeStruct((8, width), F32),
        ],
        scratch_shapes=[pltpu.VMEM((window, width), F32)],
        cost_estimate=pl.CostEstimate(
            flops=2 * window * width * width * 2 + 20 * window * rows * width * 2,
            bytes_accessed=20 * window * width,
            transcendentals=0,
        ),
        name="attend_back",
    )(go, qn, kn, v, q_hat, k_hat, q_scale, k_scale, probs, attn_own, attn_far, q_gain, k_gain)


def attn_weight_kernel(a_ref, gq_ref, gkv_ref, gr_ref, o_ref, keep_ref, send_ref, a_t_ref, gr_t_ref):
    rows = gq_ref.shape[0]
    half = keep_ref.shape[0]
    step = pl.program_id(0)
    pairs = pl.num_programs(0) - 2

    @pl.when(step == 0)
    def _():
        a_t_ref[...] = a_ref[...].T
        gr_t_ref[...] = gr_ref[...].T

    @pl.when(step < pairs)
    def _():
        for part, ref in ((slice(0, half), keep_ref), (slice(half, 2 * half), send_ref)):
            ref[:, :PAIR] = nn(a_t_ref[part, REACH : REACH + rows], gq_ref[...]).astype(BF16)
            ref[:, PAIR:] = nn(a_t_ref[part, :], gkv_ref[...]).astype(BF16)

    @pl.when(step >= pairs)
    def _():
        for part, ref in ((slice(0, half), keep_ref), (slice(half, 2 * half), send_ref)):
            ref[...] = nn(gr_t_ref[part, :], o_ref[...]).astype(BF16)


def attn_weight_grads(a_win, gq, gkv, gr, o):
    window, width = a_win.shape
    rows = gr.shape[0]
    half = width // 2
    pairs = width // PAIR
    wide = 3 * PAIR
    whole = lambda shape: pl.BlockSpec(shape, lambda p: (0,) * len(shape))
    out = pl.BlockSpec((half, wide), lambda p: (0, p))
    return pl.pallas_call(
        attn_weight_kernel,
        grid=(pairs + 2,),
        in_specs=[
            whole((window, width)),
            pl.BlockSpec((rows, PAIR), lambda p: (0, jnp.minimum(p, pairs - 1))),
            pl.BlockSpec((window, 2 * PAIR), lambda p: (0, jnp.minimum(p, pairs - 1))),
            whole((rows, width)),
            pl.BlockSpec((rows, wide), lambda p: (0, jnp.maximum(p - pairs, 0))),
        ],
        out_specs=[out, out],
        out_shape=[jax.ShapeDtypeStruct((half, 4 * width), BF16)] * 2,
        scratch_shapes=[pltpu.VMEM((width, window), BF16), pltpu.VMEM((width, rows), BF16)],
        cost_estimate=pl.CostEstimate(
            flops=2 * width * width * (2 * window + 2 * rows), bytes_accessed=8 * width * width, transcendentals=0
        ),
        name="attn_weight_grads",
    )(a_win, gq, gkv, gr, o)


def mlp_weight_kernel(m_ref, gh_ref, gz_ref, act_ref, keep_ref, send_ref, m_t_ref, gz_t_ref):
    half = keep_ref.shape[0]
    step = pl.program_id(0)
    steps = pl.num_programs(0) // 2

    @pl.when(step == 0)
    def _():
        m_t_ref[...] = m_ref[...].T
        gz_t_ref[...] = gz_ref[...].T

    @pl.when(step < steps)
    def _():
        keep_ref[...] = nn(m_t_ref[:half, :], gh_ref[...]).astype(BF16)
        send_ref[...] = nn(m_t_ref[half:, :], gh_ref[...]).astype(BF16)

    @pl.when(step >= steps)
    def _():
        keep_ref[...] = nn(gz_t_ref[:half, :], act_ref[...]).astype(BF16)
        send_ref[...] = nn(gz_t_ref[half:, :], act_ref[...]).astype(BF16)


def mlp_weight_grads(m, gh, gz, act):
    rows, width = m.shape
    half = width // 2
    hidden = gh.shape[1]
    steps = hidden // TILE
    whole = lambda shape: pl.BlockSpec(shape, lambda j: (0,) * len(shape))
    out = pl.BlockSpec((half, TILE), lambda j: (0, j))
    return pl.pallas_call(
        mlp_weight_kernel,
        grid=(2 * steps,),
        in_specs=[
            whole((rows, width)),
            pl.BlockSpec((rows, TILE), lambda j: (0, jnp.minimum(j, steps - 1))),
            whole((rows, width)),
            pl.BlockSpec((rows, TILE), lambda j: (0, jnp.maximum(j - steps, 0))),
        ],
        out_specs=[out, out],
        out_shape=[jax.ShapeDtypeStruct((half, 2 * hidden), BF16)] * 2,
        scratch_shapes=[pltpu.VMEM((width, rows), BF16), pltpu.VMEM((width, rows), BF16)],
        cost_estimate=pl.CostEstimate(
            flops=4 * width * hidden * rows, bytes_accessed=4 * width * hidden, transcendentals=0
        ),
        name="mlp_weight_grads",
    )(m, gh, gz, act)


def flip(array, bit, axis="fsdp"):
    size = lax.axis_size(axis)
    return lax.ppermute(array, axis, [(i, i ^ (1 << bit)) for i in range(size)])


def ring(array):
    size = lax.axis_size("tp")
    return lax.ppermute(array, "tp", [(i, (i + 1) % size) for i in range(size)])


def hop(array, distance):
    size = lax.axis_size("tp")
    return lax.ppermute(array, "tp", [(i, i + distance) for i in range(size) if 0 <= i + distance < size])


def bits_of(size):
    return size.bit_length() - 1


def row_bits(first_top):
    count = bits_of(lax.axis_size("fsdp"))
    tops = [count - 1, count - 2] if first_top else [count - 2, count - 1]
    return list(range(1, count - 2)), tops


def over_tp(block):
    pieces = [block]
    for _ in range(lax.axis_size("tp") - 1):
        pieces.append(ring(pieces[-1]))
    return pieces


def over_rows(block, first_top):
    low, tops = row_bits(first_top)
    have = []
    for bit in low + tops:
        axis = sum(other > bit for other in have)
        block = jnp.stack([block, flip(block, bit)], axis=axis)
        have.append(bit)
    return block.reshape((-1, block.shape[-1]))


def add(left, right, kind=BF16):
    return (left.astype(F32) + right.astype(F32)).astype(kind)


def reduce_rows(keep, send, first_top):
    low, tops = row_bits(first_top)
    block = add(keep, flip(send, 0))
    order = tops + low[::-1]
    have = sorted(order, reverse=True)
    block = block.reshape((2,) * len(have) + (-1, block.shape[-1]))
    for bit in order:
        axis = have.index(bit)
        mine = lax.index_in_dim(block, 0, axis, keepdims=False)
        other = lax.index_in_dim(block, 1, axis, keepdims=False)
        block = add(mine, flip(other, bit))
        have.remove(bit)
    return block


def reduce_tp(pieces):
    total = pieces[1]
    for piece in pieces[2:]:
        total = add(ring(total), piece)
    return add(ring(total), pieces[0], F32)


def gather_layer(w_qkv, w_out, w_fc1, w_fc2, first_top):
    chunk, _, head_cols = w_qkv.shape
    size = lax.axis_size("tp")
    pairs = size * head_cols // PAIR
    pieces = over_tp(jnp.concatenate([w_qkv.reshape(chunk, 3 * head_cols), w_out.T], axis=1))
    qkv = jnp.concatenate([piece[:, : 3 * head_cols].reshape(chunk, 3, head_cols) for piece in pieces], axis=2)
    qkv = qkv.reshape(chunk, 3, pairs, PAIR).transpose(0, 2, 1, 3).reshape(chunk, -1)
    attn = jnp.concatenate([qkv] + [piece[:, 3 * head_cols :] for piece in pieces], axis=1)
    attn = over_rows(attn, first_top)
    pieces = over_tp(jnp.concatenate([w_fc1, w_fc2.T], axis=1))
    cols = w_fc1.shape[1]
    mlp_w = jnp.concatenate([piece[:, :cols] for piece in pieces] + [piece[:, cols:] for piece in pieces], axis=1)
    mlp_w = over_rows(mlp_w, not first_top)
    return attn, flip(attn, 0), mlp_w, flip(mlp_w, 0)


def split_tp(array, axis=-1):
    return jnp.split(array, lax.axis_size("tp"), axis=axis)


def reduce_attn(keep, send, first_top):
    block = reduce_rows(keep, send, first_top)
    chunk, total = block.shape
    width = total // 4
    qkv = block[:, : 3 * width].reshape(chunk, width // PAIR, 3, PAIR).transpose(0, 2, 1, 3).reshape(chunk, 3, width)
    pieces = [
        jnp.concatenate([left.reshape(chunk, -1), right], axis=1)
        for left, right in zip(split_tp(qkv), split_tp(block[:, 3 * width :]))
    ]
    total = reduce_tp(pieces)
    cols = total.shape[1] // 4
    return total[:, : 3 * cols].reshape(chunk, 3, cols), total[:, 3 * cols :].T


def reduce_mlp(keep, send, first_top):
    block = reduce_rows(keep, send, first_top)
    hidden = block.shape[1] // 2
    pieces = [
        jnp.concatenate([left, right], axis=1)
        for left, right in zip(split_tp(block[:, :hidden]), split_tp(block[:, hidden:]))
    ]
    total = reduce_tp(pieces)
    cols = total.shape[1] // 2
    return total[:, :cols], total[:, cols:].T


def body(
    tokens, segment_ids, patch_pos, row_table, col_table, ln_gain, ln_bias, qkv_bias, qk_gain, query_bias, out_bias,
    fc1_bias, fc2_bias, w_qkv, w_out, w_fc1, w_fc2, cotangent,
):
    layers = w_qkv.shape[0]
    rows, width = tokens.shape
    fsdp, tp = lax.axis_size("fsdp"), lax.axis_size("tp")
    f_index, t_index = lax.axis_index("fsdp"), lax.axis_index("tp")
    hidden = fc1_bias.shape[1] * fsdp * tp
    grid = row_table.shape[0]
    fine = width // (fsdp * tp)
    parts = hidden // width

    place = jnp.arange(width, dtype=jnp.int32)
    chunk = width // fsdp
    slot = place // chunk
    away = (slot % (fsdp // 2)) * 2 + slot // (fsdp // 2)
    feature_at = (f_index ^ away) * chunk + place % chunk
    head_cols = width // tp
    head_at = ((t_index - place // head_cols) % tp) * head_cols + place % head_cols
    far = place // fine
    arrived_at = ((f_index ^ (far // tp)) * tp + (t_index ^ (far % tp))) * fine + place % fine
    to_feature = (arrived_at[:, None] == feature_at[None, :]).astype(BF16)
    to_head = (arrived_at[:, None] == head_at[None, :]).astype(BF16)
    reorder = (place[:, None] == feature_at[None, :]).astype(BF16)
    device = jnp.arange(fsdp * tp, dtype=jnp.int32)
    device_at = (f_index ^ (device // tp)) * tp + (t_index ^ (device % tp))
    wanted = ((t_index - device // fsdp) % tp) * fsdp + device % fsdp
    to_hidden = (wanted[:, None] == device_at[None, :]).astype(BF16)

    shares = [row_table, col_table] + [
        item.reshape(-1, fine) for item in (ln_gain, ln_bias, out_bias, fc2_bias, qkv_bias, qk_gain, query_bias)
    ]
    small = jnp.concatenate(shares + [fc1_bias.reshape(layers * parts, fine)], axis=0)
    count = small.shape[0]
    flat = small.reshape(1, -1)
    for bit in range(bits_of(tp)):
        flat = jnp.concatenate([flat, flip(flat, bit, "tp")], axis=0)
    for bit in range(bits_of(fsdp)):
        flat = jnp.concatenate([flat, flip(flat, bit)], axis=0)
    gathered = flat.reshape(fsdp * tp, count, fine)
    lined = gathered.transpose(1, 0, 2).reshape(count, width)
    wide = 2 * grid + 6 * layers
    by_feature = jnp.dot(lined[:wide], to_feature, preferred_element_type=F32)
    by_head = jnp.dot(lined[wide : wide + 6 * layers], to_head, preferred_element_type=F32)
    up_shift = jnp.einsum(
        "or,rlsi->losi",
        to_hidden,
        gathered[:, wide + 6 * layers :].reshape(fsdp * tp, layers, parts, fine),
        preferred_element_type=F32,
    ).reshape(layers, 1, hidden)
    rows_full = by_feature[:grid].astype(BF16)
    cols_full = by_feature[grid : 2 * grid].astype(BF16)
    rest = by_feature[2 * grid :]
    gains = rest[: 2 * layers].reshape(layers, 2, 1, width)
    shifts = rest[2 * layers : 4 * layers].reshape(layers, 2, 1, width)
    out_shift = rest[4 * layers : 5 * layers].reshape(layers, 1, width)
    last_shift = rest[5 * layers :].reshape(layers, 1, width)
    pairs = width // PAIR
    proj_shift = by_head[: 3 * layers].reshape(layers, 3, pairs, PAIR).transpose(0, 2, 1, 3).reshape(layers, 1, 3 * width)
    head_gain = by_head[3 * layers : 5 * layers].reshape(layers, 2, 1, width)
    head_shift = by_head[5 * layers :].reshape(layers, 1, width)

    weights = [
        gather_layer(w_qkv[layer], w_out[layer], w_fc1[layer], w_fc2[layer], layer % 2 == 0) for layer in range(layers)
    ]

    grid_ids = jnp.arange(grid, dtype=jnp.int32)
    row_hot = patch_pos[0][:, None] == grid_ids[None, :]
    col_hot = patch_pos[1][:, None] == grid_ids[None, :]
    residual = (
        jnp.dot(tokens, reorder, preferred_element_type=F32)
        + jnp.dot(row_hot.astype(BF16), rows_full, preferred_element_type=F32)
        + jnp.dot(col_hot.astype(BF16), cols_full, preferred_element_type=F32)
    )
    segments = segment_ids[0]
    padded = jnp.pad(segments, (REACH, REACH), constant_values=-1)
    seg_k = lax.dynamic_slice_in_dim(padded, t_index * rows, rows + 2 * REACH).reshape(-1, 1)
    seg_q = lax.dynamic_slice_in_dim(segments, t_index * rows, rows).reshape(1, -1)
    spill = REACH - rows

    hat, _ = row_norm(residual)
    a_own = (hat * gains[0, 0] + shifts[0, 0]).astype(BF16)
    saved = []
    for layer in range(layers):
        attn_own, attn_far, mlp_own, mlp_far = weights[layer]
        a_win = jnp.concatenate(
            [hop(a_own[rows - spill :], 2), hop(a_own, 1), a_own, hop(a_own, -1), hop(a_own[:spill], -2)], axis=0
        )
        qn, kn, v, q_hat, k_hat, q_scale, k_scale, probs, o = attend(
            a_win, attn_own, attn_far, proj_shift[layer], head_gain[layer, 0], head_gain[layer, 1], head_shift[layer],
            seg_k, seg_q, rows,
        )
        after = min(layer + 1, layers - 1)
        mid, m, act, slope, x2, a_next = mlp(
            o, residual, attn_own, attn_far, out_shift[layer], gains[layer, 1], shifts[layer, 1], mlp_own, mlp_far,
            up_shift[layer], last_shift[layer], gains[after, 0], shifts[after, 0],
        )
        saved.append((residual, a_win, qn, kn, v, q_hat, k_hat, q_scale, k_scale, probs, o, mid, m, act, slope))
        residual, a_own = x2, a_next

    restore = functools.partial(
        lax.dot_general, dimension_numbers=(((1,), (1,)), ((), ())), precision=HIGHEST, preferred_element_type=F32
    )
    exact = reorder.astype(F32)
    activations = restore(residual, exact)
    grad = jnp.dot(cotangent, exact, precision=HIGHEST, preferred_element_type=F32)
    kept = [None] * layers
    w_qkv_grad, w_out_grad, w_fc1_grad, w_fc2_grad = ([None] * layers for _ in range(4))
    for layer in reversed(range(layers)):
        attn_own, attn_far, mlp_own, mlp_far = weights[layer]
        x, a_win, qn, kn, v, q_hat, k_hat, q_scale, k_scale, probs, o, mid, m, act, slope = saved[layer]
        gz, gh, up_grad, g1, gr, go, mlp_small = mlp_back(
            grad, mlp_own, mlp_far, slope, mid, gains[layer, 1], attn_own, attn_far
        )
        keep, send = mlp_weight_grads(m, gh, gz, act)
        w_fc1_grad[layer], w_fc2_grad[layer] = reduce_mlp(keep, send, layer % 2 == 0)
        gq, gkv, mine, left, right, attn_small = attend_back(
            go, qn, kn, v, q_hat, k_hat, q_scale, k_scale, probs, attn_own, attn_far, head_gain[layer, 0],
            head_gain[layer, 1],
        )
        keep, send = attn_weight_grads(a_win, gq, gkv, gr, o)
        w_qkv_grad[layer], w_out_grad[layer] = reduce_attn(keep, send, layer % 2 == 1)
        ends = jnp.concatenate([hop(right[rows:], 2), hop(left[:spill], -2)], axis=0).astype(F32)
        attn_grad = mine + hop(right[:rows], 1).astype(F32) + hop(left[spill:], -1).astype(F32) + ends
        hat, scale = row_norm(x)
        grad = g1 + row_norm_back(attn_grad * gains[layer, 0], hat, scale)
        kept[layer] = (
            jnp.sum(attn_grad * hat, axis=0), jnp.sum(attn_grad, axis=0), mlp_small, attn_small,
            up_grad.reshape(parts, width),
        )

    token_grad = restore(grad, exact)
    row_grad = jnp.einsum("tg,td->gd", row_hot.astype(F32), grad, precision=HIGHEST)
    col_grad = jnp.einsum("tg,td->gd", col_hot.astype(F32), grad, precision=HIGHEST)
    featured = [row_grad, col_grad]
    featured.append(jnp.stack([line for a_gain, _, sums, _, _ in kept for line in (a_gain, sums[2])]))
    featured.append(jnp.stack([line for _, a_shift, sums, _, _ in kept for line in (a_shift, sums[3])]))
    featured.append(jnp.stack([sums[1] for _, _, sums, _, _ in kept]))
    featured.append(jnp.stack([sums[0] for _, _, sums, _, _ in kept]))
    headed = jnp.concatenate(
        [sums[3:6] for _, _, _, sums, _ in kept]
        + [sums[0:2] for _, _, _, sums, _ in kept]
        + [sums[2:3] for _, _, _, sums, _ in kept]
    )
    spread = jnp.concatenate(
        [restore(jnp.concatenate(featured), to_feature.astype(F32)), restore(headed, to_head.astype(F32))]
    )
    spread = spread.reshape(-1, fsdp * tp, fine).transpose(1, 0, 2)
    up_all = jnp.stack([item[4] for item in kept]).reshape(layers, fsdp * tp, parts * fine)
    up_all = jnp.einsum("or,lok->rlk", to_hidden.astype(F32), up_all, precision=HIGHEST)
    flat = jnp.concatenate([spread.reshape(fsdp * tp, -1), up_all.reshape(fsdp * tp, -1)], axis=1)
    for bit in reversed(range(bits_of(fsdp))):
        middle = flat.shape[0] // 2
        flat = flat[:middle] + flip(flat[middle:], bit)
    for bit in reversed(range(bits_of(tp))):
        middle = flat.shape[0] // 2
        flat = flat[:middle] + flip(flat[middle:], bit, "tp")
    flat = flat.reshape(-1)
    sizes = [grid, grid, 2 * layers, 2 * layers, layers, layers, 3 * layers, 2 * layers, layers, layers * parts]
    shapes = [
        (grid, fine), (grid, fine), (layers, 2, fine), (layers, 2, fine), (layers, fine), (layers, fine),
        (layers, 3, fine), (layers, 2, fine), (layers, fine), (layers, parts * fine),
    ]
    found = []
    start = 0
    for lines, shape in zip(sizes, shapes):
        found.append(flat[start : start + lines * fine].reshape(shape))
        start += lines * fine
    rows_g, cols_g, gain_g, shift_g, out_g, last_g, proj_g, head_gain_g, head_shift_g, up_g = found
    return (
        activations, token_grad, rows_g, cols_g, gain_g, shift_g, proj_g, head_gain_g, head_shift_g, out_g, up_g, last_g,
        jnp.stack(w_qkv_grad), jnp.stack(w_out_grad), jnp.stack(w_fc1_grad), jnp.stack(w_fc2_grad),
    )


def solution(mesh):
    both = ("fsdp", "tp")
    in_specs = (
        P(both, None), P("fsdp", None), P(None, both), P(None, both), P(None, both), P(None, None, both),
        P(None, None, both), P(None, None, both), P(None, None, both), P(None, both), P(None, both), P(None, both),
        P(None, both), P(None, "fsdp", None, "tp"), P(None, "tp", "fsdp"), P(None, "fsdp", "tp"), P(None, "tp", "fsdp"),
        P(both, None),
    )
    out_specs = (
        P(both, None), P(both, None), P(None, both), P(None, both), P(None, None, both), P(None, None, both),
        P(None, None, both), P(None, None, both), P(None, both), P(None, both), P(None, both), P(None, both),
        P(None, "fsdp", None, "tp"), P(None, "tp", "fsdp"), P(None, "fsdp", "tp"), P(None, "tp", "fsdp"),
    )
    return jax.shard_map(body, mesh=mesh, in_specs=in_specs, out_specs=out_specs, check_vma=False)
```

time: 2150 us -> 884 us (0.41)
  blocking collectives: 714 us -> 0 us
  waiting for transfers between devices: 1080 us -> 378 us
  Pallas kernels: 0 us -> 185 us
  matrix products: 132 us -> 16.8 us
  starting transfers between devices: 2.59 us -> 84.6 us
  local copies, waits for them, and re-layouts: 89.4 us -> 136 us
  loops' own time: 26.8 us -> 0 us
    all_gather x14 -> x0, blocking collectives: 714 us -> none  [the longest x1 71.5 us: body(): lax.all_gather(row_table, ('fsdp', 'tp'), axis=1, tiled=True)]
    reduce_scatter x14 -> x0, waiting for transfers between devices: 466 us -> none  [the longest x4 134 us: sum_inputs(): lax.psum_scatter(term(jnp.int32(0), own_rows * lax.axis_size('tp')).astyp...]
    unnamed x38 -> x0, waiting for transfers between devices: 432 us -> none
    ppermute x0 -> x74, waiting for transfers between devices: none -> 378 us  [the longest x34 258 us: flip(): return lax.ppermute(array, axis, [(i, i ^ 1 << bit) for i in range(size)])]
    pallas_call x0 -> x12, Pallas kernels: none -> 185 us  [the longest x2 47.7 us: attend(): pl.pallas_call(attend_kernel, grid=(pairs,), in_specs=[whole((window, wid...]
    all_gather x12 -> x0, waiting for transfers between devices: 182 us -> none  [the longest x4 122 us: gather_grads(): return lax.all_gather(rows, 'tp', axis=0, tiled=True)]
    dot_general x52 -> x14, matrix products: 122 us -> 16.8 us  [the longest x1 2.2 us: body(): token_grad = restore(grad, exact)]
    ppermute x0 -> x74, starting transfers between devices: none -> 84.6 us  [the longest x16 37.6 us: hop(): lax.ppermute(array, 'tp', [(i, i + distance) for i in range(size) if 0 <=...]
  transfers between devices with their start and end apart: 32 -> 74, of which waited for: 24 -> 35; matrix products, arithmetic and copies ran while one was open for 6% -> 23% of each run, Pallas kernels for 0% -> 16%
where the time goes in v1:
time: 884 us; the launch traced here: 872 us
  waiting for transfers between devices  378 us (43%)
  Pallas kernels  185 us (21%)
  local copies, waits for them, and re-layouts  136 us (15%)
  starting transfers between devices  84.6 us (10%)
  other arithmetic  67.9 us (8%)
  matrix products  16.8 us (2%)
    ppermute x34, waiting for transfers between devices, flip(): return lax.ppermute(array, axis, [(i, i ^ 1 << bit) for i in range(size)])  258 us
    ppermute x24, waiting for transfers between devices, ring(): return lax.ppermute(array, 'tp', [(i, (i + 1) % size) for i in range(size)])  74.5 us
    pallas_call x2, Pallas kernels, attend(): pl.pallas_call(attend_kernel, grid=(pairs,), in_specs=[whole((window, wid...  47.7 us
    ppermute x16, waiting for transfers between devices, hop(): lax.ppermute(array, 'tp', [(i, i + distance) for i in range(size) if 0 <=...  46 us
    pallas_call x2, Pallas kernels, attend_back(): pl.pallas_call(attend_back_kernel, grid=(pairs,), in_specs=[col(rows), co...  44.7 us
    ppermute x16, starting transfers between devices, hop(): lax.ppermute(array, 'tp', [(i, i + distance) for i in range(size) if 0 <=...  37.6 us
    ppermute x34, starting transfers between devices, flip(): return lax.ppermute(array, axis, [(i, i ^ 1 << bit) for i in range(size)])  29.3 us
    unnamed x199, local copies, waits for them, and re-layouts  24.5 us
  transfers between devices with their start and end apart: 74, of which 35 were waited for; matrix products, arithmetic and copies ran while one was open for 23% of the time, Pallas kernels for 16%

profile of v1, /device:TPU:0, one launch (start us, length us, event | category | flops | bytes accessed | tf_op | source)
XLA Modules:
  0.0 871.6 jit_solution(11600754602293966658)
XLA Ops:
  8.0 3.1 collective-permute-start
  14.8 3.1 collective-permute-start.31
  30.3 9.5 %collective-permute-done.1 = bf16[2,3840]{1,0:T(2,128)(2,1)S(1)} collective-permute-done((bf16[2,3840]{1,0:T(2,128)(2,1)S(1)}, bf16[2,3840]{1,0:T(2,128)(2,1)S(1)}, u32[]{:S(2)}, u32[]{:S(2)}) %collective-permute-start.1) | collective-permute-done | bytes 15392 | tf_op jit(solution)/shard_map/ppermute | solution.py:473
  65.2 5.3 collective-permute-done.32
  71.4 5.4 collective-permute-done.16
  77.0 6.1 collective-permute-done.33
  83.8 4.1 collective-permute-done.17
  94.8 22.2 %collective-permute-done.18 = bf16[96,6144]{1,0:T(8,128)(2,1)S(1)} collective-permute-done((bf16[96,6144]{1,0:T(8,128)(2,1)S(1)}, bf16[96,6144]{1,0:T(8,128)(2,1)S(1)}, u32[]{:S(2)}, u32[]{:S(2)}) %collective-permute-start.18) | collective-permute-done | bytes 1179680 | tf_op jit(solution)/shard_map/ppermute | solution.py:473
  159.1 49.9 %collective-permute-done.12 = bf16[96,3072]{1,0:T(8,128)(2,1)} collective-permute-done((bf16[96,3072]{1,0:T(8,128)(2,1)}, bf16[96,3072]{1,0:T(8,128)(2,1)}, u32[]{:S(2)}, u32[]{:S(2)}) %collective-permute-start.12) | collective-permute-done | bytes 589856 | tf_op jit(solution)/shard_map/ppermute | solution.py:473
  213.4 4.1 fusion.102
  218.0 4.3 pad_maximum_fusion
  228.2 71.7 %collective-permute-done.28 = bf16[96,3072]{1,0:T(8,128)(2,1)S(1)} collective-permute-done((bf16[96,3072]{1,0:T(8,128)(2,1)S(1)}, bf16[96,3072]{1,0:T(8,128)(2,1)S(1)}, u32[]{:S(2)}, u32[]{:S(2)}) %collective-permute-start.28) | collective-permute-done | bytes 589856 | tf_op jit(solution)/shard_map/ppermute | solution.py:473
  331.5 9.4 %collective-permute-done.7 = bf16[256,768]{1,0:T(8,128)(2,1)S(1)} collective-permute-done((bf16[256,768]{1,0:T(8,128)(2,1)S(1)}, bf16[256,768]{1,0:T(8,128)(2,1)S(1)}, u32[]{:S(2)}, u32[]{:S(2)}) %collective-permute-start.7) | collective-permute-done | bytes 393248 | tf_op jit(solution)/shard_map/ppermute | solution.py:483
  343.1 10.5 %collective-permute-done.8 = bf16[128,768]{1,0:T(8,128)(2,1)S(1)} collective-permute-done((bf16[128,768]{1,0:T(8,128)(2,1)}, bf16[128,768]{1,0:T(8,128)(2,1)S(1)}, u32[]{:S(2)}, u32[]{:S(2)}) %collective-permute-start.8) | collective-permute-done | bytes 196640 | tf_op jit(solution)/shard_map/ppermute | solution.py:483
  357.8 23.9 %attend.2 = (bf16[256,768]{1,0:T(8,128)(2,1)}, bf16[1024,768]{1,0:T(8,128)(2,1)}, bf16[1024,768]{1,0:T(8,128)(2,1)}, bf16[256,768]{1,0:T(8,128)(2,1)}, bf16[1024...) custom-call(bf16[1024,768]{1,0:T(8,128)(2,1)} %copy-done.47, ...), custom_call_target="tpu_custom_call" | custom-call | flops 8858370048 | bytes 15728640 | tf_op jit(solution)/shard_map/attend/pallas_call | solution.py:118
  381.7 12.2 %mlp.2 = (f32[256,768]{1,0:T(8,128)}, bf16[256,768]{1,0:T(8,128)(2,1)}, bf16[256,3072]{1,0:T(8,128)(2,1)}, bf16[256,3072]{1,0:T(8,128)(2,1)}, f32[256,768]{1,0:T(8,128)}, /*index=5*/bf16[256,768]{1,0:T(8,128)(2,1)}) custom-call(bf16[256,768]{1,0:T(8,128)(2,1)} %get-tuple-element.79.o_ref, f32[256,768]{1,0:T(8,128)} %copy-done.2, ...), custom_call_target="tpu_custom_call" | custom-call | flops 2717908992 | bytes 10616832 | tf_op jit(solution)/shard_map/mlp/pallas_call | solution.py:185
  397.7 4.9 collective-permute-start.21
  404.7 4.4 collective-permute-done.21
  410.7 12.2 %collective-permute-done.24 = bf16[128,768]{1,0:T(8,128)(2,1)S(1)} collective-permute-done((bf16[128,768]{1,0:T(8,128)(2,1)S(1)}, bf16[128,768]{1,0:T(8,128)(2,1)S(1)}, u32[]{:S(2)}, u32[]{:S(2)}) %collective-permute-start.24) | collective-permute-done | bytes 196640 | tf_op jit(solution)/shard_map/ppermute | solution.py:483
  424.1 23.9 %attend.3 = (bf16[256,768]{1,0:T(8,128)(2,1)}, bf16[1024,768]{1,0:T(8,128)(2,1)}, bf16[1024,768]{1,0:T(8,128)(2,1)}, bf16[256,768]{1,0:T(8,128)(2,1)}, bf16[1024...) custom-call(bf16[1024,768]{1,0:T(8,128)(2,1)} %copy-done.46, ...), custom_call_target="tpu_custom_call" | custom-call | flops 8858370048 | bytes 15728640 | tf_op jit(solution)/shard_map/attend/pallas_call | solution.py:118
  448.0 12.2 %mlp.3 = (f32[256,768]{1,0:T(8,128)}, bf16[256,768]{1,0:T(8,128)(2,1)}, bf16[256,3072]{1,0:T(8,128)(2,1)}, bf16[256,3072]{1,0:T(8,128)(2,1)}, f32[256,768]{1,0:T(8,128)}, /*index=5*/bf16[256,768]{1,0:T(8,128)(2,1)}) custom-call(bf16[256,768]{1,0:T(8,128)(2,1)} %get-tuple-element.81.o_ref, f32[256,768]{1,0:T(8,128)} %get-tuple-element.82.x_ref, ...), custom_call_target="tpu_custom_call" | custom-call | flops 2717908992 | bytes 10616832 | tf_op jit(solution)/shard_map/mlp/pallas_call | solution.py:185
  460.2 11.8 %mlp_back.2 = (bf16[256,768]{1,0:T(8,128)(2,1)}, bf16[256,3072]{1,0:T(8,128)(2,1)}, f32[1,3072]{1,0:T(1,128)}, f32[256,768]{1,0:T(8,128)}, bf16[256,768]{1,0:T(8...) custom-call(f32[256,768]{1,0:T(8,128)} %fusion.19.g_ref, bf16[384,6144]{1,0:T(8,128)(2,1)} %bitcast.74.up_own_ref.down_own_ref, ...), custom_call_target="tpu_custom_call" | custom-call | flops 2717908992 | bytes 10616832 | tf_op jit(solution)/shard_map/mlp_back/pallas_call | solution.py:259
  472.1 22.4 %attend_back.2 = (bf16[256,768]{1,0:T(8,128)(2,1)}, bf16[1024,1536]{1,0:T(8,128)(2,1)}, f32[256,768]{1,0:T(8,128)}, bf16[384,768]{1,0:T(8,128)(2,1)}, bf16[384,768]{1,0:T(8,128)(2,1)}, /*index=5*/f32[8,768]{1,0:T(8,128)}) custom-call(bf16[256,768]{1,0:T(8,128)(2,1)} %get-tuple-element.87.go_ref, bf16[256,768]{1,0:T(8,128)(2,1)} %get-tuple-element.88.qn_ref, ...), custom_call_target="tpu_custom_call" | custom-call | flops 10468982784 | bytes 15728640 | tf_op jit(solution)/shard_map/attend_back/pallas_call | solution.py:345
  505.1 4.0 collective-permute-start.39
  510.8 11.6 %mlp_weight_grads.3 = (bf16[384,6144]{1,0:T(8,128)(2,1)}, bf16[384,6144]{1,0:T(8,128)(2,1)}) custom-call(bf16[256,768]{1,0:T(8,128)(2,1)} %get-tuple-element.136.m_ref, bf16[256,3072]{1,0:T(8,128)(2,1)} %get-tuple-element.137.gh_ref, bf16[256,768]{1,0:T(8,128)(2,1)} %get-tuple-element.138.gz_ref, bf16[256,3072]{1,0:T(8,128)(2,1)} %get-tuple-element.139.act_ref), custom_call_target="tpu_custom_call" | custom-call | flops 2415919104 | bytes 9437184 | tf_op jit(solution)/shard_map/mlp_weight_grads/pallas_call | solution.py:452
  529.2 11.8 %mlp_back.3 = (bf16[256,768]{1,0:T(8,128)(2,1)}, bf16[256,3072]{1,0:T(8,128)(2,1)}, f32[1,3072]{1,0:T(1,128)}, f32[256,768]{1,0:T(8,128)}, bf16[256,768]{1,0:T(8...) custom-call(f32[256,768]{1,0:T(8,128)} %multiply_add_fusion.1.g_ref, ...), custom_call_target="tpu_custom_call" | custom-call | flops 2717908992 | bytes 10616832 | tf_op jit(solution)/shard_map/mlp_back/pallas_call | solution.py:259
  541.1 22.4 %attend_back.3 = (bf16[256,768]{1,0:T(8,128)(2,1)}, bf16[1024,1536]{1,0:T(8,128)(2,1)}, f32[256,768]{1,0:T(8,128)}, bf16[384,768]{1,0:T(8,128)(2,1)}, bf16[384,768]{1,0:T(8,128)(2,1)}, /*index=5*/f32[8,768]{1,0:T(8,128)}) custom-call(bf16[256,768]{1,0:T(8,128)(2,1)} %get-tuple-element.102.go_ref, bf16[256,768]{1,0:T(8,128)(2,1)} %get-tuple-element.103.qn_ref, ...), custom_call_target="tpu_custom_call" | custom-call | flops 10468982784 | bytes 15728640 | tf_op jit(solution)/shard_map/attend_back/pallas_call | solution.py:345
  572.3 8.0 collective-permute-start.43
  586.6 9.6 %collective-permute-done.44 = bf16[128,768]{1,0:T(8,128)(2,1)} collective-permute-done((bf16[128,768]{1,0:T(8,128)(2,1)}, bf16[128,768]{1,0:T(8,128)(2,1)}, u32[]{:S(2)}, u32[]{:S(2)}) %collective-permute-start.44) | collective-permute-done | bytes 196640 | tf_op jit(solution)/shard_map/ppermute | solution.py:483
  608.3 10.5 %attn_weight_grads.3 = (bf16[384,3072]{1,0:T(8,128)(2,1)}, bf16[384,3072]{1,0:T(8,128)(2,1)}) custom-call(bf16[1024,768]{1,0:T(8,128)(2,1)} %copy-done.46, bf16[256,768]{1,0:T(8,128)(2,1)} %get-tuple-element.125.gq_ref, bf16[1024,1536]{1,0:T(8,128)(2,1)} %get-tuple-element.126.gkv_ref, bf16[256,768]{1,0:T(8,128)(2,1)} %get-tuple-element.127.gr_ref, ...), custom_call_target="tpu_custom_call" | custom-call | flops 3019898880 | bytes 4718592 | tf_op jit(solution)/shard_map/attn_weight_grads/pallas_call | solution.py:404
  624.8 11.6 %mlp_weight_grads.2 = (bf16[384,6144]{1,0:T(8,128)(2,1)}, bf16[384,6144]{1,0:T(8,128)(2,1)}) custom-call(bf16[256,768]{1,0:T(8,128)(2,1)} %get-tuple-element.130.m_ref, bf16[256,3072]{1,0:T(8,128)(2,1)} %get-tuple-element.131.gh_ref, bf16[256,768]{1,0:T(8,128)(2,1)} %get-tuple-element.132.gz_ref, bf16[256,3072]{1,0:T(8,128)(2,1)} %get-tuple-element.133.act_ref), custom_call_target="tpu_custom_call" | custom-call | flops 2415919104 | bytes 9437184 | tf_op jit(solution)/shard_map/mlp_weight_grads/pallas_call | solution.py:452
  637.0 10.5 %attn_weight_grads.2 = (bf16[384,3072]{1,0:T(8,128)(2,1)}, bf16[384,3072]{1,0:T(8,128)(2,1)}) custom-call(bf16[1024,768]{1,0:T(8,128)(2,1)} %copy-done.47, bf16[256,768]{1,0:T(8,128)(2,1)} %get-tuple-element.120.gq_ref, bf16[1024,1536]{1,0:T(8,128)(2,1)} %get-tuple-element.121.gkv_ref, bf16[256,768]{1,0:T(8,128)(2,1)} %get-tuple-element.122.gr_ref, ...), custom_call_target="tpu_custom_call" | custom-call | flops 3019898880 | bytes 4718592 | tf_op jit(solution)/shard_map/attn_weight_grads/pallas_call | solution.py:404
  662.0 20.8 %collective-permute-done.57 = bf16[2,96,3072]{2,1,0:T(8,128)(2,1)} collective-permute-done((bf16[2,96,3072]{2,1,0:T(8,128)(2,1)}, bf16[2,96,3072]{2,1,0:T(8,128)(2,1)}, u32[]{:S(2)}, u32[]{:S(2)}) %collective-permute-start.57) | collective-permute-done | bytes 1179680 | tf_op jit(solution)/shard_map/ppermute | solution.py:473
  692.6 7.8 collective-permute-done.58
  707.4 4.1 collective-permute-done.59
  726.4 3.0 collective-permute-done.61
  731.7 5.6 add_convert_fusion
  742.8 4.1 collective-permute-done.55
  750.3 5.7 add_convert_fusion.1
  757.2 34.7 %collective-permute-done.69 = bf16[2,96,6144]{2,1,0:T(8,128)(2,1)S(1)} collective-permute-done((bf16[2,96,6144]{2,1,0:T(8,128)(2,1)}, bf16[2,96,6144]{2,1,0:T(8,128)(2,1)S(1)}, u32[]{:S(2)}, u32[]{:S(2)}) %collective-permute-start.69) | collective-permute-done | bytes 2359328 | tf_op jit(solution)/shard_map/ppermute | solution.py:473
  793.4 17.5 %collective-permute-done.63 = bf16[2,96,6144]{2,1,0:T(8,128)(2,1)S(1)} collective-permute-done((bf16[2,96,6144]{2,1,0:T(8,128)(2,1)S(1)}, bf16[2,96,6144]{2,1,0:T(8,128)(2,1)S(1)}, u32[]{:S(2)}, u32[]{:S(2)}) %collective-permute-start.63) | collective-permute-done | bytes 2359328 | tf_op jit(solution)/shard_map/ppermute | solution.py:473
  813.3 16.7 %collective-permute-done.70 = bf16[96,6144]{1,0:T(8,128)(2,1)S(1)} collective-permute-done((bf16[96,6144]{1,0:T(8,128)(2,1)S(1)}, bf16[96,6144]{1,0:T(8,128)(2,1)S(1)}, u32[]{:S(2)}, u32[]{:S(2)}) %collective-permute-start.70) | collective-permute-done | bytes 1179680 | tf_op jit(solution)/shard_map/ppermute | solution.py:473
  831.3 10.4 %collective-permute-done.71 = bf16[96,1536]{1,0:T(8,128)(2,1)S(1)} collective-permute-done((bf16[96,1536]{1,0:T(8,128)(2,1)S(1)}, bf16[96,1536]{1,0:T(8,128)(2,1)S(1)}, u32[]{:S(2)}, u32[]{:S(2)}) %collective-permute-start.71) | collective-permute-done | bytes 294944 | tf_op jit(solution)/shard_map/ppermute | solution.py:478
  841.8 6.2 collective-permute-done.65
  848.2 6.2 collective-permute-done.72
  854.5 6.2 collective-permute-done.66
  860.8 3.5 collective-permute-done.73
  864.4 4.9 collective-permute-done.67
  (587 shorter events, 274.5 us)
Async XLA Ops:
  8.0 16.3 %collective-permute-start = (bf16[1,3840]{1,0:T(2,128)(2,1)S(1)}, bf16[1,3840]{1,0:T(2,128)(2,1)S(1)}, u32[]{:S(2)}, u32[]{:S(2)}) collective-permute-start(bf16[1,3840]{1,0:T(2,128)(2,1)S(1)} %reshape.515), channel_id=1, source_target_pairs={{0,1},{1,0},{2,3},{3,2},{4,5},{5,4},{6,7},{7,6},{8,9},{9,8},{10,11... | collective-permute-start | bytes 23048 | tf_op jit(solution)/shard_map/ppermute | solution.py:473
  13.9 34.0 %collective-permute-start.9 = (bf16[96,768]{0,1:T(8,128)(2,1)}, bf16[96,768]{0,1:T(8,128)(2,1)}, u32[]{:S(2)}, u32[]{:S(2)}) collective-permute-start(bf16[96,768]{0,1:T(8,128)(2,1)} %pad_maximum_fusion.19), channel_id=1, source_target_pairs={{0,1},{1,2},{2,3},{3,0},{4,5},{5,6},{6,7},{7,4},{8,9},{9,10},{10,1... | collective-permute-start | bytes 442376 | tf_op jit(solution)/shard_map/ppermute | solution.py:478
  14.8 43.2 %collective-permute-start.31 = (bf16[96,1536]{1,0:T(8,128)(2,1)}, bf16[96,1536]{1,0:T(8,128)(2,1)}, u32[]{:S(2)}, u32[]{:S(2)}) collective-permute-start(bf16[96,1536]{1,0:T(8,128)(2,1)} %pad_maximum_fusion.15), channel_id=1, source_target_pairs={{0,1},{1,2},{2,3},{3,0},{4,5},{5,6},{6,7},{7,4},{8,9},{9,10},{10,1... | collective-permute-start | bytes 884744 | tf_op jit(solution)/shard_map/ppermute | solution.py:478
  17.9 44.2 %collective-permute-start.15 = (bf16[96,1536]{1,0:T(8,128)(2,1)S(1)}, bf16[96,1536]{1,0:T(8,128)(2,1)}, u32[]{:S(2)}, u32[]{:S(2)}) collective-permute-start(bf16[96,1536]{1,0:T(8,128)(2,1)S(1)} %pad_maximum_fusion.14), channel_id=1, source_target_pairs={{0,1},{1,2},{2,3},{3,0},{4,5},{5,6},{6,7},{7,4},{8,9},{9,10},{10,1... | collective-permute-start | bytes 884744 | tf_op jit(solution)/shard_map/ppermute | solution.py:478
  19.3 30.1 %collective-permute-start.25 = (bf16[96,768]{0,1:T(8,128)(2,1)}, bf16[96,768]{0,1:T(8,128)(2,1)}, u32[]{:S(2)}, u32[]{:S(2)}) collective-permute-start(bf16[96,768]{0,1:T(8,128)(2,1)} %pad_maximum_fusion.20), channel_id=1, source_target_pairs={{0,1},{1,2},{2,3},{3,0},{4,5},{5,6},{6,7},{7,4},{8,9},{9,10},{10,1... | collective-permute-start | bytes 442376 | tf_op jit(solution)/shard_map/ppermute | solution.py:478
  24.4 15.4 %collective-permute-start.1 = (bf16[2,3840]{1,0:T(2,128)(2,1)S(1)}, bf16[2,3840]{1,0:T(2,128)(2,1)S(1)}, u32[]{:S(2)}, u32[]{:S(2)}) collective-permute-start(bf16[2,3840]{1,0:T(2,128)(2,1)S(1)} %pad_maximum_fusion.26), channel_id=1, source_target_pairs={{0,2},{1,3},{2,0},{3,1},{4,6},{5,7},{6,4},{7,5},{8,10},{9,11},{10,... | collective-permute-start | bytes 46088 | tf_op jit(solution)/shard_map/ppermute | solution.py:473
  50.9 43.1 %collective-permute-start.10 = (bf16[96,768]{0,1:T(8,128)(2,1)}, bf16[96,768]{0,1:T(8,128)(2,1)}, u32[]{:S(2)}, u32[]{:S(2)}) collective-permute-start(bf16[96,768]{0,1:T(8,128)(2,1)} %collective-permute-done.9), channel_id=1, source_target_pairs={{0,1},{1,2},{2,3},{3,0},{4,5},{5,6},{6,7},{7,4},{8,9},{9,10},{10,1... | collective-permute-start | bytes 442376 | tf_op jit(solution)/shard_map/ppermute | solution.py:478
  52.9 97.4 %collective-permute-start.26 = (bf16[96,768]{0,1:T(8,128)(2,1)}, bf16[96,768]{0,1:T(8,128)(2,1)}, u32[]{:S(2)}, u32[]{:S(2)}) collective-permute-start(bf16[96,768]{0,1:T(8,128)(2,1)} %collective-permute-done.25), channel_id=1, source_target_pairs={{0,1},{1,2},{2,3},{3,0},{4,5},{5,6},{6,7},{7,4},{8,9},{9,10},{10,1... | collective-permute-start | bytes 442376 | tf_op jit(solution)/shard_map/ppermute | solution.py:478
  62.1 14.7 %collective-permute-start.16 = (bf16[96,1536]{1,0:T(8,128)(2,1)}, bf16[96,1536]{1,0:T(8,128)(2,1)S(1)}, u32[]{:S(2)}, u32[]{:S(2)}) collective-permute-start(bf16[96,1536]{1,0:T(8,128)(2,1)} %collective-permute-done.15), channel_id=1, source_target_pairs={{0,1},{1,2},{2,3},{3,0},{4,5},{5,6},{6,7},{7,4},{8,9},{9,10},{10,1... | collective-permute-start | bytes 884744 | tf_op jit(solution)/shard_map/ppermute | solution.py:478
  90.4 26.6 %collective-permute-start.18 = (bf16[96,6144]{1,0:T(8,128)(2,1)S(1)}, bf16[96,6144]{1,0:T(8,128)(2,1)S(1)}, u32[]{:S(2)}, u32[]{:S(2)}) collective-permute-start(bf16[96,6144]{1,0:T(8,128)(2,1)S(1)} %slice_dynamic-update-slice_fusion.6), channel_id=1, source_target_pairs={{0,8},{4,12},{8,0},{12,4},{16,24},{20,28},{24,16},{28,20},{1,9},{5... | collective-permute-start | bytes 3538952 | tf_op jit(solution)/shard_map/ppermute | solution.py:473
  94.0 36.4 %collective-permute-start.11 = (bf16[96,768]{0,1:T(8,128)(2,1)}, bf16[96,768]{0,1:T(8,128)(2,1)}, u32[]{:S(2)}, u32[]{:S(2)}) collective-permute-start(bf16[96,768]{0,1:T(8,128)(2,1)} %collective-permute-done.10), channel_id=1, source_target_pairs={{0,1},{1,2},{2,3},{3,0},{4,5},{5,6},{6,7},{7,4},{8,9},{9,10},{10,1... | collective-permute-start | bytes 442376 | tf_op jit(solution)/shard_map/ppermute | solution.py:478
  119.9 98.1 %collective-permute-start.19 = (bf16[2,96,6144]{2,1,0:T(8,128)(2,1)}, bf16[2,96,6144]{2,1,0:T(8,128)(2,1)}, u32[]{:S(2)}, u32[]{:S(2)}) collective-permute-start(bf16[2,96,6144]{2,1,0:T(8,128)(2,1)} %get-tuple-element.283), channel_id=1, source_target_pairs={{0,16},{4,20},{8,24},{12,28},{16,0},{20,4},{24,8},{28,12},{1,17},{... | collective-permute-start | bytes 7077896 | tf_op jit(solution)/shard_map/ppermute | solution.py:473
  121.1 92.2 %collective-permute-start.34 = (bf16[96,6144]{1,0:T(8,128)(2,1)}, bf16[96,6144]{1,0:T(8,128)(2,1)}, u32[]{:S(2)}, u32[]{:S(2)}) collective-permute-start(bf16[96,6144]{1,0:T(8,128)(2,1)} %slice_dynamic-update-slice_fusion), channel_id=1, source_target_pairs={{0,16},{4,20},{8,24},{12,28},{16,0},{20,4},{24,8},{28,12},{1,17},{... | collective-permute-start | bytes 3538952 | tf_op jit(solution)/shard_map/ppermute | solution.py:473
  124.5 203.0 %collective-permute-start.6 = (bf16[256,768]{1,0:T(8,128)(2,1)S(1)}, bf16[256,768]{1,0:T(8,128)(2,1)}, u32[]{:S(2)}, u32[]{:S(2)}) collective-permute-start(bf16[256,768]{1,0:T(8,128)(2,1)S(1)} %add_convert_fusion.4), channel_id=1, source_target_pairs={{0,1},{1,2},{2,3},{4,5},{5,6},{6,7},{8,9},{9,10},{10,11},{12,13},{... | collective-permute-start | bytes 1179656 | tf_op jit(solution)/shard_map/ppermute | solution.py:483
  142.3 66.7 %collective-permute-start.12 = (bf16[96,3072]{1,0:T(8,128)(2,1)}, bf16[96,3072]{1,0:T(8,128)(2,1)}, u32[]{:S(2)}, u32[]{:S(2)}) collective-permute-start(bf16[96,3072]{1,0:T(8,128)(2,1)} %concatenate.153), channel_id=1, source_target_pairs={{0,16},{4,20},{8,24},{12,28},{16,0},{20,4},{24,8},{28,12},{1,17},{... | collective-permute-start | bytes 1769480 | tf_op jit(solution)/shard_map/ppermute | solution.py:473
  211.9 91.6 %collective-permute-start.13 = (bf16[2,96,3072]{2,1,0:T(8,128)(2,1)}, bf16[2,96,3072]{2,1,0:T(8,128)(2,1)}, u32[]{:S(2)}, u32[]{:S(2)}) collective-permute-start(bf16[2,96,3072]{2,1,0:T(8,128)(2,1)} %get-tuple-element.303), channel_id=1, source_target_pairs={{0,8},{4,12},{8,0},{12,4},{16,24},{20,28},{24,16},{28,20},{1,9},{5... | collective-permute-start | bytes 3538952 | tf_op jit(solution)/shard_map/ppermute | solution.py:473
  217.5 88.1 %collective-permute-start.35 = (bf16[2,96,6144]{2,1,0:T(8,128)(2,1)}, bf16[2,96,6144]{2,1,0:T(8,128)(2,1)}, u32[]{:S(2)}, u32[]{:S(2)}) collective-permute-start(bf16[2,96,6144]{2,1,0:T(8,128)(2,1)} %get-tuple-element.281), channel_id=1, source_target_pairs={{0,8},{4,12},{8,0},{12,4},{16,24},{20,28},{24,16},{28,20},{1,9},{5... | collective-permute-start | bytes 7077896 | tf_op jit(solution)/shard_map/ppermute | solution.py:473
  222.3 159.4 %collective-permute-start.20 = (bf16[384,6144]{1,0:T(8,128)(2,1)}, bf16[384,6144]{1,0:T(8,128)(2,1)}, u32[]{:S(2)}, u32[]{:S(2)}) collective-permute-start(bf16[384,6144]{1,0:T(8,128)(2,1)} %bitcast.40.up_own_ref.down_own_ref), channel_id=1, source_target_pairs={{0,4},{4,0},{8,12},{12,8},{16,20},{20,16},{24,28},{28,24},{1,5},{5... | collective-permute-start | bytes 14155784 | tf_op jit(solution)/shard_map/ppermute | solution.py:473
  224.7 75.2 %collective-permute-start.28 = (bf16[96,3072]{1,0:T(8,128)(2,1)S(1)}, bf16[96,3072]{1,0:T(8,128)(2,1)S(1)}, u32[]{:S(2)}, u32[]{:S(2)}) collective-permute-start(bf16[96,3072]{1,0:T(8,128)(2,1)S(1)} %concatenate.159), channel_id=1, source_target_pairs={{0,8},{4,12},{8,0},{12,4},{16,24},{20,28},{24,16},{28,20},{1,9},{5... | collective-permute-start | bytes 1769480 | tf_op jit(solution)/shard_map/ppermute | solution.py:473
  303.4 51.4 %collective-permute-start.29 = (bf16[2,96,3072]{2,1,0:T(8,128)(2,1)}, bf16[2,96,3072]{2,1,0:T(8,128)(2,1)}, u32[]{:S(2)}, u32[]{:S(2)}) collective-permute-start(bf16[2,96,3072]{2,1,0:T(8,128)(2,1)} %get-tuple-element.301), channel_id=1, source_target_pairs={{0,16},{4,20},{8,24},{12,28},{16,0},{20,4},{24,8},{28,12},{1,17},{... | collective-permute-start | bytes 3538952 | tf_op jit(solution)/shard_map/ppermute | solution.py:473
  305.6 52.2 %collective-permute-start.14 = (bf16[384,3072]{1,0:T(8,128)(2,1)S(1)}, bf16[384,3072]{1,0:T(8,128)(2,1)}, u32[]{:S(2)}, u32[]{:S(2)}) collective-permute-start(bf16[384,3072]{1,0:T(8,128)(2,1)S(1)} %bitcast.232), channel_id=1, source_target_pairs={{0,4},{4,0},{8,12},{12,8},{16,20},{20,16},{24,28},{28,24},{1,5},{5... | collective-permute-start | bytes 7077896 | tf_op jit(solution)/shard_map/ppermute | solution.py:473
  312.5 135.4 %collective-permute-start.36 = (bf16[384,6144]{1,0:T(8,128)(2,1)}, bf16[384,6144]{1,0:T(8,128)(2,1)}, u32[]{:S(2)}, u32[]{:S(2)}) collective-permute-start(bf16[384,6144]{1,0:T(8,128)(2,1)} %bitcast.74.up_own_ref.down_own_ref), channel_id=1, source_target_pairs={{0,4},{4,0},{8,12},{12,8},{16,20},{20,16},{24,28},{28,24},{1,5},{5... | collective-permute-start | bytes 14155784 | tf_op jit(solution)/shard_map/ppermute | solution.py:473
  327.5 13.4 %collective-permute-start.7 = (bf16[256,768]{1,0:T(8,128)(2,1)S(1)}, bf16[256,768]{1,0:T(8,128)(2,1)S(1)}, u32[]{:S(2)}, u32[]{:S(2)}) collective-permute-start(bf16[256,768]{1,0:T(8,128)(2,1)S(1)} %add_convert_fusion.4), channel_id=1, source_target_pairs={{1,0},{2,1},{3,2},{5,4},{6,5},{7,6},{9,8},{10,9},{11,10},{13,12},{... | collective-permute-start | bytes 1179656 | tf_op jit(solution)/shard_map/ppermute | solution.py:483
  340.9 12.7 %collective-permute-start.8 = (bf16[128,768]{1,0:T(8,128)(2,1)}, bf16[128,768]{1,0:T(8,128)(2,1)S(1)}, u32[]{:S(2)}, u32[]{:S(2)}) collective-permute-start(bf16[128,768]{1,0:T(8,128)(2,1)} %get-tuple-element.332), channel_id=1, source_target_pairs={{2,0},{3,1},{6,4},{7,5},{10,8},{11,9},{14,12},{15,13},{18,16},{19,... | collective-permute-start | bytes 589832 | tf_op jit(solution)/shard_map/ppermute | solution.py:483
  357.8 66.3 %collective-permute-start.30 = (bf16[384,3072]{1,0:T(8,128)(2,1)}, bf16[384,3072]{1,0:T(8,128)(2,1)}, u32[]{:S(2)}, u32[]{:S(2)}) collective-permute-start(bf16[384,3072]{1,0:T(8,128)(2,1)} %bitcast.62.own_ref.mix_own_ref), channel_id=1, source_target_pairs={{0,4},{4,0},{8,12},{12,8},{16,20},{20,16},{24,28},{28,24},{1,5},{5... | collective-permute-start | bytes 7077896 | tf_op jit(solution)/shard_map/ppermute | solution.py:473
  393.9 16.7 %collective-permute-start.22 = (bf16[256,768]{1,0:T(8,128)(2,1)}, bf16[256,768]{1,0:T(8,128)(2,1)S(1)}, u32[]{:S(2)}, u32[]{:S(2)}) collective-permute-start(bf16[256,768]{1,0:T(8,128)(2,1)} %get-tuple-element.80), channel_id=1, source_target_pairs={{0,1},{1,2},{2,3},{4,5},{5,6},{6,7},{8,9},{9,10},{10,11},{12,13},{... | collective-permute-start | bytes 1179656 | tf_op jit(solution)/shard_map/ppermute | solution.py:483
  395.3 15.4 %collective-permute-start.23 = (bf16[256,768]{1,0:T(8,128)(2,1)}, bf16[256,768]{1,0:T(8,128)(2,1)S(1)}, u32[]{:S(2)}, u32[]{:S(2)}) collective-permute-start(bf16[256,768]{1,0:T(8,128)(2,1)} %get-tuple-element.80), channel_id=1, source_target_pairs={{1,0},{2,1},{3,2},{5,4},{6,5},{7,6},{9,8},{10,9},{11,10},{13,12},{... | collective-permute-start | bytes 1179656 | tf_op jit(solution)/shard_map/ppermute | solution.py:483
  409.1 13.8 %collective-permute-start.24 = (bf16[128,768]{1,0:T(8,128)(2,1)S(1)}, bf16[128,768]{1,0:T(8,128)(2,1)S(1)}, u32[]{:S(2)}, u32[]{:S(2)}) collective-permute-start(bf16[128,768]{1,0:T(8,128)(2,1)S(1)} %get-tuple-element.330), channel_id=1, source_target_pairs={{2,0},{3,1},{6,4},{7,5},{10,8},{11,9},{14,12},{15,13},{18,16},{19,... | collective-permute-start | bytes 589832 | tf_op jit(solution)/shard_map/ppermute | solution.py:483
  501.5 25.1 %collective-permute-start.37 = (bf16[256,768]{1,0:T(8,128)(2,1)S(1)}, bf16[256,768]{1,0:T(8,128)(2,1)S(1)}, u32[]{:S(2)}, u32[]{:S(2)}) collective-permute-start(bf16[256,768]{1,0:T(8,128)(2,1)S(1)} %slice.568), channel_id=1, source_target_pairs={{0,1},{1,2},{2,3},{4,5},{5,6},{6,7},{8,9},{9,10},{10,11},{12,13},{... | collective-permute-start | bytes 1179656 | tf_op jit(solution)/shard_map/ppermute | solution.py:483
  503.8 22.8 %collective-permute-start.38 = (bf16[256,768]{1,0:T(8,128)(2,1)S(1)}, bf16[256,768]{1,0:T(8,128)(2,1)S(1)}, u32[]{:S(2)}, u32[]{:S(2)}) collective-permute-start(bf16[256,768]{1,0:T(8,128)(2,1)S(1)} %slice.569), channel_id=1, source_target_pairs={{1,0},{2,1},{3,2},{5,4},{6,5},{7,6},{9,8},{10,9},{11,10},{13,12},{... | collective-permute-start | bytes 1179656 | tf_op jit(solution)/shard_map/ppermute | solution.py:483
  505.1 21.4 %collective-permute-start.39 = (bf16[128,768]{1,0:T(8,128)(2,1)}, bf16[128,768]{1,0:T(8,128)(2,1)S(1)}, u32[]{:S(2)}, u32[]{:S(2)}) collective-permute-start(bf16[128,768]{1,0:T(8,128)(2,1)} %slice.570), channel_id=1, source_target_pairs={{0,2},{1,3},{4,6},{5,7},{8,10},{9,11},{12,14},{13,15},{16,18},{17,... | collective-permute-start | bytes 589832 | tf_op jit(solution)/shard_map/ppermute | solution.py:483
  509.1 17.4 %collective-permute-start.40 = (bf16[128,768]{1,0:T(8,128)(2,1)}, bf16[128,768]{1,0:T(8,128)(2,1)S(1)}, u32[]{:S(2)}, u32[]{:S(2)}) collective-permute-start(bf16[128,768]{1,0:T(8,128)(2,1)} %slice.571), channel_id=1, source_target_pairs={{2,0},{3,1},{6,4},{7,5},{10,8},{11,9},{14,12},{15,13},{18,16},{19,... | collective-permute-start | bytes 589832 | tf_op jit(solution)/shard_map/ppermute | solution.py:483
  522.4 209.3 %collective-permute-start.68 = (bf16[384,6144]{1,0:T(8,128)(2,1)}, bf16[384,6144]{1,0:T(8,128)(2,1)}, u32[]{:S(2)}, u32[]{:S(2)}) collective-permute-start(bf16[384,6144]{1,0:T(8,128)(2,1)} %get-tuple-element.141), channel_id=1, source_target_pairs={{0,4},{4,0},{8,12},{12,8},{16,20},{20,16},{24,28},{28,24},{1,5},{5... | collective-permute-start | bytes 14155784 | tf_op jit(solution)/shard_map/ppermute | solution.py:473
  569.0 27.1 %collective-permute-start.41 = (bf16[256,768]{1,0:T(8,128)(2,1)S(1)}, bf16[256,768]{1,0:T(8,128)(2,1)S(1)}, u32[]{:S(2)}, u32[]{:S(2)}) collective-permute-start(bf16[256,768]{1,0:T(8,128)(2,1)S(1)} %slice.572), channel_id=1, source_target_pairs={{0,1},{1,2},{2,3},{4,5},{5,6},{6,7},{8,9},{9,10},{10,11},{12,13},{... | collective-permute-start | bytes 1179656 | tf_op jit(solution)/shard_map/ppermute | solution.py:483
  571.0 25.1 %collective-permute-start.42 = (bf16[256,768]{1,0:T(8,128)(2,1)S(1)}, bf16[256,768]{1,0:T(8,128)(2,1)S(1)}, u32[]{:S(2)}, u32[]{:S(2)}) collective-permute-start(bf16[256,768]{1,0:T(8,128)(2,1)S(1)} %slice.573), channel_id=1, source_target_pairs={{1,0},{2,1},{3,2},{5,4},{6,5},{7,6},{9,8},{10,9},{11,10},{13,12},{... | collective-permute-start | bytes 1179656 | tf_op jit(solution)/shard_map/ppermute | solution.py:483
  572.3 14.3 %collective-permute-start.43 = (bf16[128,768]{1,0:T(8,128)(2,1)}, bf16[128,768]{1,0:T(8,128)(2,1)S(1)}, u32[]{:S(2)}, u32[]{:S(2)}) collective-permute-start(bf16[128,768]{1,0:T(8,128)(2,1)} %slice.574), channel_id=1, source_target_pairs={{0,2},{1,3},{4,6},{5,7},{8,10},{9,11},{12,14},{13,15},{16,18},{17,... | collective-permute-start | bytes 589832 | tf_op jit(solution)/shard_map/ppermute | solution.py:483
  580.4 15.8 %collective-permute-start.44 = (bf16[128,768]{1,0:T(8,128)(2,1)}, bf16[128,768]{1,0:T(8,128)(2,1)}, u32[]{:S(2)}, u32[]{:S(2)}) collective-permute-start(bf16[128,768]{1,0:T(8,128)(2,1)} %slice.575), channel_id=1, source_target_pairs={{2,0},{3,1},{6,4},{7,5},{10,8},{11,9},{14,12},{15,13},{18,16},{19,... | collective-permute-start | bytes 589832 | tf_op jit(solution)/shard_map/ppermute | solution.py:483
  618.8 32.8 %collective-permute-start.56 = (bf16[384,3072]{1,0:T(8,128)(2,1)}, bf16[384,3072]{1,0:T(8,128)(2,1)}, u32[]{:S(2)}, u32[]{:S(2)}) collective-permute-start(bf16[384,3072]{1,0:T(8,128)(2,1)} %get-tuple-element.129), channel_id=1, source_target_pairs={{0,4},{4,0},{8,12},{12,8},{16,20},{20,16},{24,28},{28,24},{1,5},{5... | collective-permute-start | bytes 7077896 | tf_op jit(solution)/shard_map/ppermute | solution.py:473
  636.4 114.0 %collective-permute-start.62 = (bf16[384,6144]{1,0:T(8,128)(2,1)}, bf16[384,6144]{1,0:T(8,128)(2,1)}, u32[]{:S(2)}, u32[]{:S(2)}) collective-permute-start(bf16[384,6144]{1,0:T(8,128)(2,1)} %get-tuple-element.135), channel_id=1, source_target_pairs={{0,4},{4,0},{8,12},{12,8},{16,20},{20,16},{24,28},{28,24},{1,5},{5... | collective-permute-start | bytes 14155784 | tf_op jit(solution)/shard_map/ppermute | solution.py:473
  655.3 27.5 %collective-permute-start.57 = (bf16[2,96,3072]{2,1,0:T(8,128)(2,1)}, bf16[2,96,3072]{2,1,0:T(8,128)(2,1)}, u32[]{:S(2)}, u32[]{:S(2)}) collective-permute-start(bf16[2,96,3072]{2,1,0:T(8,128)(2,1)} %bitcast.94), channel_id=1, source_target_pairs={{0,16},{4,20},{8,24},{12,28},{16,0},{20,4},{24,8},{28,12},{1,17},{... | collective-permute-start | bytes 3538952 | tf_op jit(solution)/shard_map/ppermute | solution.py:473
  658.7 29.2 %collective-permute-start.51 = (bf16[2,96,3072]{2,1,0:T(8,128)(2,1)}, bf16[2,96,3072]{2,1,0:T(8,128)(2,1)}, u32[]{:S(2)}, u32[]{:S(2)}) collective-permute-start(bf16[2,96,3072]{2,1,0:T(8,128)(2,1)} %get-tuple-element.277), channel_id=1, source_target_pairs={{0,8},{4,12},{8,0},{12,4},{16,24},{20,28},{24,16},{28,20},{1,9},{5... | collective-permute-start | bytes 3538952 | tf_op jit(solution)/shard_map/ppermute | solution.py:473
  686.4 13.9 %collective-permute-start.58 = (bf16[96,3072]{1,0:T(8,128)(2,1)}, bf16[96,3072]{1,0:T(8,128)(2,1)}, u32[]{:S(2)}, u32[]{:S(2)}) collective-permute-start(bf16[96,3072]{1,0:T(8,128)(2,1)} %slice_bitcast_fusion.9), channel_id=1, source_target_pairs={{0,8},{4,12},{8,0},{12,4},{16,24},{20,28},{24,16},{28,20},{1,9},{5... | collective-permute-start | bytes 1769480 | tf_op jit(solution)/shard_map/ppermute | solution.py:473
  706.6 15.0 %collective-permute-start.52 = (bf16[96,3072]{1,0:T(8,128)(2,1)}, bf16[96,3072]{1,0:T(8,128)(2,1)S(1)}, u32[]{:S(2)}, u32[]{:S(2)}) collective-permute-start(bf16[96,3072]{1,0:T(8,128)(2,1)} %copy.509), channel_id=1, source_target_pairs={{0,16},{4,20},{8,24},{12,28},{16,0},{20,4},{24,8},{28,12},{1,17},{... | collective-permute-start | bytes 1769480 | tf_op jit(solution)/shard_map/ppermute | solution.py:473
  741.3 50.6 %collective-permute-start.69 = (bf16[2,96,6144]{2,1,0:T(8,128)(2,1)}, bf16[2,96,6144]{2,1,0:T(8,128)(2,1)S(1)}, u32[]{:S(2)}, u32[]{:S(2)}) collective-permute-start(bf16[2,96,6144]{2,1,0:T(8,128)(2,1)} %slice_bitcast_fusion), channel_id=1, source_target_pairs={{0,8},{4,12},{8,0},{12,4},{16,24},{20,28},{24,16},{28,20},{1,9},{5... | collective-permute-start | bytes 7077896 | tf_op jit(solution)/shard_map/ppermute | solution.py:473
  756.6 54.3 %collective-permute-start.63 = (bf16[2,96,6144]{2,1,0:T(8,128)(2,1)S(1)}, bf16[2,96,6144]{2,1,0:T(8,128)(2,1)S(1)}, u32[]{:S(2)}, u32[]{:S(2)}) collective-permute-start(bf16[2,96,6144]{2,1,0:T(8,128)(2,1)S(1)} %bitcast.252), channel_id=1, source_target_pairs={{0,16},{4,20},{8,24},{12,28},{16,0},{20,4},{24,8},{28,12},{1,17},{... | collective-permute-start | bytes 7077896 | tf_op jit(solution)/shard_map/ppermute | solution.py:473
  792.8 37.2 %collective-permute-start.70 = (bf16[96,6144]{1,0:T(8,128)(2,1)S(1)}, bf16[96,6144]{1,0:T(8,128)(2,1)S(1)}, u32[]{:S(2)}, u32[]{:S(2)}) collective-permute-start(bf16[96,6144]{1,0:T(8,128)(2,1)S(1)} %slice_bitcast_fusion.2), channel_id=1, source_target_pairs={{0,16},{4,20},{8,24},{12,28},{16,0},{20,4},{24,8},{28,12},{1,17},{... | collective-permute-start | bytes 3538952 | tf_op jit(solution)/shard_map/ppermute | solution.py:473
  811.7 18.7 %collective-permute-start.64 = (bf16[96,6144]{1,0:T(8,128)(2,1)S(1)}, bf16[96,6144]{1,0:T(8,128)(2,1)S(1)}, u32[]{:S(2)}, u32[]{:S(2)}) collective-permute-start(bf16[96,6144]{1,0:T(8,128)(2,1)S(1)} %slice_bitcast_fusion.4), channel_id=1, source_target_pairs={{0,8},{4,12},{8,0},{12,4},{16,24},{20,28},{24,16},{28,20},{1,9},{5... | collective-permute-start | bytes 3538952 | tf_op jit(solution)/shard_map/ppermute | solution.py:473
  830.9 17.1 %collective-permute-start.65 = (bf16[96,1536]{1,0:T(8,128)(2,1)S(1)}, bf16[96,1536]{1,0:T(8,128)(2,1)S(1)}, u32[]{:S(2)}, u32[]{:S(2)}) collective-permute-start(bf16[96,1536]{1,0:T(8,128)(2,1)S(1)} %pad_maximum_fusion.16), channel_id=1, source_target_pairs={{0,1},{1,2},{2,3},{3,0},{4,5},{5,6},{6,7},{7,4},{8,9},{9,10},{10,1... | collective-permute-start | bytes 884744 | tf_op jit(solution)/shard_map/ppermute | solution.py:478
  (109 other events, 1793.2 us)

commit v2 on v1

v2 whole, which is shorter than its diff:
```python
import functools

import jax
import jax.numpy as jnp
from jax import lax
from jax.experimental import pallas as pl
from jax.experimental.pallas import tpu as pltpu
from jax.sharding import PartitionSpec as P

HD = 64
PAIR = 128
REACH = 384
EPS = 1e-06
FILL = -1e30
ROOT_HALF = 0.7071067811865476
INV_ROOT_TWO_PI = 0.3989422804014327
HIGHEST = lax.Precision.HIGHEST
F32 = jnp.float32
BF16 = jnp.bfloat16
MESH = pl.DeviceIdType.MESH
ANY = pl.BlockSpec(memory_space=pl.ANY)


def nn(left, right):
    return lax.dot_general(left, right, (((1,), (0,)), ((), ())), preferred_element_type=F32)


def nt(left, right):
    return lax.dot_general(left, right, (((1,), (1,)), ((), ())), preferred_element_type=F32)


def halves(array):
    middle = array.shape[1] // 2
    return array[:, :middle], array[:, middle:]


def row_norm(value):
    centered = value - jnp.mean(value, axis=-1, keepdims=True)
    scale = lax.rsqrt(jnp.mean(centered * centered, axis=-1, keepdims=True) + EPS)
    return centered * scale, scale


def row_norm_back(grad_hat, normed, scale):
    return scale * (
        grad_hat
        - jnp.mean(grad_hat, axis=-1, keepdims=True)
        - normed * jnp.mean(grad_hat * normed, axis=-1, keepdims=True)
    )


def head_mean(value, exact=False):
    wide = value.shape[1]
    rows = lax.broadcasted_iota(jnp.int32, (wide, wide), 0) // HD
    cols = lax.broadcasted_iota(jnp.int32, (wide, wide), 1) // HD
    spread = jnp.where(rows == cols, 1.0 / HD, 0.0).astype(BF16)
    high = value.astype(BF16)
    mean = nn(high, spread)
    if exact:
        mean += nn((value - high.astype(F32)).astype(BF16), spread)
    return mean


def head_norm(value):
    centered = value - head_mean(value, exact=True)
    scale = lax.rsqrt(head_mean(centered * centered) + EPS)
    return centered * scale, scale


def head_norm_back(grad_hat, normed, scale):
    return scale * (grad_hat - head_mean(grad_hat) - normed * head_mean(grad_hat * normed))


def only(array, part):
    return jnp.where(lax.broadcasted_iota(jnp.int32, (1, PAIR), 1) // HD == part, array, jnp.zeros_like(array))


def side(*parts):
    return jnp.concatenate(parts, axis=1)


def whole(shape):
    return pl.BlockSpec(shape, lambda step: (0,) * len(shape))


def column(height, wide, every=1, first=0):
    return pl.BlockSpec((height, wide), lambda step: (0, step * every + first))


def shaped(shape, kind=BF16):
    return jax.ShapeDtypeStruct(shape, kind)


class Gather:
    KINDS = 7

    def __init__(self, shard, near, far, send, recv, local):
        self.shard, self.near, self.far, self.send, self.recv, self.local = shard, near, far, send, recv, local
        self.chunk, self.wide = shard.shape
        self.pieces = near.shape[1] // self.wide
        fsdp, tp = lax.axis_index("fsdp"), lax.axis_index("tp")
        size = lax.axis_size("tp")
        self.x, self.y, self.core = ({"fsdp": jnp.bitwise_xor(fsdp, bit)} for bit in (2, 4, 1))
        self.right, self.left = {"tp": lax.rem(tp + 1, size)}, {"tp": lax.rem(tp + size - 1, size)}

    def greet(self):
        barrier = pltpu.get_barrier_semaphore()
        for target in (self.x, self.y, self.core, self.left):
            pl.semaphore_signal(barrier, inc=1, device_id=target, device_id_type=MESH)
        pl.semaphore_wait(barrier, 4)

    def at(self, piece, start, count, half=None):
        first, wide = piece * self.wide, self.wide
        if half is not None:
            wide //= 2
            first += half * wide
        return self.near.at[pl.ds(start * self.chunk, count * self.chunk), pl.ds(first, wide)]

    def copy(self, piece, kind, source, target, device):
        return pltpu.make_async_remote_copy(
            src_ref=source, dst_ref=target, send_sem=self.send.at[piece, kind], recv_sem=self.recv.at[piece, kind],
            device_id=device, device_id_type=MESH,
        )

    def copies(self, piece, stage):
        if stage == "z":
            source = self.shard if piece == 0 else self.at(piece, 0, 1)
            return [self.copy(piece, 0, source, self.at(piece + 1, 0, 1), self.right)]
        if stage == "first":
            half = self.wide // 2
            left = self.shard.at[:, pl.ds(0, half)] if piece == 0 else self.at(piece, 0, 1, 0)
            right = self.shard.at[:, pl.ds(half, half)] if piece == 0 else self.at(piece, 0, 1, 1)
            return [
                self.copy(piece, 1, left, self.at(piece, 1, 1, 0), self.x),
                self.copy(piece, 2, right, self.at(piece, 2, 1, 1), self.y),
            ]
        if stage == "second":
            return [
                self.copy(piece, 3, self.at(piece, 0, 2, 0), self.at(piece, 2, 2, 0), self.y),
                self.copy(piece, 4, self.at(piece, 0, 1, 1), self.at(piece, 1, 1, 1), self.x),
                self.copy(piece, 5, self.at(piece, 2, 1, 1), self.at(piece, 3, 1, 1), self.x),
            ]
        span = pl.ds(piece * self.wide, self.wide)
        return [self.copy(piece, 6, self.near.at[:, span], self.far.at[:, span], self.core)]

    def start(self, piece, stage):
        for copy in self.copies(piece, stage):
            copy.start()

    def arrived(self, piece, stage):
        for copy in self.copies(piece, stage):
            copy.wait_recv()

    def run(self, event):
        name, piece = event
        if name == "begin":
            self.greet()
            own = pltpu.make_async_copy(self.shard, self.at(0, 0, 1), self.local)
            own.start()
            self.start(0, "z")
            self.start(0, "first")
            own.wait()
        elif name == "A":
            self.arrived(piece - 1, "z")
            if piece + 1 < self.pieces:
                self.start(piece, "z")
            self.start(piece, "first")
        elif name == "B":
            self.arrived(piece, "first")
            self.start(piece, "second")
        elif name == "C":
            self.arrived(piece, "second")
            self.start(piece, "core")
        else:
            for piece in range(self.pieces):
                self.arrived(piece, "core")
                for stage in ("z", "first", "second", "core"):
                    if stage != "z" or piece + 1 < self.pieces:
                        for copy in self.copies(piece, stage):
                            copy.wait_send()


def gather_events(pieces):
    order = [("begin", 0)]
    for piece in range(pieces):
        if piece:
            order.append(("A", piece))
        if piece > 1:
            order.append(("C", piece - 2))
        if piece:
            order.append(("B", piece - 1))
    order += [("C", pieces - 2), ("B", pieces - 1), ("C", pieces - 1), ("end", 0)]
    return order


def spaced(events, counts):
    table = []
    for count in counts:
        table.append(events[:count])
        events = events[count:]
    return table + [events]


def gather_specs(shard, pieces, halved):
    chunk, wide = shard.shape
    full = shaped((halved, pieces * wide))
    semaphores = pltpu.SemaphoreType.DMA((pieces, Gather.KINDS))
    return [whole((chunk, wide))], [full, full], [semaphores, semaphores, pltpu.SemaphoreType.DMA]


def gather_kernel(shard_ref, near_ref, far_ref, send, recv, local):
    gather = Gather(shard_ref, near_ref, far_ref, send, recv, local)
    for event in gather_events(gather.pieces):
        gather.run(event)


def params(collective=None):
    if collective is None:
        return pltpu.CompilerParams()
    return pltpu.CompilerParams(collective_id=collective, has_side_effects=True)


def gather_alone(shard, pieces, halved, collective):
    operands, results, scratch = gather_specs(shard, pieces, halved)
    return pl.pallas_call(
        gather_kernel,
        grid=(1,),
        in_specs=operands,
        out_specs=[ANY] * 2,
        out_shape=results,
        scratch_shapes=scratch,
        compiler_params=params(collective),
        name="gather_block",
    )(shard)


def halo_kernel(a_ref, out_ref, send, recv):
    rows = a_ref.shape[0]
    spill = REACH - rows
    place, size = lax.axis_index("tp"), lax.axis_size("tp")
    out_ref[REACH : REACH + rows, :] = a_ref[...]
    moves = [
        (1, pl.ds(0, rows), pl.ds(spill, rows)),
        (-1, pl.ds(0, rows), pl.ds(REACH + rows, rows)),
        (2, pl.ds(rows - spill, spill), pl.ds(0, spill)),
        (-2, pl.ds(0, spill), pl.ds(REACH + 2 * rows, spill)),
    ]
    barrier = pltpu.get_barrier_semaphore()
    inside = lambda other: jnp.logical_and(other >= 0, other < size)
    for distance, _, _ in moves:

        @pl.when(inside(place + distance))
        def _():
            pl.semaphore_signal(barrier, inc=1, device_id={"tp": place + distance}, device_id_type=MESH)

    pl.semaphore_wait(barrier, jnp.minimum(place, 2) + jnp.minimum(size - 1 - place, 2))

    def copy(index):
        distance, source, target = moves[index]
        return pltpu.make_async_remote_copy(
            src_ref=a_ref.at[source, :], dst_ref=out_ref.at[target, :], send_sem=send.at[index], recv_sem=recv.at[index],
            device_id={"tp": place + distance}, device_id_type=MESH,
        )

    for index, (distance, _, _) in enumerate(moves):

        @pl.when(inside(place + distance))
        def _():
            copy(index).start()

        @pl.when(jnp.logical_not(inside(place - distance)))
        def _():
            target = moves[index][2]
            out_ref[target, :] = jnp.zeros((target.size, out_ref.shape[1]), BF16)

    for index, (distance, _, _) in enumerate(moves):

        @pl.when(inside(place + distance))
        def _():
            copy(index).wait_send()

        @pl.when(inside(place - distance))
        def _():
            copy(index).wait_recv()


def halo(a_own, collective):
    rows, width = a_own.shape
    return pl.pallas_call(
        halo_kernel,
        grid=(1,),
        in_specs=[whole((rows, width))],
        out_specs=whole((rows + 2 * REACH, width)),
        out_shape=shaped((rows + 2 * REACH, width)),
        scratch_shapes=[pltpu.SemaphoreType.DMA((4,)), pltpu.SemaphoreType.DMA((4,))],
        compiler_params=params(collective),
        name="halo",
    )(a_own)


class Rows:
    def __init__(self, layers, grid):
        self.layers, self.grid = layers, grid

    def ln_gain(self, layer, which):
        return 2 * self.grid + 2 * layer + which

    def ln_bias(self, layer, which):
        return 2 * self.grid + 2 * self.layers + 2 * layer + which

    def out_bias(self, layer):
        return 2 * self.grid + 4 * self.layers + layer

    def last_bias(self, layer):
        return 2 * self.grid + 5 * self.layers + layer

    def proj_bias(self, layer, which):
        return 3 * layer + which

    def head_gain(self, layer, which):
        return 3 * self.layers + 2 * layer + which

    def head_bias(self, layer):
        return 5 * self.layers + layer


def line(ref, row, start=0, wide=None):
    return ref[row : row + 1, start : start + (wide or ref.shape[1] - start)]


def hooked(gather, table, slots):
    step = pl.program_id(0)

    def at(slot):
        if gather is None:
            return
        for index in range(slot, len(table) - 1, slots):
            if table[index]:

                @pl.when(step == index // slots)
                def _(events=table[index]):
                    for event in events:
                        gather.run(event)

    def after():
        if gather is None:
            return

        @pl.when(step == pl.num_programs(0) - 1)
        def _():
            for event in table[-1]:
                gather.run(event)

    return at, after


def attend_kernel(*refs, rows_of, layer, table):
    a_ref, near_ref, far_ref, heads_ref, feats_ref, x_ref, seg_k_ref, seg_q_ref = refs[:8]
    rest = refs[8:]
    gather = None
    if table:
        gather = Gather(rest[0], *rest[11:13], *rest[-3:])
        rest = rest[1:11] + rest[13:-3]
    q_ref, kv_ref, q_hat_ref, k_hat_ref, q_scale_ref, k_scale_ref, p_ref, o_ref, mid_ref, m_ref = rest[:10]
    mask_ref, acc_ref = rest[10:]
    rows = q_ref.shape[0]
    half = near_ref.shape[0]
    step = pl.program_id(0)
    at, after = hooked(gather, table, 2)
    at(0)

    @pl.when(step == 0)
    def _():
        mask_ref[...] = jnp.where(seg_k_ref[...] == seg_q_ref[...], 0.0, FILL)
        acc_ref[...] = jnp.zeros_like(acc_ref)

    tile = lambda row, which: line(heads_ref, row, which * PAIR, PAIR)
    bias = [rows_of.proj_bias(layer, which) for which in range(3)]
    q_gain, k_gain = (rows_of.head_gain(layer, which) for which in range(2))
    q_shift = rows_of.head_bias(layer)
    near, distant = halves(a_ref[...])
    own, own_far = halves(a_ref[REACH : REACH + rows, :])
    kv = nn(near, near_ref[:, PAIR : 4 * PAIR]) + nn(distant, far_ref[:, PAIR : 4 * PAIR])
    kv += side(tile(bias[1], 0), tile(bias[2], 0), tile(bias[1], 1) + tile(bias[2], 2))
    q = side(
        nn(own, near_ref[:, :PAIR]) + nn(own_far, far_ref[:, :PAIR]),
        nn(own, near_ref[:, 4 * PAIR : 5 * PAIR]) + nn(own_far, far_ref[:, 4 * PAIR : 5 * PAIR]),
    ) + line(heads_ref, bias[0], 0, 2 * PAIR)
    q_hat, q_scale = head_norm(q)
    k_hat, k_scale = head_norm(side(kv[:, :PAIR], kv[:, 2 * PAIR :]))
    qn = (q_hat * line(heads_ref, q_gain, 0, 2 * PAIR) + line(heads_ref, q_shift, 0, 2 * PAIR)).astype(BF16)
    qn = side(qn[:, :PAIR], only(qn[:, PAIR:], 0))
    kn = (k_hat * line(heads_ref, k_gain, 0, 2 * PAIR)).astype(BF16)
    v = kv[:, PAIR:].astype(BF16)
    low = lax.broadcasted_iota(jnp.int32, (1, PAIR), 1) < HD
    first, second = kn[:, :PAIR], jnp.where(low, kn[:, PAIR:], v[:, PAIR:])
    values = v[:, :PAIR]
    q_ref[...] = qn
    kv_ref[...] = side(first, values, second)
    q_hat_ref[...] = q_hat.astype(BF16)
    k_hat_ref[...] = k_hat.astype(BF16)
    q_scale_ref[...] = q_scale.astype(BF16)
    k_scale_ref[...] = k_scale.astype(BF16)
    at(1)
    values_t, second_t = values.T, second.T
    mixed = []
    for head in range(3):
        keys = (first, first, second)[head]
        query = only(qn[:, PAIR * (head // 2) : PAIR * (head // 2 + 1)] * HD ** (-0.5), head % 2).astype(BF16)
        scores = nt(keys, query) + mask_ref[...]
        weights = jnp.exp(scores - jnp.max(scores, axis=0, keepdims=True))
        total = jnp.sum(weights, axis=0, keepdims=True)
        probs = (weights * (1.0 / total)).astype(BF16)
        p_ref[head] = probs
        mixed.append(nn((values_t[:HD], values_t[HD:], second_t[HD:])[head], probs))
    o = jnp.concatenate([jnp.zeros_like(mixed[2]), mixed[2], mixed[0], mixed[1]], axis=0).T.astype(BF16)
    o_ref[...] = o
    acc_ref[:, :half] += nt(o, near_ref[:, 4 * PAIR :])
    acc_ref[:, half:] += nt(o, far_ref[:, 4 * PAIR :])

    @pl.when(step == pl.num_programs(0) - 1)
    def _():
        mid = x_ref[...] + (acc_ref[...] + line(feats_ref, rows_of.out_bias(layer)))
        mid_ref[...] = mid
        hat, _ = row_norm(mid)
        m_ref[...] = (
            hat * line(feats_ref, rows_of.ln_gain(layer, 1)) + line(feats_ref, rows_of.ln_bias(layer, 1))
        ).astype(BF16)

    after()


def attend(a_win, near, far, heads, feats, x, seg_k, seg_q, rows_of, layer, shard=None, collective=None):
    window, width = a_win.shape
    rows = x.shape[0]
    half = width // 2
    pieces = near.shape[1] // (6 * PAIR)
    extra = gather_specs(shard, pieces, half) if shard is not None else ([], [], [])
    table = spaced(gather_events(pieces), [1, 0, 1, 1, 1, 1, 1, 2]) if shard is not None else None
    outs = [(rows, 2 * PAIR), (window, 3 * PAIR), (rows, 2 * PAIR), (window, 2 * PAIR), (rows, 2 * PAIR), (window, 2 * PAIR)]
    return pl.pallas_call(
        functools.partial(attend_kernel, rows_of=rows_of, layer=layer, table=table),
        grid=(pieces,),
        in_specs=[
            whole((window, width)), column(half, 6 * PAIR), column(half, 6 * PAIR), column(heads.shape[0], 3 * PAIR),
            whole(feats.shape), whole((rows, width)), whole((window, 1)), whole((1, rows)), *extra[0],
        ],
        out_specs=[column(*shape) for shape in outs]
        + [pl.BlockSpec((3, window, rows), lambda step: (step, 0, 0)), column(rows, 2 * PAIR)]
        + [whole((rows, width))] * 2 + [ANY] * len(extra[1]),
        out_shape=[shaped((height, pieces * wide)) for height, wide in outs]
        + [shaped((3 * pieces, window, rows)), shaped((rows, pieces * 2 * PAIR)), shaped((rows, width), F32), shaped((rows, width))]
        + extra[1],
        scratch_shapes=[pltpu.VMEM((window, rows), F32), pltpu.VMEM((rows, width), F32), *extra[2]],
        compiler_params=params(collective),
        cost_estimate=pl.CostEstimate(
            flops=2 * window * width * width * 2 + 8 * window * rows * width * 4,
            bytes_accessed=20 * window * width,
            transcendentals=3 * pieces * window * rows,
        ),
        name="attend",
    )(a_win, near, far, heads, feats, x, seg_k, seg_q, *([] if shard is None else [shard]))


def mlp_kernel(*refs, rows_of, layer, table):
    m_ref, mid_ref, up_near_ref, up_far_ref, down_near_ref, down_far_ref, up_shift_ref, feats_ref = refs[:8]
    rest = refs[8:]
    gather = None
    if table:
        gather = Gather(rest[0], *rest[5:7], *rest[-3:])
        rest = rest[1:5] + rest[7:-3]
    act_ref, slope_ref, x2_ref, a_ref, acc_ref = rest
    half = up_near_ref.shape[0]
    step = pl.program_id(0)
    at, after = hooked(gather, table, 2)
    at(0)

    @pl.when(step == 0)
    def _():
        acc_ref[...] = jnp.zeros_like(acc_ref)

    near, distant = halves(m_ref[...])
    hidden = nn(near, up_near_ref[...]) + nn(distant, up_far_ref[...]) + up_shift_ref[...]
    at(1)
    phi = 0.5 * (1.0 + lax.erf(hidden * ROOT_HALF))
    act = (hidden * phi).astype(BF16)
    act_ref[...] = act
    slope_ref[...] = (phi + hidden * jnp.exp(-0.5 * hidden * hidden) * INV_ROOT_TWO_PI).astype(BF16)
    acc_ref[:, :half] += nt(act, down_near_ref[...])
    acc_ref[:, half:] += nt(act, down_far_ref[...])

    @pl.when(step == pl.num_programs(0) - 1)
    def _():
        x2 = mid_ref[...] + (acc_ref[...] + line(feats_ref, rows_of.last_bias(layer)))
        x2_ref[...] = x2
        hat, _ = row_norm(x2)
        after = min(layer + 1, rows_of.layers - 1)
        a_ref[...] = (
            hat * line(feats_ref, rows_of.ln_gain(after, 0)) + line(feats_ref, rows_of.ln_bias(after, 0))
        ).astype(BF16)

    after()


def mlp(m, mid, near, far, up_shift, feats, rows_of, layer, shard=None, collective=None):
    rows, width = mid.shape
    half = width // 2
    hidden = up_shift.shape[1]
    pieces = lax.axis_size("tp")
    wide = hidden // pieces
    extra = gather_specs(shard, pieces, half) if shard is not None else ([], [], [])
    table = spaced(gather_events(pieces), [1, 0, 1, 1, 1, 1, 1, 2]) if shard is not None else None
    full = whole((rows, width))
    return pl.pallas_call(
        functools.partial(mlp_kernel, rows_of=rows_of, layer=layer, table=table),
        grid=(pieces,),
        in_specs=[
            full, full, column(half, wide, 2), column(half, wide, 2), column(half, wide, 2, 1), column(half, wide, 2, 1),
            column(1, wide), whole(feats.shape), *extra[0],
        ],
        out_specs=[column(rows, wide), column(rows, wide), full, full] + [ANY] * len(extra[1]),
        out_shape=[shaped((rows, hidden)), shaped((rows, hidden)), shaped((rows, width), F32), shaped((rows, width))] + extra[1],
        scratch_shapes=[pltpu.VMEM((rows, width), F32), *extra[2]],
        compiler_params=params(collective),
        cost_estimate=pl.CostEstimate(
            flops=4 * rows * width * hidden, bytes_accessed=4 * width * hidden, transcendentals=2 * rows * hidden
        ),
        name="mlp",
    )(m, mid, near, far, near, far, up_shift, feats, *([] if shard is None else [shard]))


def mlp_back_kernel(
    g_ref, down_near_ref, down_far_ref, slope_ref, up_near_ref, up_far_ref, mid_ref, feats_ref,
    gz_ref, gh_ref, up_shift_grad_ref, g1_ref, gr_ref, small_ref, acc_ref, *, gain_row,
):
    half = up_near_ref.shape[0]
    step = pl.program_id(0)

    @pl.when(step == 0)
    def _():
        gz_ref[...] = g_ref[...].astype(BF16)
        acc_ref[...] = jnp.zeros_like(acc_ref)

    near, distant = halves(gz_ref[...])
    gh = ((nn(near, down_near_ref[...]) + nn(distant, down_far_ref[...])) * slope_ref[...].astype(F32)).astype(BF16)
    gh_ref[...] = gh
    up_shift_grad_ref[...] = jnp.sum(gh.astype(F32), axis=0, keepdims=True)
    acc_ref[:, :half] += nt(gh, up_near_ref[...])
    acc_ref[:, half:] += nt(gh, up_far_ref[...])

    @pl.when(step == pl.num_programs(0) - 1)
    def _():
        gm = acc_ref[...]
        hat, scale = row_norm(mid_ref[...])
        g1 = g_ref[...] + row_norm_back(gm * line(feats_ref, gain_row), hat, scale)
        gr = g1.astype(BF16)
        g1_ref[...] = g1
        gr_ref[...] = gr
        small_ref[...] = jnp.zeros_like(small_ref)
        small_ref[0:1, :] = jnp.sum(gz_ref[...].astype(F32), axis=0, keepdims=True)
        small_ref[1:2, :] = jnp.sum(gr.astype(F32), axis=0, keepdims=True)
        small_ref[2:3, :] = jnp.sum(gm * hat, axis=0, keepdims=True)
        small_ref[3:4, :] = jnp.sum(gm, axis=0, keepdims=True)


def mlp_back(grad, near, far, slope, mid, feats, gain_row):
    rows, width = grad.shape
    half = width // 2
    hidden = slope.shape[1]
    pieces = lax.axis_size("tp")
    wide = hidden // pieces
    full = whole((rows, width))
    return pl.pallas_call(
        functools.partial(mlp_back_kernel, gain_row=gain_row),
        grid=(pieces,),
        in_specs=[
            full, column(half, wide, 2, 1), column(half, wide, 2, 1), column(rows, wide), column(half, wide, 2),
            column(half, wide, 2), full, whole(feats.shape),
        ],
        out_specs=[full, column(rows, wide), column(1, wide), full, full, whole((8, width))],
        out_shape=[
            shaped((rows, width)), shaped((rows, hidden)), shaped((1, hidden), F32), shaped((rows, width), F32),
            shaped((rows, width)), shaped((8, width), F32),
        ],
        scratch_shapes=[pltpu.VMEM((rows, width), F32)],
        cost_estimate=pl.CostEstimate(
            flops=4 * rows * width * hidden, bytes_accessed=4 * width * hidden, transcendentals=0
        ),
        name="mlp_back",
    )(grad, near, far, slope, near, far, mid, feats)


def attend_back_kernel(
    gr_ref, q_ref, kv_ref, q_hat_ref, k_hat_ref, q_scale_ref, k_scale_ref, p_ref, near_ref, far_ref, heads_ref,
    gq_ref, gkv_ref, mine_ref, left_ref, right_ref, small_ref, acc_ref, *, rows_of, layer,
):
    rows = gr_ref.shape[0]
    half = near_ref.shape[0]
    step = pl.program_id(0)

    @pl.when(step == 0)
    def _():
        acc_ref[...] = jnp.zeros_like(acc_ref)

    near, distant = halves(gr_ref[...])
    go = (nn(near, near_ref[:, 4 * PAIR :]) + nn(distant, far_ref[:, 4 * PAIR :])).astype(BF16)
    qn, kv = q_ref[...], kv_ref[...]
    first, values, second = kv[:, :PAIR], kv[:, PAIR : 2 * PAIR], kv[:, 2 * PAIR :]
    first_t, second_t = first.T, second.T
    grad_q, grad_k, grad_v = [], [], []
    for head in range(3):
        go_head = only(go[:, PAIR:], head) if head < 2 else only(go[:, :PAIR], 1)
        query = only(qn[:, PAIR * (head // 2) : PAIR * (head // 2 + 1)] * HD ** (-0.5), head % 2).astype(BF16)
        stored = p_ref[head]
        probs = stored.astype(F32)
        grad_probs = nt((values, values, second)[head], go_head)
        delta = jnp.sum(probs * grad_probs, axis=0, keepdims=True)
        grad_scores = (probs * (grad_probs - delta)).astype(BF16)
        grad_v.append(nn(stored, go_head))
        grad_k.append(nn(grad_scores, query))
        grad_q.append(nn((first_t[:HD], first_t[HD:], second_t[:HD])[head], grad_scores))
    zero = jnp.zeros_like(grad_q[2])
    grad_q = (jnp.concatenate(grad_q + [zero], axis=0) * HD ** (-0.5)).T
    grad_k = side(grad_k[0] + grad_k[1], grad_k[2])
    pair_v, last_v = grad_v[0] + grad_v[1], grad_v[2]
    q_hat = q_hat_ref[...].astype(F32)
    k_hat = k_hat_ref[...].astype(F32)
    gain = lambda which: line(heads_ref, rows_of.head_gain(layer, which), 0, 2 * PAIR)
    gq = head_norm_back(grad_q * gain(0), q_hat, q_scale_ref[...].astype(F32)).astype(BF16)
    gk = head_norm_back(grad_k * gain(1), k_hat, k_scale_ref[...].astype(F32)).astype(BF16)
    gkv = side(gk[:, :PAIR], pair_v.astype(BF16), gk[:, PAIR:] + last_v.astype(BF16))
    gq_ref[...] = gq
    gkv_ref[...] = gkv
    total = lambda value: jnp.sum(value.astype(F32), axis=0, keepdims=True)
    small_ref[...] = jnp.zeros_like(small_ref)
    small_ref[0:1, : 2 * PAIR] = total(grad_q * q_hat)
    small_ref[1:2, : 2 * PAIR] = total(grad_k * k_hat)
    small_ref[2:3, : 2 * PAIR] = total(grad_q)
    small_ref[3:4, : 2 * PAIR] = total(gq)
    small_ref[4:5, : 2 * PAIR] = total(gk)
    small_ref[5:6, :PAIR] = total(pair_v.astype(BF16))
    small_ref[5:6, 2 * PAIR :] = total(last_v.astype(BF16))
    acc_ref[:, :half] += nt(gkv, near_ref[:, PAIR : 4 * PAIR])
    acc_ref[:, half:] += nt(gkv, far_ref[:, PAIR : 4 * PAIR])
    own = slice(REACH, REACH + rows)
    for ref, cols in ((near_ref, slice(0, half)), (far_ref, slice(half, 2 * half))):
        acc_ref[own, cols] += nt(gq[:, :PAIR], ref[:, :PAIR]) + nt(gq[:, PAIR:], ref[:, 4 * PAIR : 5 * PAIR])

    @pl.when(step == pl.num_programs(0) - 1)
    def _():
        left_ref[...] = acc_ref[:REACH, :].astype(BF16)
        mine_ref[...] = acc_ref[own, :]
        right_ref[...] = acc_ref[REACH + rows :, :].astype(BF16)


def attend_back(gr, stored, near, far, heads, rows_of, layer):
    rows, width = gr.shape
    half = width // 2
    window = rows + 2 * REACH
    pieces = near.shape[1] // (6 * PAIR)
    full = whole((rows, width))
    return pl.pallas_call(
        functools.partial(attend_back_kernel, rows_of=rows_of, layer=layer),
        grid=(pieces,),
        in_specs=[
            full, column(rows, 2 * PAIR), column(window, 3 * PAIR), column(rows, 2 * PAIR), column(window, 2 * PAIR),
            column(rows, 2 * PAIR), column(window, 2 * PAIR), pl.BlockSpec((3, window, rows), lambda step: (step, 0, 0)),
            column(half, 6 * PAIR), column(half, 6 * PAIR), column(heads.shape[0], 3 * PAIR),
        ],
        out_specs=[
            column(rows, 2 * PAIR), column(window, 3 * PAIR), full, whole((REACH, width)), whole((REACH, width)),
            column(8, 3 * PAIR),
        ],
        out_shape=[
            shaped((rows, pieces * 2 * PAIR)), shaped((window, pieces * 3 * PAIR)), shaped((rows, width), F32),
            shaped((REACH, width)), shaped((REACH, width)), shaped((8, pieces * 3 * PAIR), F32),
        ],
        scratch_shapes=[pltpu.VMEM((window, width), F32)],
        cost_estimate=pl.CostEstimate(
            flops=2 * window * width * width * 2 + 20 * window * rows * width * 2,
            bytes_accessed=20 * window * width,
            transcendentals=0,
        ),
        name="attend_back",
    )(gr, *stored, near, far, heads)


def attn_weight_kernel(a_ref, gq_ref, gkv_ref, gr_ref, o_ref, keep_ref, send_ref, a_t_ref, gr_t_ref):
    rows = gq_ref.shape[0]
    half = keep_ref.shape[0]

    @pl.when(pl.program_id(0) == 0)
    def _():
        a_t_ref[...] = a_ref[...].T
        gr_t_ref[...] = gr_ref[...].T

    for part, ref in ((slice(0, half), keep_ref), (slice(half, 2 * half), send_ref)):
        from_q = nn(a_t_ref[part, REACH : REACH + rows], gq_ref[...])
        from_o = nn(gr_t_ref[part, :], o_ref[...])
        ref[:, :PAIR] = from_q[:, :PAIR].astype(BF16)
        ref[:, PAIR : 4 * PAIR] = nn(a_t_ref[part, :], gkv_ref[...]).astype(BF16)
        ref[:, 4 * PAIR : 5 * PAIR] = (from_q[:, PAIR:] + from_o[:, :PAIR]).astype(BF16)
        ref[:, 5 * PAIR :] = from_o[:, PAIR:].astype(BF16)


def attn_weight_grads(a_win, gq, gkv, gr, o):
    window, width = a_win.shape
    rows = gr.shape[0]
    half = width // 2
    pieces = gq.shape[1] // (2 * PAIR)
    out = column(half, 6 * PAIR)
    return pl.pallas_call(
        attn_weight_kernel,
        grid=(pieces,),
        in_specs=[
            whole((window, width)), column(rows, 2 * PAIR), column(window, 3 * PAIR), whole((rows, width)),
            column(rows, 2 * PAIR),
        ],
        out_specs=[out, out],
        out_shape=[shaped((half, pieces * 6 * PAIR))] * 2,
        scratch_shapes=[pltpu.VMEM((width, window), BF16), pltpu.VMEM((width, rows), BF16)],
        cost_estimate=pl.CostEstimate(
            flops=2 * width * width * (2 * window + 2 * rows), bytes_accessed=8 * width * width, transcendentals=0
        ),
        name="attn_weight_grads",
    )(a_win, gq, gkv, gr, o)


def mlp_weight_kernel(m_ref, gh_ref, gz_ref, act_ref, keep_ref, send_ref, m_t_ref, gz_t_ref):
    half = keep_ref.shape[0]
    wide = gh_ref.shape[1]

    @pl.when(pl.program_id(0) == 0)
    def _():
        m_t_ref[...] = m_ref[...].T
        gz_t_ref[...] = gz_ref[...].T

    for part, ref in ((slice(0, half), keep_ref), (slice(half, 2 * half), send_ref)):
        ref[:, :wide] = nn(m_t_ref[part, :], gh_ref[...]).astype(BF16)
        ref[:, wide:] = nn(gz_t_ref[part, :], act_ref[...]).astype(BF16)


def mlp_weight_grads(m, gh, gz, act):
    rows, width = m.shape
    half = width // 2
    hidden = gh.shape[1]
    pieces = lax.axis_size("tp")
    wide = hidden // pieces
    out = column(half, 2 * wide)
    return pl.pallas_call(
        mlp_weight_kernel,
        grid=(pieces,),
        in_specs=[whole((rows, width)), column(rows, wide), whole((rows, width)), column(rows, wide)],
        out_specs=[out, out],
        out_shape=[shaped((half, 2 * hidden))] * 2,
        scratch_shapes=[pltpu.VMEM((width, rows), BF16), pltpu.VMEM((width, rows), BF16)],
        cost_estimate=pl.CostEstimate(
            flops=4 * width * hidden * rows, bytes_accessed=4 * width * hidden, transcendentals=0
        ),
        name="mlp_weight_grads",
    )(m, gh, gz, act)


def flip(array, bit, axis="fsdp"):
    size = lax.axis_size(axis)
    return lax.ppermute(array, axis, [(i, i ^ (1 << bit)) for i in range(size)])


def ring(array):
    size = lax.axis_size("tp")
    return lax.ppermute(array, "tp", [(i, (i + 1) % size) for i in range(size)])


def hop(array, distance):
    size = lax.axis_size("tp")
    return lax.ppermute(array, "tp", [(i, i + distance) for i in range(size) if 0 <= i + distance < size])


def bits_of(size):
    return size.bit_length() - 1


def row_bits(first_top):
    count = bits_of(lax.axis_size("fsdp"))
    tops = [count - 1, count - 2] if first_top else [count - 2, count - 1]
    return list(range(1, count - 2)), tops


def gather_by_permutes(block, first_top):
    pieces = [block]
    for _ in range(lax.axis_size("tp") - 1):
        pieces.append(ring(pieces[-1]))
    block = jnp.concatenate(pieces, axis=1)
    low, tops = row_bits(first_top)
    have = []
    for bit in low + tops:
        axis = sum(other > bit for other in have)
        block = jnp.stack([block, flip(block, bit)], axis=axis)
        have.append(bit)
    block = block.reshape((-1, block.shape[-1]))
    return block, flip(block, 0)


def add(left, right, kind=BF16):
    return (left.astype(F32) + right.astype(F32)).astype(kind)


def reduce_by_permutes(keep, send, first_top):
    low, tops = row_bits(first_top)
    block = add(keep, flip(send, 0))
    order = tops + low[::-1]
    have = sorted(order, reverse=True)
    block = block.reshape((2,) * len(have) + (-1, block.shape[-1]))
    for bit in order:
        axis = have.index(bit)
        mine = lax.index_in_dim(block, 0, axis, keepdims=False)
        other = lax.index_in_dim(block, 1, axis, keepdims=False)
        block = add(mine, flip(other, bit))
        have.remove(bit)
    pieces = jnp.split(block, lax.axis_size("tp"), axis=1)
    total = pieces[1]
    for piece in pieces[2:]:
        total = add(ring(total), piece)
    return add(ring(total), pieces[0], F32)


def attn_shard(w_qkv, w_out):
    q, k, v = (w_qkv[:, which] for which in range(3))
    o = w_out.T
    return side(q[:, :PAIR], k[:, :PAIR], v[:, :PAIR], k[:, PAIR:], v[:, PAIR:], q[:, PAIR:], o[:, PAIR:], o[:, :PAIR])


def attn_unshard(block):
    tile = lambda start, wide=PAIR: block[:, start : start + wide]
    q = side(tile(0), tile(4 * PAIR, HD))
    k = side(tile(PAIR), tile(3 * PAIR, HD))
    v = side(tile(2 * PAIR), tile(3 * PAIR + HD, HD))
    o = side(tile(5 * PAIR), tile(4 * PAIR + HD, HD))
    return jnp.stack([q, k, v], axis=1), o.T


def body(
    tokens, segment_ids, patch_pos, row_table, col_table, ln_gain, ln_bias, qkv_bias, qk_gain, query_bias, out_bias,
    fc1_bias, fc2_bias, w_qkv, w_out, w_fc1, w_fc2, cotangent,
):
    layers = w_qkv.shape[0]
    rows, width = tokens.shape
    half = width // 2
    fsdp, tp = lax.axis_size("fsdp"), lax.axis_size("tp")
    f_index, t_index = lax.axis_index("fsdp"), lax.axis_index("tp")
    hidden = fc1_bias.shape[1] * fsdp * tp
    grid = row_table.shape[0]
    fine = width // (fsdp * tp)
    parts = hidden // width
    in_kernel = fsdp == 8
    rows_of = Rows(layers, grid)

    place = jnp.arange(width, dtype=jnp.int32)
    chunk = width // fsdp
    slot = place // chunk
    away = (slot % (fsdp // 2)) * 2 + slot // (fsdp // 2)
    feature_at = (f_index ^ away) * chunk + place % chunk
    head_cols = width // tp
    spot = jnp.arange(tp * 3 * PAIR, dtype=jnp.int32)
    tile, part = spot % (3 * PAIR) // PAIR, spot % PAIR // HD
    head = jnp.where(tile == 0, part, jnp.where(tile == part + 1, 2, -fsdp * tp))
    head_at = ((t_index - spot // (3 * PAIR)) % tp) * head_cols + head * HD + spot % HD
    far = place // fine
    arrived_at = ((f_index ^ (far // tp)) * tp + (t_index ^ (far % tp))) * fine + place % fine
    to_feature = (arrived_at[:, None] == feature_at[None, :]).astype(BF16)
    to_head = (arrived_at[:, None] == head_at[None, :]).astype(BF16)
    reorder = (place[:, None] == feature_at[None, :]).astype(BF16)
    device = jnp.arange(fsdp * tp, dtype=jnp.int32)
    device_at = (f_index ^ (device // tp)) * tp + (t_index ^ (device % tp))
    wanted = ((t_index - device // fsdp) % tp) * fsdp + device % fsdp
    to_hidden = (wanted[:, None] == device_at[None, :]).astype(BF16)

    shares = [row_table, col_table] + [
        item.reshape(-1, fine) for item in (ln_gain, ln_bias, out_bias, fc2_bias, qkv_bias, qk_gain, query_bias)
    ]
    small = jnp.concatenate(shares + [fc1_bias.reshape(layers * parts, fine)], axis=0)
    count = small.shape[0]
    flat = small.reshape(1, -1)
    for bit in range(bits_of(tp)):
        flat = jnp.concatenate([flat, flip(flat, bit, "tp")], axis=0)
    for bit in range(bits_of(fsdp)):
        flat = jnp.concatenate([flat, flip(flat, bit)], axis=0)
    gathered = flat.reshape(fsdp * tp, count, fine)
    lined = gathered.transpose(1, 0, 2).reshape(count, width)
    wide = 2 * grid + 6 * layers
    feats = jnp.dot(lined[:wide], to_feature, preferred_element_type=F32)
    heads = jnp.dot(lined[wide : wide + 6 * layers], to_head, preferred_element_type=F32)
    up_shift = jnp.einsum(
        "or,rlsi->losi",
        to_hidden,
        gathered[:, wide + 6 * layers :].reshape(fsdp * tp, layers, parts, fine),
        preferred_element_type=F32,
    ).reshape(layers, 1, hidden)

    attn_shards = [attn_shard(w_qkv[layer], w_out[layer]) for layer in range(layers)]
    mlp_shards = [side(w_fc1[layer], w_fc2[layer].T) for layer in range(layers)]
    if in_kernel:
        attn_near, attn_far = gather_alone(attn_shards[0], tp, half, 0)

    grid_ids = jnp.arange(grid, dtype=jnp.int32)
    row_hot = patch_pos[0][:, None] == grid_ids[None, :]
    col_hot = patch_pos[1][:, None] == grid_ids[None, :]
    residual = (
        jnp.dot(tokens, reorder, preferred_element_type=F32)
        + jnp.dot(row_hot.astype(BF16), feats[:grid].astype(BF16), preferred_element_type=F32)
        + jnp.dot(col_hot.astype(BF16), feats[grid : 2 * grid].astype(BF16), preferred_element_type=F32)
    )
    segments = segment_ids[0]
    padded = jnp.pad(segments, (REACH, REACH), constant_values=-1)
    seg_k = lax.dynamic_slice_in_dim(padded, t_index * rows, rows + 2 * REACH).reshape(-1, 1)
    seg_q = lax.dynamic_slice_in_dim(segments, t_index * rows, rows).reshape(1, -1)
    spill = REACH - rows

    hat, _ = row_norm(residual)
    a_own = (hat * feats[rows_of.ln_gain(0, 0)] + feats[rows_of.ln_bias(0, 0)]).astype(BF16)
    saved, weights = [], []
    for layer in range(layers):
        if in_kernel:
            a_win = halo(a_own, 10 + layer)
            *kept, mid, m, mlp_near, mlp_far = attend(
                a_win, attn_near, attn_far, heads, feats, residual, seg_k, seg_q, rows_of, layer, mlp_shards[layer],
                20 + layer,
            )
        else:
            a_win = jnp.concatenate(
                [hop(a_own[rows - spill :], 2), hop(a_own, 1), a_own, hop(a_own, -1), hop(a_own[:spill], -2)], axis=0
            )
            attn_near, attn_far = gather_by_permutes(attn_shards[layer], layer % 2 == 0)
            *kept, mid, m = attend(a_win, attn_near, attn_far, heads, feats, residual, seg_k, seg_q, rows_of, layer)
            mlp_near, mlp_far = gather_by_permutes(mlp_shards[layer], layer % 2 == 1)
        weights.append((attn_near, attn_far, mlp_near, mlp_far))
        if in_kernel and layer + 1 < layers:
            act, slope, x2, a_own, attn_near, attn_far = mlp(
                m, mid, mlp_near, mlp_far, up_shift[layer], feats, rows_of, layer, attn_shards[layer + 1], 30 + layer
            )
        else:
            act, slope, x2, a_own = mlp(m, mid, mlp_near, mlp_far, up_shift[layer], feats, rows_of, layer)
        saved.append((residual, a_win, kept, mid, m, act, slope))
        residual = x2

    restore = functools.partial(
        lax.dot_general, dimension_numbers=(((1,), (1,)), ((), ())), precision=HIGHEST, preferred_element_type=F32
    )
    exact = reorder.astype(F32)
    activations = restore(residual, exact)
    grad = jnp.dot(cotangent, exact, precision=HIGHEST, preferred_element_type=F32)
    kept_sums = [None] * layers
    w_qkv_grad, w_out_grad, w_fc1_grad, w_fc2_grad = ([None] * layers for _ in range(4))
    for layer in reversed(range(layers)):
        attn_near, attn_far, mlp_near, mlp_far = weights[layer]
        x, a_win, kept, mid, m, act, slope = saved[layer]
        *stored, o = kept
        gz, gh, up_grad, g1, gr, mlp_small = mlp_back(
            grad, mlp_near, mlp_far, slope, mid, feats, rows_of.ln_gain(layer, 1)
        )
        keep, send = mlp_weight_grads(m, gh, gz, act)
        block = reduce_by_permutes(keep, send, layer % 2 == 0)
        middle = block.shape[1] // 2
        w_fc1_grad[layer], w_fc2_grad[layer] = block[:, :middle], block[:, middle:].T
        gq, gkv, mine, left, right, attn_small = attend_back(gr, stored, attn_near, attn_far, heads, rows_of, layer)
        keep, send = attn_weight_grads(a_win, gq, gkv, gr, o)
        w_qkv_grad[layer], w_out_grad[layer] = attn_unshard(reduce_by_permutes(keep, send, layer % 2 == 1))
        ends = jnp.concatenate([hop(right[rows:], 2), hop(left[:spill], -2)], axis=0).astype(F32)
        attn_grad = mine + hop(right[:rows], 1).astype(F32) + hop(left[spill:], -1).astype(F32) + ends
        hat, scale = row_norm(x)
        grad = g1 + row_norm_back(attn_grad * feats[rows_of.ln_gain(layer, 0)], hat, scale)
        kept_sums[layer] = (
            jnp.sum(attn_grad * hat, axis=0), jnp.sum(attn_grad, axis=0), mlp_small, attn_small,
            up_grad.reshape(parts, width),
        )

    token_grad = restore(grad, exact)
    row_grad = jnp.einsum("tg,td->gd", row_hot.astype(F32), grad, precision=HIGHEST)
    col_grad = jnp.einsum("tg,td->gd", col_hot.astype(F32), grad, precision=HIGHEST)
    featured = [row_grad, col_grad]
    featured.append(jnp.stack([item for a_gain, _, sums, _, _ in kept_sums for item in (a_gain, sums[2])]))
    featured.append(jnp.stack([item for _, a_shift, sums, _, _ in kept_sums for item in (a_shift, sums[3])]))
    featured.append(jnp.stack([sums[1] for _, _, sums, _, _ in kept_sums]))
    featured.append(jnp.stack([sums[0] for _, _, sums, _, _ in kept_sums]))
    headed = jnp.concatenate(
        [sums[3:6] for _, _, _, sums, _ in kept_sums]
        + [sums[0:2] for _, _, _, sums, _ in kept_sums]
        + [sums[2:3] for _, _, _, sums, _ in kept_sums]
    )
    spread = jnp.concatenate(
        [restore(jnp.concatenate(featured), to_feature.astype(F32)), restore(headed, to_head.astype(F32))]
    )
    spread = spread.reshape(-1, fsdp * tp, fine).transpose(1, 0, 2)
    up_all = jnp.stack([item[4] for item in kept_sums]).reshape(layers, fsdp * tp, parts * fine)
    up_all = jnp.einsum("or,lok->rlk", to_hidden.astype(F32), up_all, precision=HIGHEST)
    flat = jnp.concatenate([spread.reshape(fsdp * tp, -1), up_all.reshape(fsdp * tp, -1)], axis=1)
    for bit in reversed(range(bits_of(fsdp))):
        middle = flat.shape[0] // 2
        flat = flat[:middle] + flip(flat[middle:], bit)
    for bit in reversed(range(bits_of(tp))):
        middle = flat.shape[0] // 2
        flat = flat[:middle] + flip(flat[middle:], bit, "tp")
    flat = flat.reshape(-1)
    sizes = [grid, grid, 2 * layers, 2 * layers, layers, layers, 3 * layers, 2 * layers, layers, layers * parts]
    shapes = [
        (grid, fine), (grid, fine), (layers, 2, fine), (layers, 2, fine), (layers, fine), (layers, fine),
        (layers, 3, fine), (layers, 2, fine), (layers, fine), (layers, parts * fine),
    ]
    found = []
    start = 0
    for lines, shape in zip(sizes, shapes):
        found.append(flat[start : start + lines * fine].reshape(shape))
        start += lines * fine
    rows_g, cols_g, gain_g, shift_g, out_g, last_g, proj_g, head_gain_g, head_shift_g, up_g = found
    return (
        activations, token_grad, rows_g, cols_g, gain_g, shift_g, proj_g, head_gain_g, head_shift_g, out_g, up_g, last_g,
        jnp.stack(w_qkv_grad), jnp.stack(w_out_grad), jnp.stack(w_fc1_grad), jnp.stack(w_fc2_grad),
    )


def solution(mesh):
    both = ("fsdp", "tp")
    in_specs = (
        P(both, None), P("fsdp", None), P(None, both), P(None, both), P(None, both), P(None, None, both),
        P(None, None, both), P(None, None, both), P(None, None, both), P(None, both), P(None, both), P(None, both),
        P(None, both), P(None, "fsdp", None, "tp"), P(None, "tp", "fsdp"), P(None, "fsdp", "tp"), P(None, "tp", "fsdp"),
        P(both, None),
    )
    out_specs = (
        P(both, None), P(both, None), P(None, both), P(None, both), P(None, None, both), P(None, None, both),
        P(None, None, both), P(None, None, both), P(None, both), P(None, both), P(None, both), P(None, both),
        P(None, "fsdp", None, "tp"), P(None, "tp", "fsdp"), P(None, "fsdp", "tp"), P(None, "tp", "fsdp"),
    )
    return jax.shard_map(body, mesh=mesh, in_specs=in_specs, out_specs=out_specs, check_vma=False)
```

time: 884 us -> 690 us (0.78)
  waiting for transfers between devices: 378 us -> 166 us
  Pallas kernels: 185 us -> 343 us
  local copies, waits for them, and re-layouts: 136 us -> 59.8 us
  other arithmetic: 67.9 us -> 37 us
  starting transfers between devices: 84.6 us -> 55.8 us
    pallas_call x12 -> x15, Pallas kernels: 185 us -> 343 us  [the longest x2 114 us: attend(): pl.pallas_call(functools.partial(attend_kernel, rows_of=rows_of, layer=la...]
    ppermute x34 -> x22, waiting for transfers between devices: 258 us -> 113 us  [flip(): return lax.ppermute(array, axis, [(i, i ^ 1 << bit) for i in range(size)])]
    ppermute x16 -> x8, waiting for transfers between devices: 46 us -> 0.02 us  [hop(): lax.ppermute(array, 'tp', [(i, i + distance) for i in range(size) if 0 <=...]
    slice x38 -> x26, local copies, waits for them, and re-layouts: 36.1 us -> 5.35 us  [the longest x2 2.98 us: body(): featured.append(jnp.stack([sums[0] for _, _, sums, _, _ in kept_sums]))]
    another operation x8 -> x6, other arithmetic: 22.2 us -> 0.06 us  [attn_unshard(): return (jnp.stack([q, k, v], axis=1), o.T)]
    ppermute x24 -> x12, waiting for transfers between devices: 74.5 us -> 52.8 us  [ring(): return lax.ppermute(array, 'tp', [(i, (i + 1) % size) for i in range(size)])]
    unnamed x199 -> x121, local copies, waits for them, and re-layouts: 24.5 us -> 6.4 us
    ppermute x24 -> x12, starting transfers between devices: 17.7 us -> 3.82 us  [ring(): return lax.ppermute(array, 'tp', [(i, (i + 1) % size) for i in range(size)])]
  transfers between devices with their start and end apart: 74 -> 42, of which waited for: 35 -> 23; matrix products, arithmetic and copies ran while one was open for 23% -> 13% of each run, Pallas kernels for 16% -> 15%
where the time goes in v2:
time: 690 us; the launch traced here: 682 us
  Pallas kernels  343 us (50%)
  waiting for transfers between devices  166 us (24%)
  local copies, waits for them, and re-layouts  59.8 us (9%)
  starting transfers between devices  55.8 us (8%)
  other arithmetic  37 us (5%)
  matrix products  18 us (3%)
    pallas_call x2, Pallas kernels, attend(): pl.pallas_call(functools.partial(attend_kernel, rows_of=rows_of, layer=la...  114 us
    ppermute x22, waiting for transfers between devices, flip(): return lax.ppermute(array, axis, [(i, i ^ 1 << bit) for i in range(size)])  113 us
    ppermute x12, waiting for transfers between devices, ring(): return lax.ppermute(array, 'tp', [(i, (i + 1) % size) for i in range(size)])  52.8 us
    pallas_call x2, Pallas kernels, mlp(): pl.pallas_call(functools.partial(mlp_kernel, rows_of=rows_of, layer=layer...  47.4 us
    pallas_call x2, Pallas kernels, attend_back(): pl.pallas_call(functools.partial(attend_back_kernel, rows_of=rows_of, lay...  47.4 us
    pallas_call x2, Pallas kernels, halo(): pl.pallas_call(halo_kernel, grid=(1,), in_specs=[whole((rows, width))], o...  46.4 us
    pallas_call x1, Pallas kernels, gather_alone(): pl.pallas_call(gather_kernel, grid=(1,), in_specs=operands, out_specs=[AN...  35.2 us
    ppermute x22, starting transfers between devices, flip(): return lax.ppermute(array, axis, [(i, i ^ 1 << bit) for i in range(size)])  27.7 us
  transfers between devices with their start and end apart: 42, of which 23 were waited for; matrix products, arithmetic and copies ran while one was open for 13% of the time, Pallas kernels for 15%

profile of v2, /device:TPU:0, one launch (start us, length us, event | category | flops | bytes accessed | tf_op | source)
XLA Modules:
  0.0 681.6 jit_solution(7485351599231461682)
XLA Ops:
  8.0 3.1 collective-permute-start
  15.9 2.2 fusion.22.g_ref
  19.0 2.7 collective-permute-start.1
  23.4 35.2 %gather_block.1 = (bf16[384,3072]{1,0:T(8,128)(2,1)}, bf16[384,3072]{1,0:T(8,128)(2,1)}) custom-call(bf16[96,768]{1,0:T(8,128)(2,1)} %concatenate.102.shard_ref), custom_call_target="tpu_custom_call" | custom-call | tf_op jit(solution)/shard_map/gather_block/pallas_call | solution.py:224
  62.6 3.8 collective-permute-done.3
  67.5 3.9 collective-permute-done.4
  76.9 21.0 %halo.2.refs_0_.a_ref = bf16[1024,768]{1,0:T(8,128)(2,1)} custom-call(bf16[256,768]{1,0:T(8,128)(2,1)} %add_convert_fusion.4.a_ref), custom_call_target="tpu_custom_call" | custom-call | tf_op jit(solution)/shard_map/halo/pallas_call | solution.py:288
  100.7 55.3 %attend.2 = (bf16[256,1024]{1,0:T(8,128)(2,1)}, bf16[1024,1536]{1,0:T(8,128)(2,1)}, bf16[256,1024]{1,0:T(8,128)(2,1)}, bf16[1024,1024]{1,0:T(8,128)(2,1)}, bf16[...) custom-call(bf16[1024,768]{1,0:T(8,128)(2,1)} %halo.2.refs_0_.a_ref,, ...), custom_call_target="tpu_custom_call" | custom-call | flops 8858370048 | bytes 15728640 | tf_op jit(solution)/shard_map/attend/pallas_call | solution.py:440
  156.0 37.5 %mlp.2 = (bf16[256,3072]{1,0:T(8,128)(2,1)}, bf16[256,3072]{1,0:T(8,128)(2,1)}, f32[256,768]{1,0:T(8,128)}, bf16[256,768]{1,0:T(8,128)(2,1)}, bf16[384,3072]{1,0:T(8,128)(2,1)}, /*index=5*/bf16[384,3072]{1,0:T(8,128)(2,1)}) custom-call(bf16[256,768]{1,0:T(8,128)(2,1)} %get-tuple-element.85.refs_0_.m_ref, f32[256,768]{1,0:T(8,128)} %get-tuple-element.86.refs_1_.mid_ref, ...), custom_call_target="tpu_custom_call" | custom-call | flops 2415919104 | bytes 9437184 | tf_op jit(solution)/shard_map/mlp/pallas_call | solution.py:513
  193.4 25.3 %halo.3.refs_0_.a_ref = bf16[1024,768]{1,0:T(8,128)(2,1)} custom-call(bf16[256,768]{1,0:T(8,128)(2,1)} %get-tuple-element.89.a_ref), custom_call_target="tpu_custom_call" | custom-call | tf_op jit(solution)/shard_map/halo/pallas_call | solution.py:288
  219.6 58.3 %attend.3 = (bf16[256,1024]{1,0:T(8,128)(2,1)}, bf16[1024,1536]{1,0:T(8,128)(2,1)}, bf16[256,1024]{1,0:T(8,128)(2,1)}, bf16[1024,1024]{1,0:T(8,128)(2,1)}, bf16[...) custom-call(bf16[1024,768]{1,0:T(8,128)(2,1)} %halo.3.refs_0_.a_ref,, ...), custom_call_target="tpu_custom_call" | custom-call | flops 8858370048 | bytes 15728640 | tf_op jit(solution)/shard_map/attend/pallas_call | solution.py:440
  277.9 10.0 %mlp.3 = (bf16[256,3072]{1,0:T(8,128)(2,1)}, bf16[256,3072]{1,0:T(8,128)(2,1)}, f32[256,768]{1,0:T(8,128)}, bf16[256,768]{1,0:T(8,128)(2,1)}) custom-call(bf16[256,768]{1,0:T(8,128)(2,1)} %get-tuple-element.93.refs_0_.m_ref, f32[256,768]{1,0:T(8,128)} %get-tuple-element.94.refs_1_.mid_ref, ...), custom_call_target="tpu_custom_call" | custom-call | flops 2415919104 | bytes 9437184 | tf_op jit(solution)/shard_map/mlp/pallas_call | solution.py:513
  287.8 10.4 %mlp_back.2 = (bf16[256,768]{1,0:T(8,128)(2,1)}, bf16[256,3072]{1,0:T(8,128)(2,1)}, f32[1,3072]{1,0:T(1,128)}, f32[256,768]{1,0:T(8,128)}, bf16[256,768]{1,0:T(8,128)(2,1)}, /*index=5*/f32[8,768]{1,0:T(8,128)}) custom-call(f32[256,768]{1,0:T(8,128)} %fusion.22.g_ref, bf16[384,6144]{1,0:T(8,128)(2,1)} %get-tuple-element.95.refs_2_.refs_4_.down_near_ref.up_near_ref, ...), custom_call_target="tpu_custom_call" | custom-call | flops 2415919104 | bytes 9437184 | tf_op jit(solution)/shard_map/mlp_back/pallas_call | solution.py:572
  298.3 23.6 %attend_back.2 = (bf16[256,1024]{1,0:T(8,128)(2,1)}, bf16[1024,1536]{1,0:T(8,128)(2,1)}, f32[256,768]{1,0:T(8,128)}, bf16[384,768]{1,0:T(8,128)(2,1)}, bf16[384,768]{1,0:T(8,128)(2,1)}, /*index=5*/f32[8,1536]{1,0:T(8,128)}) custom-call(bf16[256,768]{1,0:T(8,128)(2,1)} %get-tuple-element.100.gr_ref, bf16[256,1024]{1,0:T(8,128)(2,1)} %get-tuple-element.101.q_ref, ...), custom_call_target="tpu_custom_call" | custom-call | flops 10468982784 | bytes 15728640 | tf_op jit(solution)/shard_map/attend_back/pallas_call | solution.py:661
  329.2 2.8 collective-permute-start.5
  333.4 4.7 collective-permute-start.7
  340.0 7.3 %mlp_weight_grads.3 = (bf16[384,6144]{1,0:T(8,128)(2,1)}, bf16[384,6144]{1,0:T(8,128)(2,1)}) custom-call(bf16[256,768]{1,0:T(8,128)(2,1)} %get-tuple-element.93.refs_0_.m_ref, bf16[256,3072]{1,0:T(8,128)(2,1)} %get-tuple-element.145.gh_ref, bf16[256,768]{1,0:T(8,128)(2,1)} %get-tuple-element.146.gz_ref, bf16[256,3072]{1,0:T(8,128)(2,1)} %get-tuple-element.147.act_ref), custom_call_target="tpu_custom_call" | custom-call | flops 2415919104 | bytes 9437184 | tf_op jit(solution)/shard_map/mlp_weight_grads/pallas_call | solution.py:749
  349.4 2.0 reduce.49
  353.8 2.2 multiply_reduce_fusion
  357.2 10.4 %mlp_back.3 = (bf16[256,768]{1,0:T(8,128)(2,1)}, bf16[256,3072]{1,0:T(8,128)(2,1)}, f32[1,3072]{1,0:T(1,128)}, f32[256,768]{1,0:T(8,128)}, bf16[256,768]{1,0:T(8,128)(2,1)}, /*index=5*/f32[8,768]{1,0:T(8,128)}) custom-call(f32[256,768]{1,0:T(8,128)} %multiply_add_fusion.1.g_ref, ...), custom_call_target="tpu_custom_call" | custom-call | flops 2415919104 | bytes 9437184 | tf_op jit(solution)/shard_map/mlp_back/pallas_call | solution.py:572
  367.6 23.7 %attend_back.3 = (bf16[256,1024]{1,0:T(8,128)(2,1)}, bf16[1024,1536]{1,0:T(8,128)(2,1)}, f32[256,768]{1,0:T(8,128)}, bf16[384,768]{1,0:T(8,128)(2,1)}, bf16[384,768]{1,0:T(8,128)(2,1)}, /*index=5*/f32[8,1536]{1,0:T(8,128)}) custom-call(bf16[256,768]{1,0:T(8,128)(2,1)} %get-tuple-element.113.gr_ref, bf16[256,1024]{1,0:T(8,128)(2,1)} %get-tuple-element.114.q_ref, ...), custom_call_target="tpu_custom_call" | custom-call | flops 10468982784 | bytes 15728640 | tf_op jit(solution)/shard_map/attend_back/pallas_call | solution.py:661
  398.9 4.6 collective-permute-start.9
  403.4 6.8 %collective-permute-start.11 = (bf16[128,768]{1,0:T(8,128)(2,1)}, bf16[128,768]{1,0:T(8,128)(2,1)}, u32[]{:S(2)}, u32[]{:S(2)}) collective-permute-start(bf16[128,768]{1,0:T(8,128)(2,1)} %slice.435), channel_id=1, source_target_pairs={{0,2},{1,3},{4,6},{5,7},{8,10},{9,11},{12,14},{13,15},{16,18},{17,... | collective-permute-start | bytes 589832 | tf_op jit(solution)/shard_map/ppermute | solution.py:775
  414.3 3.7 fusion
  436.6 8.7 %attn_weight_grads.3 = (bf16[384,3072]{1,0:T(8,128)(2,1)}, bf16[384,3072]{1,0:T(8,128)(2,1)}) custom-call(bf16[1024,768]{1,0:T(8,128)(2,1)} %halo.3.refs_0_.a_ref, bf16[256,1024]{1,0:T(8,128)(2,1)} %get-tuple-element.135.gq_ref, bf16[1024,1536]{1,0:T(8,128)(2,1)} %get-tuple-element.136.gkv_ref, bf16[256,768]{1,0:T(8,128)(2,1)} %get-tuple-element.100.gr_ref, ...), custom_call_target="tpu_custom_call" | custom-call | flops 3019898880 | bytes 4718592 | tf_op jit(solution)/shard_map/attn_weight_grads/pallas_call | solution.py:711
  445.4 2.1 collective-permute-start.14
  447.4 2.2 fusion.18
  451.5 7.2 %mlp_weight_grads.2 = (bf16[384,6144]{1,0:T(8,128)(2,1)}, bf16[384,6144]{1,0:T(8,128)(2,1)}) custom-call(bf16[256,768]{1,0:T(8,128)(2,1)} %get-tuple-element.85.refs_0_.m_ref, bf16[256,3072]{1,0:T(8,128)(2,1)} %get-tuple-element.140.gh_ref, bf16[256,768]{1,0:T(8,128)(2,1)} %get-tuple-element.141.gz_ref, bf16[256,3072]{1,0:T(8,128)(2,1)} %get-tuple-element.142.act_ref), custom_call_target="tpu_custom_call" | custom-call | flops 2415919104 | bytes 9437184 | tf_op jit(solution)/shard_map/mlp_weight_grads/pallas_call | solution.py:749
  459.2 4.3 collective-permute-start.16
  463.5 8.7 %attn_weight_grads.2 = (bf16[384,3072]{1,0:T(8,128)(2,1)}, bf16[384,3072]{1,0:T(8,128)(2,1)}) custom-call(bf16[1024,768]{1,0:T(8,128)(2,1)} %halo.2.refs_0_.a_ref, bf16[256,1024]{1,0:T(8,128)(2,1)} %get-tuple-element.130.gq_ref, bf16[1024,1536]{1,0:T(8,128)(2,1)} %get-tuple-element.131.gkv_ref, bf16[256,768]{1,0:T(8,128)(2,1)} %get-tuple-element.113.gr_ref, ...), custom_call_target="tpu_custom_call" | custom-call | flops 3019898880 | bytes 4718592 | tf_op jit(solution)/shard_map/attn_weight_grads/pallas_call | solution.py:711
  472.4 2.2 fusion.16
  476.3 2.5 add_convert_fusion.2
  483.3 23.0 %collective-permute-done.25 = bf16[2,96,3072]{2,1,0:T(8,128)(2,1)S(1)} collective-permute-done((bf16[2,96,3072]{2,1,0:T(8,128)(2,1)S(1)}, bf16[2,96,3072]{2,1,0:T(8,128)(2,1)S(1)}, u32[]{:S(2)}, u32[]{:S(2)}) %collective-permute-start.25) | collective-permute-done | bytes 1179680 | tf_op jit(solution)/shard_map/ppermute | solution.py:765
  510.2 11.3 %collective-permute-done.26 = bf16[96,3072]{1,0:T(8,128)(2,1)S(1)} collective-permute-done((bf16[96,3072]{1,0:T(8,128)(2,1)S(1)}, bf16[96,3072]{1,0:T(8,128)(2,1)S(1)}, u32[]{:S(2)}, u32[]{:S(2)}) %collective-permute-start.26) | collective-permute-done | bytes 589856 | tf_op jit(solution)/shard_map/ppermute | solution.py:765
  525.0 3.7 collective-permute-done.27
  537.2 5.8 collective-permute-done.29
  544.7 5.6 add_convert_fusion
  555.8 3.3 collective-permute-done.23
  561.1 6.1 add_convert_fusion.1
  569.6 33.9 %collective-permute-done.37 = bf16[2,96,6144]{2,1,0:T(8,128)(2,1)S(1)} collective-permute-done((bf16[2,96,6144]{2,1,0:T(8,128)(2,1)}, bf16[2,96,6144]{2,1,0:T(8,128)(2,1)S(1)}, u32[]{:S(2)}, u32[]{:S(2)}) %collective-permute-start.37) | collective-permute-done | bytes 2359328 | tf_op jit(solution)/shard_map/ppermute | solution.py:765
  606.2 15.9 %collective-permute-done.31 = bf16[2,96,6144]{2,1,0:T(8,128)(2,1)S(1)} collective-permute-done((bf16[2,96,6144]{2,1,0:T(8,128)(2,1)S(1)}, bf16[2,96,6144]{2,1,0:T(8,128)(2,1)S(1)}, u32[]{:S(2)}, u32[]{:S(2)}) %collective-permute-start.31) | collective-permute-done | bytes 2359328 | tf_op jit(solution)/shard_map/ppermute | solution.py:765
  624.7 15.4 %collective-permute-done.38 = bf16[96,6144]{1,0:T(8,128)(2,1)S(1)} collective-permute-done((bf16[96,6144]{1,0:T(8,128)(2,1)S(1)}, bf16[96,6144]{1,0:T(8,128)(2,1)S(1)}, u32[]{:S(2)}, u32[]{:S(2)}) %collective-permute-start.38) | collective-permute-done | bytes 1179680 | tf_op jit(solution)/shard_map/ppermute | solution.py:765
  641.8 10.3 %collective-permute-done.39 = bf16[96,1536]{1,0:T(8,128)(2,1)S(1)} collective-permute-done((bf16[96,1536]{1,0:T(8,128)(2,1)S(1)}, bf16[96,1536]{1,0:T(8,128)(2,1)S(1)}, u32[]{:S(2)}, u32[]{:S(2)}) %collective-permute-start.39) | collective-permute-done | bytes 294944 | tf_op jit(solution)/shard_map/ppermute | solution.py:770
  652.3 6.2 collective-permute-done.33
  658.6 6.2 collective-permute-done.40
  664.9 5.8 collective-permute-done.34
  670.8 3.0 collective-permute-done.41
  674.0 5.3 collective-permute-done.35
  (383 shorter events, 119.8 us)
Async XLA Ops:
  8.0 11.0 %collective-permute-start = (bf16[1,3840]{1,0:T(2,128)(2,1)S(1)}, bf16[1,3840]{1,0:T(2,128)(2,1)S(1)}, u32[]{:S(2)}, u32[]{:S(2)}) collective-permute-start(bf16[1,3840]{1,0:T(2,128)(2,1)S(1)} %reshape.455), channel_id=1, source_target_pairs={{0,1},{1,0},{2,3},{3,2},{4,5},{5,4},{6,7},{7,6},{8,9},{9,8},{10,11... | collective-permute-start | bytes 23048 | tf_op jit(solution)/shard_map/ppermute | solution.py:765
  11.1 88.1 %copy-start.44 = (s32[1536]{0:T(1024)}, s32[1536]{0:T(1024)S(1)}, u32[]{:S(2)}) copy-start(s32[1536]{0:T(1024)S(1)} %fusion.60) | copy-start | bytes 18436
  11.2 63.2 %copy-start.29 = (s32[768]{0:T(1024)}, s32[768]{0:T(1024)S(1)}, u32[]{:S(2)}) copy-start(s32[768]{0:T(1024)S(1)} %get-tuple-element.321) | copy-start | bytes 9220
  11.2 88.0 %copy-start.48 = (s32[768]{0:T(1024)}, s32[768]{0:T(1024)S(1)}, u32[]{:S(2)}) copy-start(s32[768]{0:T(1024)S(1)} %get-tuple-element.322) | copy-start | bytes 9220
  11.9 62.1 %copy-start.40 = (s32[1,256]{1,0:T(1,128)}, s32[1,256]{1,0:T(1,128)S(1)}, u32[]{:S(2)}) copy-start(s32[1,256]{1,0:T(1,128)S(1)} %get-tuple-element.315) | copy-start | bytes 3076
  19.0 79.2 %copy-start.46 = (s32[32]{0:T(128)}, s32[32]{0:T(128)S(1)}, u32[]{:S(2)}) copy-start(s32[32]{0:T(128)S(1)} %get-tuple-element.323) | copy-start | bytes 388
  19.0 79.2 %copy-start.47 = (s32[32]{0:T(128)}, s32[32]{0:T(128)S(1)}, u32[]{:S(2)}) copy-start(s32[32]{0:T(128)S(1)} %get-tuple-element.324) | copy-start | bytes 388
  19.0 41.6 %collective-permute-start.1 = (bf16[2,3840]{1,0:T(2,128)(2,1)S(1)}, bf16[2,3840]{1,0:T(2,128)(2,1)S(1)}, u32[]{:S(2)}, u32[]{:S(2)}) collective-permute-start(bf16[2,3840]{1,0:T(2,128)(2,1)S(1)} %pad_maximum_fusion.10), channel_id=1, source_target_pairs={{0,2},{1,3},{2,0},{3,1},{4,6},{5,7},{6,4},{7,5},{8,10},{9,11},{10,... | collective-permute-start | bytes 46088 | tf_op jit(solution)/shard_map/ppermute | solution.py:765
  60.7 1.3 collective-permute-start.2
  62.1 4.3 collective-permute-start.3
  66.5 4.9 collective-permute-start.4
  329.2 24.5 %collective-permute-start.5 = (bf16[256,768]{1,0:T(8,128)(2,1)}, bf16[256,768]{1,0:T(8,128)(2,1)S(1)}, u32[]{:S(2)}, u32[]{:S(2)}) collective-permute-start(bf16[256,768]{1,0:T(8,128)(2,1)} %slice.428), channel_id=1, source_target_pairs={{0,1},{1,2},{2,3},{4,5},{5,6},{6,7},{8,9},{9,10},{10,11},{12,13},{... | collective-permute-start | bytes 1179656 | tf_op jit(solution)/shard_map/ppermute | solution.py:775
  332.1 21.7 %collective-permute-start.6 = (bf16[256,768]{1,0:T(8,128)(2,1)S(1)}, bf16[256,768]{1,0:T(8,128)(2,1)S(1)}, u32[]{:S(2)}, u32[]{:S(2)}) collective-permute-start(bf16[256,768]{1,0:T(8,128)(2,1)S(1)} %slice.429), channel_id=1, source_target_pairs={{1,0},{2,1},{3,2},{5,4},{6,5},{7,6},{9,8},{10,9},{11,10},{13,12},{... | collective-permute-start | bytes 1179656 | tf_op jit(solution)/shard_map/ppermute | solution.py:775
  333.4 20.3 %collective-permute-start.7 = (bf16[128,768]{1,0:T(8,128)(2,1)}, bf16[128,768]{1,0:T(8,128)(2,1)}, u32[]{:S(2)}, u32[]{:S(2)}) collective-permute-start(bf16[128,768]{1,0:T(8,128)(2,1)} %slice.430), channel_id=1, source_target_pairs={{0,2},{1,3},{4,6},{5,7},{8,10},{9,11},{12,14},{13,15},{16,18},{17,... | collective-permute-start | bytes 589832 | tf_op jit(solution)/shard_map/ppermute | solution.py:775
  338.1 15.7 %collective-permute-start.8 = (bf16[128,768]{1,0:T(8,128)(2,1)}, bf16[128,768]{1,0:T(8,128)(2,1)}, u32[]{:S(2)}, u32[]{:S(2)}) collective-permute-start(bf16[128,768]{1,0:T(8,128)(2,1)} %slice.431), channel_id=1, source_target_pairs={{2,0},{3,1},{6,4},{7,5},{10,8},{11,9},{14,12},{15,13},{18,16},{19,... | collective-permute-start | bytes 589832 | tf_op jit(solution)/shard_map/ppermute | solution.py:775
  347.4 197.3 %collective-permute-start.36 = (bf16[384,6144]{1,0:T(8,128)(2,1)}, bf16[384,6144]{1,0:T(8,128)(2,1)}, u32[]{:S(2)}, u32[]{:S(2)}) collective-permute-start(bf16[384,6144]{1,0:T(8,128)(2,1)} %get-tuple-element.149), channel_id=1, source_target_pairs={{0,4},{4,0},{8,12},{12,8},{16,20},{20,16},{24,28},{28,24},{1,5},{5... | collective-permute-start | bytes 14155784 | tf_op jit(solution)/shard_map/ppermute | solution.py:765
  397.6 28.5 %collective-permute-start.10 = (bf16[256,768]{1,0:T(8,128)(2,1)}, bf16[256,768]{1,0:T(8,128)(2,1)S(1)}, u32[]{:S(2)}, u32[]{:S(2)}) collective-permute-start(bf16[256,768]{1,0:T(8,128)(2,1)} %slice.434), channel_id=1, source_target_pairs={{1,0},{2,1},{3,2},{5,4},{6,5},{7,6},{9,8},{10,9},{11,10},{13,12},{... | collective-permute-start | bytes 1179656 | tf_op jit(solution)/shard_map/ppermute | solution.py:775
  398.9 27.2 %collective-permute-start.9 = (bf16[256,768]{1,0:T(8,128)(2,1)S(1)}, bf16[256,768]{1,0:T(8,128)(2,1)S(1)}, u32[]{:S(2)}, u32[]{:S(2)}) collective-permute-start(bf16[256,768]{1,0:T(8,128)(2,1)S(1)} %slice.433), channel_id=1, source_target_pairs={{0,1},{1,2},{2,3},{4,5},{5,6},{6,7},{8,9},{9,10},{10,11},{12,13},{... | collective-permute-start | bytes 1179656 | tf_op jit(solution)/shard_map/ppermute | solution.py:775
  403.4 22.6 %collective-permute-start.11 = (bf16[128,768]{1,0:T(8,128)(2,1)}, bf16[128,768]{1,0:T(8,128)(2,1)}, u32[]{:S(2)}, u32[]{:S(2)}) collective-permute-start(bf16[128,768]{1,0:T(8,128)(2,1)} %slice.435), channel_id=1, source_target_pairs={{0,2},{1,3},{4,6},{5,7},{8,10},{9,11},{12,14},{13,15},{16,18},{17,... | collective-permute-start | bytes 589832 | tf_op jit(solution)/shard_map/ppermute | solution.py:775
  410.3 15.8 %collective-permute-start.12 = (bf16[128,768]{1,0:T(8,128)(2,1)}, bf16[128,768]{1,0:T(8,128)(2,1)}, u32[]{:S(2)}, u32[]{:S(2)}) collective-permute-start(bf16[128,768]{1,0:T(8,128)(2,1)} %slice.436), channel_id=1, source_target_pairs={{2,0},{3,1},{6,4},{7,5},{10,8},{11,9},{14,12},{15,13},{18,16},{19,... | collective-permute-start | bytes 589832 | tf_op jit(solution)/shard_map/ppermute | solution.py:775
  436.5 8.7 %collective-permute-start.13 = (f32[16,3840]{1,0:T(8,128)S(1)}, f32[16,3840]{1,0:T(8,128)S(1)}, u32[]{:S(2)}, u32[]{:S(2)}) collective-permute-start(f32[16,3840]{1,0:T(8,128)S(1)} %pad_maximum_fusion.6), channel_id=1, source_target_pairs={{0,16},{4,20},{8,24},{12,28},{16,0},{20,4},{24,8},{28,12},{1,17},{... | collective-permute-start | bytes 737288 | tf_op jit(solution)/shard_map/ppermute | solution.py:765
  445.3 31.1 %collective-permute-start.24 = (bf16[384,3072]{1,0:T(8,128)(2,1)}, bf16[384,3072]{1,0:T(8,128)(2,1)}, u32[]{:S(2)}, u32[]{:S(2)}) collective-permute-start(bf16[384,3072]{1,0:T(8,128)(2,1)} %get-tuple-element.139), channel_id=1, source_target_pairs={{0,4},{4,0},{8,12},{12,8},{16,20},{20,16},{24,28},{28,24},{1,5},{5... | collective-permute-start | bytes 7077896 | tf_op jit(solution)/shard_map/ppermute | solution.py:765
  445.4 6.0 collective-permute-start.14
  451.4 7.8 %collective-permute-start.15 = (f32[4,3840]{1,0:T(4,128)S(1)}, f32[4,3840]{1,0:T(4,128)S(1)}, u32[]{:S(2)}, u32[]{:S(2)}) collective-permute-start(f32[4,3840]{1,0:T(4,128)S(1)} %slice.544), channel_id=1, source_target_pairs={{0,4},{4,0},{8,12},{12,8},{16,20},{20,16},{24,28},{28,24},{1,5},{5... | collective-permute-start | bytes 184328 | tf_op jit(solution)/shard_map/ppermute | solution.py:765
  458.7 102.4 %collective-permute-start.30 = (bf16[384,6144]{1,0:T(8,128)(2,1)}, bf16[384,6144]{1,0:T(8,128)(2,1)}, u32[]{:S(2)}, u32[]{:S(2)}) collective-permute-start(bf16[384,6144]{1,0:T(8,128)(2,1)} %get-tuple-element.144), channel_id=1, source_target_pairs={{0,4},{4,0},{8,12},{12,8},{16,20},{20,16},{24,28},{28,24},{1,5},{5... | collective-permute-start | bytes 14155784 | tf_op jit(solution)/shard_map/ppermute | solution.py:765
  459.2 13.0 %collective-permute-start.16 = (f32[2,3840]{1,0:T(2,128)S(1)}, f32[2,3840]{1,0:T(2,128)S(1)}, u32[]{:S(2)}, u32[]{:S(2)}) collective-permute-start(f32[2,3840]{1,0:T(2,128)S(1)} %slice.546), channel_id=1, source_target_pairs={{0,2},{1,3},{2,0},{3,1},{4,6},{5,7},{6,4},{7,5},{8,10},{9,11},{10,... | collective-permute-start | bytes 92168 | tf_op jit(solution)/shard_map/ppermute | solution.py:765
  472.2 8.7 %collective-permute-start.18 = (bf16[384,3072]{1,0:T(8,128)(2,1)}, bf16[384,3072]{1,0:T(8,128)(2,1)S(1)}, u32[]{:S(2)}, u32[]{:S(2)}) collective-permute-start(bf16[384,3072]{1,0:T(8,128)(2,1)} %get-tuple-element.134), channel_id=1, source_target_pairs={{0,4},{4,0},{8,12},{12,8},{16,20},{20,16},{24,28},{28,24},{1,5},{5... | collective-permute-start | bytes 7077896 | tf_op jit(solution)/shard_map/ppermute | solution.py:765
  472.3 3.8 collective-permute-start.17
  479.1 27.3 %collective-permute-start.25 = (bf16[2,96,3072]{2,1,0:T(8,128)(2,1)S(1)}, bf16[2,96,3072]{2,1,0:T(8,128)(2,1)S(1)}, u32[]{:S(2)}, u32[]{:S(2)}) collective-permute-start(bf16[2,96,3072]{2,1,0:T(8,128)(2,1)S(1)} %bitcast.188), channel_id=1, source_target_pairs={{0,16},{4,20},{8,24},{12,28},{16,0},{20,4},{24,8},{28,12},{1,17},{... | collective-permute-start | bytes 3538952 | tf_op jit(solution)/shard_map/ppermute | solution.py:765
  481.9 27.9 %collective-permute-start.19 = (bf16[2,96,3072]{2,1,0:T(8,128)(2,1)S(1)}, bf16[2,96,3072]{2,1,0:T(8,128)(2,1)S(1)}, u32[]{:S(2)}, u32[]{:S(2)}) collective-permute-start(bf16[2,96,3072]{2,1,0:T(8,128)(2,1)S(1)} %slice_bitcast_fusion.6), channel_id=1, source_target_pairs={{0,8},{4,12},{8,0},{12,4},{16,24},{20,28},{24,16},{28,20},{1,9},{5... | collective-permute-start | bytes 3538952 | tf_op jit(solution)/shard_map/ppermute | solution.py:765
  506.8 14.7 %collective-permute-start.26 = (bf16[96,3072]{1,0:T(8,128)(2,1)S(1)}, bf16[96,3072]{1,0:T(8,128)(2,1)S(1)}, u32[]{:S(2)}, u32[]{:S(2)}) collective-permute-start(bf16[96,3072]{1,0:T(8,128)(2,1)S(1)} %slice_bitcast_fusion.8), channel_id=1, source_target_pairs={{0,8},{4,12},{8,0},{12,4},{16,24},{20,28},{24,16},{28,20},{1,9},{5... | collective-permute-start | bytes 1769480 | tf_op jit(solution)/shard_map/ppermute | solution.py:765
  521.7 7.0 %collective-permute-start.27 = (bf16[96,768]{1,0:T(8,128)(2,1)S(1)}, bf16[96,768]{1,0:T(8,128)(2,1)S(1)}, u32[]{:S(2)}, u32[]{:S(2)}) collective-permute-start(bf16[96,768]{1,0:T(8,128)(2,1)S(1)} %split.68), channel_id=1, source_target_pairs={{0,1},{1,2},{2,3},{3,0},{4,5},{5,6},{6,7},{7,4},{8,9},{9,10},{10,1... | collective-permute-start | bytes 442376 | tf_op jit(solution)/shard_map/ppermute | solution.py:770
  523.2 13.5 %collective-permute-start.20 = (bf16[96,3072]{1,0:T(8,128)(2,1)S(1)}, bf16[96,3072]{1,0:T(8,128)(2,1)S(1)}, u32[]{:S(2)}, u32[]{:S(2)}) collective-permute-start(bf16[96,3072]{1,0:T(8,128)(2,1)S(1)} %slice_bitcast_fusion.10), channel_id=1, source_target_pairs={{0,16},{4,20},{8,24},{12,28},{16,0},{20,4},{24,8},{28,12},{1,17},{... | collective-permute-start | bytes 1769480 | tf_op jit(solution)/shard_map/ppermute | solution.py:765
  528.7 7.0 %collective-permute-start.28 = (bf16[96,768]{1,0:T(8,128)(2,1)S(1)}, bf16[96,768]{1,0:T(8,128)(2,1)S(1)}, u32[]{:S(2)}, u32[]{:S(2)}) collective-permute-start(bf16[96,768]{1,0:T(8,128)(2,1)S(1)} %add_convert_fusion.10), channel_id=1, source_target_pairs={{0,1},{1,2},{2,3},{3,0},{4,5},{5,6},{6,7},{7,4},{8,9},{9,10},{10,1... | collective-permute-start | bytes 442376 | tf_op jit(solution)/shard_map/ppermute | solution.py:770
  535.8 7.2 %collective-permute-start.29 = (bf16[96,768]{1,0:T(8,128)(2,1)S(1)}, bf16[96,768]{1,0:T(8,128)(2,1)S(1)}, u32[]{:S(2)}, u32[]{:S(2)}) collective-permute-start(bf16[96,768]{1,0:T(8,128)(2,1)S(1)} %add_convert_fusion.9), channel_id=1, source_target_pairs={{0,1},{1,2},{2,3},{3,0},{4,5},{5,6},{6,7},{7,4},{8,9},{9,10},{10,1... | collective-permute-start | bytes 442376 | tf_op jit(solution)/shard_map/ppermute | solution.py:770
  536.8 7.7 %collective-permute-start.21 = (bf16[96,768]{1,0:T(8,128)(2,1)S(1)}, bf16[96,768]{1,0:T(8,128)(2,1)S(1)}, u32[]{:S(2)}, u32[]{:S(2)}) collective-permute-start(bf16[96,768]{1,0:T(8,128)(2,1)S(1)} %split.64), channel_id=1, source_target_pairs={{0,1},{1,2},{2,3},{3,0},{4,5},{5,6},{6,7},{7,4},{8,9},{9,10},{10,1... | collective-permute-start | bytes 442376 | tf_op jit(solution)/shard_map/ppermute | solution.py:770
  544.6 7.5 %collective-permute-start.22 = (bf16[96,768]{1,0:T(8,128)(2,1)S(1)}, bf16[96,768]{1,0:T(8,128)(2,1)S(1)}, u32[]{:S(2)}, u32[]{:S(2)}) collective-permute-start(bf16[96,768]{1,0:T(8,128)(2,1)S(1)} %add_convert_fusion.12), channel_id=1, source_target_pairs={{0,1},{1,2},{2,3},{3,0},{4,5},{5,6},{6,7},{7,4},{8,9},{9,10},{10,1... | collective-permute-start | bytes 442376 | tf_op jit(solution)/shard_map/ppermute | solution.py:770
  552.1 7.0 %collective-permute-start.23 = (bf16[96,768]{1,0:T(8,128)(2,1)S(1)}, bf16[96,768]{1,0:T(8,128)(2,1)S(1)}, u32[]{:S(2)}, u32[]{:S(2)}) collective-permute-start(bf16[96,768]{1,0:T(8,128)(2,1)S(1)} %add_convert_fusion.11), channel_id=1, source_target_pairs={{0,1},{1,2},{2,3},{3,0},{4,5},{5,6},{6,7},{7,4},{8,9},{9,10},{10,1... | collective-permute-start | bytes 442376 | tf_op jit(solution)/shard_map/ppermute | solution.py:770
  554.1 49.3 %collective-permute-start.37 = (bf16[2,96,6144]{2,1,0:T(8,128)(2,1)}, bf16[2,96,6144]{2,1,0:T(8,128)(2,1)S(1)}, u32[]{:S(2)}, u32[]{:S(2)}) collective-permute-start(bf16[2,96,6144]{2,1,0:T(8,128)(2,1)} %slice_bitcast_fusion), channel_id=1, source_target_pairs={{0,8},{4,12},{8,0},{12,4},{16,24},{20,28},{24,16},{28,20},{1,9},{5... | collective-permute-start | bytes 7077896 | tf_op jit(solution)/shard_map/ppermute | solution.py:765
  567.8 54.3 %collective-permute-start.31 = (bf16[2,96,6144]{2,1,0:T(8,128)(2,1)S(1)}, bf16[2,96,6144]{2,1,0:T(8,128)(2,1)S(1)}, u32[]{:S(2)}, u32[]{:S(2)}) collective-permute-start(bf16[2,96,6144]{2,1,0:T(8,128)(2,1)S(1)} %bitcast.187), channel_id=1, source_target_pairs={{0,16},{4,20},{8,24},{12,28},{16,0},{20,4},{24,8},{28,12},{1,17},{... | collective-permute-start | bytes 7077896 | tf_op jit(solution)/shard_map/ppermute | solution.py:765
  604.4 35.8 %collective-permute-start.38 = (bf16[96,6144]{1,0:T(8,128)(2,1)S(1)}, bf16[96,6144]{1,0:T(8,128)(2,1)S(1)}, u32[]{:S(2)}, u32[]{:S(2)}) collective-permute-start(bf16[96,6144]{1,0:T(8,128)(2,1)S(1)} %slice_bitcast_fusion.2), channel_id=1, source_target_pairs={{0,16},{4,20},{8,24},{12,28},{16,0},{20,4},{24,8},{28,12},{1,17},{... | collective-permute-start | bytes 3538952 | tf_op jit(solution)/shard_map/ppermute | solution.py:765
  622.9 17.6 %collective-permute-start.32 = (bf16[96,6144]{1,0:T(8,128)(2,1)S(1)}, bf16[96,6144]{1,0:T(8,128)(2,1)S(1)}, u32[]{:S(2)}, u32[]{:S(2)}) collective-permute-start(bf16[96,6144]{1,0:T(8,128)(2,1)S(1)} %slice_bitcast_fusion.4), channel_id=1, source_target_pairs={{0,8},{4,12},{8,0},{12,4},{16,24},{20,28},{24,16},{28,20},{1,9},{5... | collective-permute-start | bytes 3538952 | tf_op jit(solution)/shard_map/ppermute | solution.py:765
  640.5 11.7 %collective-permute-start.39 = (bf16[96,1536]{1,0:T(8,128)(2,1)S(1)}, bf16[96,1536]{1,0:T(8,128)(2,1)S(1)}, u32[]{:S(2)}, u32[]{:S(2)}) collective-permute-start(bf16[96,1536]{1,0:T(8,128)(2,1)S(1)} %split.76), channel_id=1, source_target_pairs={{0,1},{1,2},{2,3},{3,0},{4,5},{5,6},{6,7},{7,4},{8,9},{9,10},{10,1... | collective-permute-start | bytes 884744 | tf_op jit(solution)/shard_map/ppermute | solution.py:770
  640.9 17.6 %collective-permute-start.33 = (bf16[96,1536]{1,0:T(8,128)(2,1)S(1)}, bf16[96,1536]{1,0:T(8,128)(2,1)S(1)}, u32[]{:S(2)}, u32[]{:S(2)}) collective-permute-start(bf16[96,1536]{1,0:T(8,128)(2,1)S(1)} %split.72), channel_id=1, source_target_pairs={{0,1},{1,2},{2,3},{3,0},{4,5},{5,6},{6,7},{7,4},{8,9},{9,10},{10,1... | collective-permute-start | bytes 884744 | tf_op jit(solution)/shard_map/ppermute | solution.py:770
  652.2 12.6 %collective-permute-start.40 = (bf16[96,1536]{1,0:T(8,128)(2,1)S(1)}, bf16[96,1536]{1,0:T(8,128)(2,1)S(1)}, u32[]{:S(2)}, u32[]{:S(2)}) collective-permute-start(bf16[96,1536]{1,0:T(8,128)(2,1)S(1)} %add_convert_fusion.6), channel_id=1, source_target_pairs={{0,1},{1,2},{2,3},{3,0},{4,5},{5,6},{6,7},{7,4},{8,9},{9,10},{10,1... | collective-permute-start | bytes 884744 | tf_op jit(solution)/shard_map/ppermute | solution.py:770
  658.5 12.1 %collective-permute-start.34 = (bf16[96,1536]{1,0:T(8,128)(2,1)S(1)}, bf16[96,1536]{1,0:T(8,128)(2,1)S(1)}, u32[]{:S(2)}, u32[]{:S(2)}) collective-permute-start(bf16[96,1536]{1,0:T(8,128)(2,1)S(1)} %add_convert_fusion.8), channel_id=1, source_target_pairs={{0,1},{1,2},{2,3},{3,0},{4,5},{5,6},{6,7},{7,4},{8,9},{9,10},{10,1... | collective-permute-start | bytes 884744 | tf_op jit(solution)/shard_map/ppermute | solution.py:770
  664.9 9.0 %collective-permute-start.41 = (bf16[96,1536]{1,0:T(8,128)(2,1)S(1)}, bf16[96,1536]{1,0:T(8,128)(2,1)S(1)}, u32[]{:S(2)}, u32[]{:S(2)}) collective-permute-start(bf16[96,1536]{1,0:T(8,128)(2,1)S(1)} %add_convert_fusion.5), channel_id=1, source_target_pairs={{0,1},{1,2},{2,3},{3,0},{4,5},{5,6},{6,7},{7,4},{8,9},{9,10},{10,1... | collective-permute-start | bytes 884744 | tf_op jit(solution)/shard_map/ppermute | solution.py:770
  670.8 8.6 %collective-permute-start.35 = (bf16[96,1536]{1,0:T(8,128)(2,1)S(1)}, bf16[96,1536]{1,0:T(8,128)(2,1)S(1)}, u32[]{:S(2)}, u32[]{:S(2)}) collective-permute-start(bf16[96,1536]{1,0:T(8,128)(2,1)S(1)} %add_convert_fusion.7), channel_id=1, source_target_pairs={{0,1},{1,2},{2,3},{3,0},{4,5},{5,6},{6,7},{7,4},{8,9},{9,10},{10,1... | collective-permute-start | bytes 884744 | tf_op jit(solution)/shard_map/ppermute | solution.py:770
  (47 other events, 521.2 us)

commit v3 on v2

--- a/solution.py
+++ b/solution.py
@@ -90,6 +90,26 @@
     return jax.ShapeDtypeStruct(shape, kind)
 
 
+class Neighbours:
+    def __init__(self):
+        fsdp, tp = lax.axis_index("fsdp"), lax.axis_index("tp")
+        self.size = lax.axis_size("tp")
+        self.tp = tp
+        self.x, self.y, self.core = ({"fsdp": jnp.bitwise_xor(fsdp, bit)} for bit in (2, 4, 1))
+        self.right = self.along(1)
+
+    def along(self, distance):
+        return {"tp": lax.rem(self.tp + distance, self.size)}
+
+    def greet(self, all_tp=False):
+        distances = range(1, self.size) if all_tp else [self.size - 1]
+        targets = [self.x, self.y, self.core] + [self.along(distance) for distance in distances]
+        barrier = pltpu.get_barrier_semaphore()
+        for target in targets:
+            pl.semaphore_signal(barrier, inc=1, device_id=target, device_id_type=MESH)
+        pl.semaphore_wait(barrier, len(targets))
+
+
 class Gather:
     KINDS = 7
 
@@ -97,16 +117,7 @@
         self.shard, self.near, self.far, self.send, self.recv, self.local = shard, near, far, send, recv, local
         self.chunk, self.wide = shard.shape
         self.pieces = near.shape[1] // self.wide
-        fsdp, tp = lax.axis_index("fsdp"), lax.axis_index("tp")
-        size = lax.axis_size("tp")
-        self.x, self.y, self.core = ({"fsdp": jnp.bitwise_xor(fsdp, bit)} for bit in (2, 4, 1))
-        self.right, self.left = {"tp": lax.rem(tp + 1, size)}, {"tp": lax.rem(tp + size - 1, size)}
-
-    def greet(self):
-        barrier = pltpu.get_barrier_semaphore()
-        for target in (self.x, self.y, self.core, self.left):
-            pl.semaphore_signal(barrier, inc=1, device_id=target, device_id_type=MESH)
-        pl.semaphore_wait(barrier, 4)
+        self.peers = Neighbours()
 
     def at(self, piece, start, count, half=None):
         first, wide = piece * self.wide, self.wide
@@ -124,23 +135,23 @@
     def copies(self, piece, stage):
         if stage == "z":
             source = self.shard if piece == 0 else self.at(piece, 0, 1)
-            return [self.copy(piece, 0, source, self.at(piece + 1, 0, 1), self.right)]
+            return [self.copy(piece, 0, source, self.at(piece + 1, 0, 1), self.peers.right)]
         if stage == "first":
             half = self.wide // 2
             left = self.shard.at[:, pl.ds(0, half)] if piece == 0 else self.at(piece, 0, 1, 0)
             right = self.shard.at[:, pl.ds(half, half)] if piece == 0 else self.at(piece, 0, 1, 1)
             return [
-                self.copy(piece, 1, left, self.at(piece, 1, 1, 0), self.x),
-                self.copy(piece, 2, right, self.at(piece, 2, 1, 1), self.y),
+                self.copy(piece, 1, left, self.at(piece, 1, 1, 0), self.peers.x),
+                self.copy(piece, 2, right, self.at(piece, 2, 1, 1), self.peers.y),
             ]
         if stage == "second":
             return [
-                self.copy(piece, 3, self.at(piece, 0, 2, 0), self.at(piece, 2, 2, 0), self.y),
-                self.copy(piece, 4, self.at(piece, 0, 1, 1), self.at(piece, 1, 1, 1), self.x),
-                self.copy(piece, 5, self.at(piece, 2, 1, 1), self.at(piece, 3, 1, 1), self.x),
+                self.copy(piece, 3, self.at(piece, 0, 2, 0), self.at(piece, 2, 2, 0), self.peers.y),
+                self.copy(piece, 4, self.at(piece, 0, 1, 1), self.at(piece, 1, 1, 1), self.peers.x),
+                self.copy(piece, 5, self.at(piece, 2, 1, 1), self.at(piece, 3, 1, 1), self.peers.x),
             ]
         span = pl.ds(piece * self.wide, self.wide)
-        return [self.copy(piece, 6, self.near.at[:, span], self.far.at[:, span], self.core)]
+        return [self.copy(piece, 6, self.near.at[:, span], self.far.at[:, span], self.peers.core)]
 
     def start(self, piece, stage):
         for copy in self.copies(piece, stage):
@@ -153,7 +164,7 @@
     def run(self, event):
         name, piece = event
         if name == "begin":
-            self.greet()
+            self.peers.greet()
             own = pltpu.make_async_copy(self.shard, self.at(0, 0, 1), self.local)
             own.start()
             self.start(0, "z")
@@ -528,14 +539,18 @@
     )(m, mid, near, far, near, far, up_shift, feats, *([] if shard is None else [shard]))
 
 
-def mlp_back_kernel(
+def mlp_back_kernel(*refs, gain_row):
+    step = pl.program_id(0)
+    mlp_back_work(*refs, gain_row, step == 0, step == pl.num_programs(0) - 1)
+
+
+def mlp_back_work(
     g_ref, down_near_ref, down_far_ref, slope_ref, up_near_ref, up_far_ref, mid_ref, feats_ref,
-    gz_ref, gh_ref, up_shift_grad_ref, g1_ref, gr_ref, small_ref, acc_ref, *, gain_row,
+    gz_ref, gh_ref, up_shift_grad_ref, g1_ref, gr_ref, small_ref, acc_ref, gain_row, opening, closing,
 ):
     half = up_near_ref.shape[0]
-    step = pl.program_id(0)
-
-    @pl.when(step == 0)
+
+    @pl.when(opening)
     def _():
         gz_ref[...] = g_ref[...].astype(BF16)
         acc_ref[...] = jnp.zeros_like(acc_ref)
@@ -547,7 +562,7 @@
     acc_ref[:, :half] += nt(gh, up_near_ref[...])
     acc_ref[:, half:] += nt(gh, up_far_ref[...])
 
-    @pl.when(step == pl.num_programs(0) - 1)
+    @pl.when(closing)
     def _():
         gm = acc_ref[...]
         hat, scale = row_norm(mid_ref[...])
@@ -589,9 +604,13 @@
     )(grad, near, far, slope, near, far, mid, feats)
 
 
-def attend_back_kernel(
+def attend_back_kernel(*refs, rows_of, layer):
+    attend_back_work(*refs, rows_of, layer, lambda: None)
+
+
+def attend_back_work(
     gr_ref, q_ref, kv_ref, q_hat_ref, k_hat_ref, q_scale_ref, k_scale_ref, p_ref, near_ref, far_ref, heads_ref,
-    gq_ref, gkv_ref, mine_ref, left_ref, right_ref, small_ref, acc_ref, *, rows_of, layer,
+    gq_ref, gkv_ref, mine_ref, left_ref, right_ref, small_ref, acc_ref, rows_of, layer, middle,
 ):
     rows = gr_ref.shape[0]
     half = near_ref.shape[0]
@@ -608,6 +627,8 @@
     first_t, second_t = first.T, second.T
     grad_q, grad_k, grad_v = [], [], []
     for head in range(3):
+        if head == 1:
+            middle()
         go_head = only(go[:, PAIR:], head) if head < 2 else only(go[:, :PAIR], 1)
         query = only(qn[:, PAIR * (head // 2) : PAIR * (head // 2 + 1)] * HD ** (-0.5), head % 2).astype(BF16)
         stored = p_ref[head]
@@ -652,34 +673,42 @@
         right_ref[...] = acc_ref[REACH + rows :, :].astype(BF16)
 
 
+def attend_back_specs(rows, width, pieces, lines):
+    half = width // 2
+    window = rows + 2 * REACH
+    full = whole((rows, width))
+    in_specs = [
+        full, column(rows, 2 * PAIR), column(window, 3 * PAIR), column(rows, 2 * PAIR), column(window, 2 * PAIR),
+        column(rows, 2 * PAIR), column(window, 2 * PAIR), pl.BlockSpec((3, window, rows), lambda step: (step, 0, 0)),
+        column(half, 6 * PAIR), column(half, 6 * PAIR), column(lines, 3 * PAIR),
+    ]
+    out_specs = [
+        column(rows, 2 * PAIR), column(window, 3 * PAIR), full, whole((REACH, width)), whole((REACH, width)), column(8, 3 * PAIR),
+    ]
+    out_shape = [
+        shaped((rows, pieces * 2 * PAIR)), shaped((window, pieces * 3 * PAIR)), shaped((rows, width), F32),
+        shaped((REACH, width)), shaped((REACH, width)), shaped((8, pieces * 3 * PAIR), F32),
+    ]
+    cost = pl.CostEstimate(
+        flops=2 * window * width * width * 2 + 20 * window * rows * width * 2,
+        bytes_accessed=20 * window * width,
+        transcendentals=0,
+    )
+    return in_specs, out_specs, out_shape, [pltpu.VMEM((window, width), F32)], cost
+
+
 def attend_back(gr, stored, near, far, heads, rows_of, layer):
     rows, width = gr.shape
-    half = width // 2
-    window = rows + 2 * REACH
     pieces = near.shape[1] // (6 * PAIR)
-    full = whole((rows, width))
+    in_specs, out_specs, out_shape, scratch, cost = attend_back_specs(rows, width, pieces, heads.shape[0])
     return pl.pallas_call(
         functools.partial(attend_back_kernel, rows_of=rows_of, layer=layer),
         grid=(pieces,),
-        in_specs=[
-            full, column(rows, 2 * PAIR), column(window, 3 * PAIR), column(rows, 2 * PAIR), column(window, 2 * PAIR),
-            column(rows, 2 * PAIR), column(window, 2 * PAIR), pl.BlockSpec((3, window, rows), lambda step: (step, 0, 0)),
-            column(half, 6 * PAIR), column(half, 6 * PAIR), column(heads.shape[0], 3 * PAIR),
-        ],
-        out_specs=[
-            column(rows, 2 * PAIR), column(window, 3 * PAIR), full, whole((REACH, width)), whole((REACH, width)),
-            column(8, 3 * PAIR),
-        ],
-        out_shape=[
-            shaped((rows, pieces * 2 * PAIR)), shaped((window, pieces * 3 * PAIR)), shaped((rows, width), F32),
-            shaped((REACH, width)), shaped((REACH, width)), shaped((8, pieces * 3 * PAIR), F32),
-        ],
-        scratch_shapes=[pltpu.VMEM((window, width), F32)],
-        cost_estimate=pl.CostEstimate(
-            flops=2 * window * width * width * 2 + 20 * window * rows * width * 2,
-            bytes_accessed=20 * window * width,
-            transcendentals=0,
-        ),
+        in_specs=in_specs,
+        out_specs=out_specs,
+        out_shape=out_shape,
+        scratch_shapes=scratch,
+        cost_estimate=cost,
         name="attend_back",
     )(gr, *stored, near, far, heads)
 
@@ -758,6 +787,351 @@
         ),
         name="mlp_weight_grads",
     )(m, gh, gz, act)
+
+
+class Scatter:
+    KINDS = 7
+
+    def __init__(self, out, away, keep, core, first, second, ring_in, send, recv):
+        self.out, self.away, self.keep, self.core_in = out, away, keep, core
+        self.first_in, self.second_in, self.ring_in, self.send, self.recv = first, second, ring_in, send, recv
+        self.chunk, self.wide = out.shape
+        self.half = self.wide // 2
+        self.pieces = keep.shape[0]
+        self.near = Neighbours()
+
+    def copy(self, piece, kind, source, target, device):
+        return pltpu.make_async_remote_copy(
+            src_ref=source, dst_ref=target, send_sem=self.send.at[piece, kind], recv_sem=self.recv.at[piece, kind],
+            device_id=device, device_id_type=MESH,
+        )
+
+    def copies(self, piece, stage):
+        c, left, right = self.chunk, pl.ds(0, self.half), pl.ds(self.half, self.half)
+        rows = lambda start, count=1: pl.ds(start * c, count * c)
+        if stage == "core":
+            return [self.copy(piece, 0, self.away.at[piece], self.core_in.at[piece], self.near.core)]
+        if stage == "first":
+            source, target = self.keep.at[piece], self.first_in.at[piece]
+            return [
+                self.copy(piece, 1, source.at[rows(2, 2), left], target.at[:, left], self.near.y),
+                self.copy(piece, 2, source.at[rows(1), right], target.at[rows(0), right], self.near.x),
+                self.copy(piece, 3, source.at[rows(3), right], target.at[rows(1), right], self.near.x),
+            ]
+        if stage == "second":
+            source, target = self.keep.at[piece], self.second_in.at[piece]
+            return [
+                self.copy(piece, 4, source.at[rows(1), left], target.at[:, left], self.near.x),
+                self.copy(piece, 5, source.at[rows(2), right], target.at[:, right], self.near.y),
+            ]
+        target = self.ring_in.at[lax.rem(piece + 1, self.pieces)]
+        return [self.copy(piece, 6, self.keep.at[piece, rows(0), :], target, self.near.right)]
+
+    def start(self, piece, stage):
+        for copy in self.copies(piece, stage):
+            copy.start()
+
+    def arrived(self, piece, stage):
+        for copy in self.copies(piece, stage):
+            copy.wait_recv()
+
+    def add(self, piece, start, count, cols, source):
+        step = 32
+
+        @pl.loop(0, count * self.chunk // step)
+        def _(index):
+            row = pl.multiple_of(index * step, step)
+            into = (piece, pl.ds(start * self.chunk + row, step), cols)
+            self.keep[into] = (self.keep[into].astype(F32) + source[pl.ds(row, step), cols].astype(F32)).astype(BF16)
+
+    def place(self, index):
+        return lax.rem(index + 1, self.pieces)
+
+    def core(self, index):
+        self.start(self.place(index), "core")
+
+    def first(self, index):
+        piece = self.place(index)
+        self.arrived(piece, "core")
+        self.add(piece, 0, 4, pl.ds(0, self.wide), self.core_in.at[piece])
+        self.start(piece, "first")
+
+    def second(self, index):
+        piece = self.place(index)
+        left, right = pl.ds(0, self.half), pl.ds(self.half, self.half)
+        self.arrived(piece, "first")
+        source = self.first_in.at[piece]
+        self.add(piece, 0, 2, left, source)
+        self.add(piece, 0, 1, right, source)
+        self.add(piece, 2, 1, right, source.at[pl.ds(self.chunk, self.chunk)])
+        self.start(piece, "second")
+
+    def last(self, index):
+        piece = self.place(index)
+        self.arrived(piece, "second")
+        kept = pl.ds(0, self.chunk)
+
+        def ring():
+            self.arrived(lax.rem(piece + self.pieces - 1, self.pieces), "ring")
+
+        def total(with_ring):
+            value = self.keep[piece, kept, :].astype(F32) + self.second_in[piece].astype(F32)
+            return value + self.ring_in[piece].astype(F32) if with_ring else value
+
+        if isinstance(index, int):
+            if index:
+                ring()
+            if index == self.pieces - 1:
+                self.out[...] = total(True)
+            else:
+                self.keep[piece, kept, :] = total(index > 0).astype(BF16)
+                self.start(piece, "ring")
+            return
+        raise NotImplementedError
+
+    def done(self):
+        for piece in range(self.pieces):
+            for stage in ("core", "first", "second", "ring"):
+                if stage != "ring" or piece:
+                    for copy in self.copies(piece, stage):
+                        copy.wait_send()
+
+
+def scatter_specs(pieces, chunk, wide):
+    buffer = lambda rows: pltpu.VMEM((pieces, rows * chunk, wide), BF16)
+    semaphores = pltpu.SemaphoreType.DMA((pieces, Scatter.KINDS))
+    return shaped((chunk, wide), F32), [buffer(4), buffer(4), buffer(4), buffer(2), buffer(1), buffer(1), semaphores, semaphores]
+
+
+def at_step(index, work):
+    @pl.when(pl.program_id(0) == index)
+    def _():
+        work()
+
+
+def attend_back_scatter_kernel(
+    gr_ref, q_ref, kv_ref, q_hat_ref, k_hat_ref, q_scale_ref, k_scale_ref, p_ref, near_ref, far_ref, heads_ref,
+    m_ref, gh_ref, gz_ref, act_ref, gq_ref, gkv_ref, mine_ref, left_ref, right_ref, small_ref, out_ref,
+    acc_ref, m_t_ref, gz_t_ref, *scratch, rows_of, layer,
+):
+    scatter = Scatter(out_ref, *scratch)
+    pieces, half, wide = scatter.pieces, near_ref.shape[0], gh_ref.shape[1]
+    step = pl.program_id(0)
+
+    @pl.when(step == 0)
+    def _():
+        scatter.near.greet()
+        m_t_ref[...] = m_ref[...].T
+        gz_t_ref[...] = gz_ref[...].T
+
+    piece = scatter.place(step)
+    for part, ref in ((slice(0, half), scatter.keep), (slice(half, 2 * half), scatter.away)):
+        ref[piece, :, :wide] = nn(m_t_ref[part, :], gh_ref[...]).astype(BF16)
+        ref[piece, :, wide:] = nn(gz_t_ref[part, :], act_ref[...]).astype(BF16)
+    scatter.core(step)
+    for index in range(2, pieces):
+        at_step(index, lambda: scatter.last(index - 2))
+
+    def middle():
+        scatter.first(step)
+
+        @pl.when(step > 0)
+        def _():
+            scatter.second(step - 1)
+
+    attend_back_work(
+        gr_ref, q_ref, kv_ref, q_hat_ref, k_hat_ref, q_scale_ref, k_scale_ref, p_ref, near_ref, far_ref, heads_ref,
+        gq_ref, gkv_ref, mine_ref, left_ref, right_ref, small_ref, acc_ref, rows_of, layer, middle,
+    )
+
+    @pl.when(step == pieces - 1)
+    def _():
+        scatter.last(pieces - 2)
+        scatter.second(pieces - 1)
+        scatter.last(pieces - 1)
+        scatter.done()
+
+
+def attend_back_scatter(gr, stored, near, far, heads, m, gh, gz, act, rows_of, layer, collective):
+    rows, width = gr.shape
+    half = width // 2
+    hidden = gh.shape[1]
+    pieces = near.shape[1] // (6 * PAIR)
+    wide = hidden // pieces
+    in_specs, out_specs, out_shape, scratch, cost = attend_back_specs(rows, width, pieces, heads.shape[0])
+    turned = pl.BlockSpec((rows, wide), lambda step: (0, lax.rem(step + 1, pieces)))
+    full = whole((rows, width))
+    result, extra = scatter_specs(pieces, half // 4, 2 * wide)
+    return pl.pallas_call(
+        functools.partial(attend_back_scatter_kernel, rows_of=rows_of, layer=layer),
+        grid=(pieces,),
+        in_specs=in_specs + [full, turned, full, turned],
+        out_specs=out_specs + [whole(result.shape)],
+        out_shape=out_shape + [result],
+        scratch_shapes=scratch + [pltpu.VMEM((width, rows), BF16)] * 2 + extra,
+        compiler_params=params(collective),
+        cost_estimate=cost,
+        name="attend_back_scatter",
+    )(gr, *stored, near, far, heads, m, gh, gz, act)
+
+
+def give_back_kernel(*refs, rows_of, layer, with_mlp):
+    a_ref, gq_ref, gkv_ref, gr_ref, o_ref, x_ref, g1_ref, mine_ref, left_ref, right_ref, feats_ref = refs[:11]
+    rest = refs[11:]
+    if with_mlp:
+        down_near_ref, down_far_ref, slope_ref, up_near_ref, up_far_ref, mid_ref = rest[:6]
+        rest = rest[6:]
+    g_ref, sums_ref, out_ref = rest[:3]
+    rest = rest[3:]
+    if with_mlp:
+        mlp_outs, rest = rest[:6], rest[6:]
+        acc_ref, rest = rest[0], rest[1:]
+    a_t_ref, gr_t_ref, total_ref, landed_ref, halo_send, halo_recv, *scratch = rest
+    scatter = Scatter(out_ref, *scratch)
+    pieces, rows = scatter.pieces, gr_ref.shape[0]
+    half = gr_ref.shape[1] // 2
+    spill = REACH - rows
+    step = pl.program_id(0)
+    moves = [
+        (1, right_ref, pl.ds(0, rows), pl.ds(0, rows), 0),
+        (-1, left_ref, pl.ds(spill, rows), pl.ds(0, rows), 0),
+        (2, right_ref, pl.ds(rows, spill), pl.ds(0, spill), 0),
+        (-2, left_ref, pl.ds(0, spill), pl.ds(0, spill), rows - spill),
+    ]
+    place, size = lax.axis_index("tp"), lax.axis_size("tp")
+    inside = lambda other: jnp.logical_and(other >= 0, other < size)
+
+    def halo_copy(index):
+        distance, ref, source, target, _ = moves[index]
+        return pltpu.make_async_remote_copy(
+            src_ref=ref.at[source, :], dst_ref=landed_ref.at[index, target, :], send_sem=halo_send.at[index],
+            recv_sem=halo_recv.at[index], device_id={"tp": place + distance}, device_id_type=MESH,
+        )
+
+    @pl.when(step == 0)
+    def _():
+        scatter.near.greet(all_tp=True)
+        for index, (distance, *_) in enumerate(moves):
+
+            @pl.when(inside(place + distance))
+            def _():
+                halo_copy(index).start()
+
+        a_t_ref[...] = a_ref[...].T
+        gr_t_ref[...] = gr_ref[...].T
+
+    @pl.when(step < pieces)
+    def _():
+        piece = scatter.place(step)
+        for part, ref in ((slice(0, half), scatter.keep), (slice(half, 2 * half), scatter.away)):
+            from_q = nn(a_t_ref[part, REACH : REACH + rows], gq_ref[...])
+            from_o = nn(gr_t_ref[part, :], o_ref[...])
+            ref[piece, :, :PAIR] = from_q[:, :PAIR].astype(BF16)
+            ref[piece, :, PAIR : 4 * PAIR] = nn(a_t_ref[part, :], gkv_ref[...]).astype(BF16)
+            ref[piece, :, 4 * PAIR : 5 * PAIR] = (from_q[:, PAIR:] + from_o[:, :PAIR]).astype(BF16)
+            ref[piece, :, 5 * PAIR :] = from_o[:, PAIR:].astype(BF16)
+        scatter.core(step)
+
+        @pl.when(step > 0)
+        def _():
+            scatter.first(step - 1)
+
+        @pl.when(step > 1)
+        def _():
+            scatter.second(step - 2)
+
+    @pl.when(step == pieces - 1)
+    def _():
+        scatter.first(pieces - 1)
+        scatter.last(0)
+        scatter.second(pieces - 2)
+        total_ref[...] = mine_ref[...]
+        for index, (distance, _, _, target, start) in enumerate(moves):
+
+            @pl.when(inside(place + distance))
+            def _():
+                halo_copy(index).wait_send()
+
+            @pl.when(inside(place - distance))
+            def _():
+                halo_copy(index).wait_recv()
+                total_ref[pl.ds(start, target.size), :] += landed_ref[index, target, :].astype(F32)
+
+        scatter.last(1)
+        total = total_ref[...]
+        hat, scale = row_norm(x_ref[...])
+        g_ref[...] = g1_ref[...] + row_norm_back(total * line(feats_ref, rows_of.ln_gain(layer, 0)), hat, scale)
+        sums_ref[...] = jnp.zeros_like(sums_ref)
+        sums_ref[0:1, :] = jnp.sum(total * hat, axis=0, keepdims=True)
+        sums_ref[1:2, :] = jnp.sum(total, axis=0, keepdims=True)
+        scatter.second(pieces - 1)
+
+    if with_mlp:
+
+        @pl.when(step >= pieces)
+        def _():
+            mlp_back_work(
+                g_ref, down_near_ref, down_far_ref, slope_ref, up_near_ref, up_far_ref, mid_ref, feats_ref, *mlp_outs,
+                acc_ref, rows_of.ln_gain(layer - 1, 1), step == pieces, step == 2 * pieces - 1,
+            )
+
+    @pl.when(step == pl.num_programs(0) - 1)
+    def _():
+        scatter.last(pieces - 2)
+        scatter.last(pieces - 1)
+        scatter.done()
+
+
+def give_back(a_win, gq, gkv, gr, o, x, g1, mine, left, right, feats, rows_of, layer, collective, before=None):
+    window, width = a_win.shape
+    rows = gr.shape[0]
+    half = width // 2
+    pieces = gq.shape[1] // (2 * PAIR)
+    full = whole((rows, width))
+    turned = lambda height, wide: pl.BlockSpec(
+        (height, wide), lambda step: (0, lax.rem(jnp.minimum(step, pieces - 1) + 1, pieces))
+    )
+    in_specs = [
+        whole((window, width)), turned(rows, 2 * PAIR), turned(window, 3 * PAIR), full, turned(rows, 2 * PAIR), full, full,
+        full, whole((REACH, width)), whole((REACH, width)), whole(feats.shape),
+    ]
+    operands = [a_win, gq, gkv, gr, o, x, g1, mine, left, right, feats]
+    result, extra = scatter_specs(pieces, half // 4, 6 * PAIR)
+    out_specs = [full, whole((8, width)), whole(result.shape)]
+    out_shape = [shaped((rows, width), F32), shaped((8, width), F32), result]
+    scratch = []
+    if before is not None:
+        near, far, slope, mid = before
+        hidden = slope.shape[1]
+        wide = hidden // pieces
+        late = lambda height, every=1, first=0: pl.BlockSpec(
+            (height, wide), lambda step: (0, jnp.maximum(step - pieces, 0) * every + first)
+        )
+        in_specs += [late(half, 2, 1), late(half, 2, 1), late(rows), late(half, 2), late(half, 2), full]
+        operands += [near, far, slope, near, far, mid]
+        out_specs += [full, late(rows), late(1), full, full, whole((8, width))]
+        out_shape += [
+            shaped((rows, width)), shaped((rows, hidden)), shaped((1, hidden), F32), shaped((rows, width), F32),
+            shaped((rows, width)), shaped((8, width), F32),
+        ]
+        scratch = [pltpu.VMEM((rows, width), F32)]
+    scratch += [
+        pltpu.VMEM((width, window), BF16), pltpu.VMEM((width, rows), BF16), pltpu.VMEM((rows, width), F32),
+        pltpu.VMEM((4, rows, width), BF16), pltpu.SemaphoreType.DMA((4,)), pltpu.SemaphoreType.DMA((4,)), *extra,
+    ]
+    return pl.pallas_call(
+        functools.partial(give_back_kernel, rows_of=rows_of, layer=layer, with_mlp=before is not None),
+        grid=(pieces if before is None else 2 * pieces,),
+        in_specs=in_specs,
+        out_specs=out_specs,
+        out_shape=out_shape,
+        scratch_shapes=scratch,
+        compiler_params=params(collective),
+        cost_estimate=pl.CostEstimate(
+            flops=2 * width * width * (2 * window + 2 * rows), bytes_accessed=20 * width * width, transcendentals=0
+        ),
+        name="give_back",
+    )(*operands)
 
 
 def flip(array, bit, axis="fsdp"):
@@ -950,28 +1324,40 @@
     grad = jnp.dot(cotangent, exact, precision=HIGHEST, preferred_element_type=F32)
     kept_sums = [None] * layers
     w_qkv_grad, w_out_grad, w_fc1_grad, w_fc2_grad = ([None] * layers for _ in range(4))
+    back = None
     for layer in reversed(range(layers)):
         attn_near, attn_far, mlp_near, mlp_far = weights[layer]
         x, a_win, kept, mid, m, act, slope = saved[layer]
         *stored, o = kept
-        gz, gh, up_grad, g1, gr, mlp_small = mlp_back(
-            grad, mlp_near, mlp_far, slope, mid, feats, rows_of.ln_gain(layer, 1)
-        )
-        keep, send = mlp_weight_grads(m, gh, gz, act)
-        block = reduce_by_permutes(keep, send, layer % 2 == 0)
-        middle = block.shape[1] // 2
-        w_fc1_grad[layer], w_fc2_grad[layer] = block[:, :middle], block[:, middle:].T
-        gq, gkv, mine, left, right, attn_small = attend_back(gr, stored, attn_near, attn_far, heads, rows_of, layer)
-        keep, send = attn_weight_grads(a_win, gq, gkv, gr, o)
-        w_qkv_grad[layer], w_out_grad[layer] = attn_unshard(reduce_by_permutes(keep, send, layer % 2 == 1))
-        ends = jnp.concatenate([hop(right[rows:], 2), hop(left[:spill], -2)], axis=0).astype(F32)
-        attn_grad = mine + hop(right[:rows], 1).astype(F32) + hop(left[spill:], -1).astype(F32) + ends
-        hat, scale = row_norm(x)
-        grad = g1 + row_norm_back(attn_grad * feats[rows_of.ln_gain(layer, 0)], hat, scale)
-        kept_sums[layer] = (
-            jnp.sum(attn_grad * hat, axis=0), jnp.sum(attn_grad, axis=0), mlp_small, attn_small,
-            up_grad.reshape(parts, width),
-        )
+        if back is None:
+            back = mlp_back(grad, mlp_near, mlp_far, slope, mid, feats, rows_of.ln_gain(layer, 1))
+        gz, gh, up_grad, g1, gr, mlp_small = back
+        back = None
+        if in_kernel:
+            gq, gkv, mine, left, right, attn_small, mlp_block = attend_back_scatter(
+                gr, stored, attn_near, attn_far, heads, m, gh, gz, act, rows_of, layer, 40 + layer
+            )
+            before = None
+            if layer:
+                before = (*weights[layer - 1][2:], saved[layer - 1][6], saved[layer - 1][3])
+            grad, norm_sums, attn_block, *back = give_back(
+                a_win, gq, gkv, gr, o, x, g1, mine, left, right, feats, rows_of, layer, 50 + layer, before
+            )
+            back = back or None
+            norm_sums = norm_sums[0], norm_sums[1]
+        else:
+            mlp_block = reduce_by_permutes(*mlp_weight_grads(m, gh, gz, act), layer % 2 == 0)
+            gq, gkv, mine, left, right, attn_small = attend_back(gr, stored, attn_near, attn_far, heads, rows_of, layer)
+            attn_block = reduce_by_permutes(*attn_weight_grads(a_win, gq, gkv, gr, o), layer % 2 == 1)
+            ends = jnp.concatenate([hop(right[rows:], 2), hop(left[:spill], -2)], axis=0).astype(F32)
+            attn_grad = mine + hop(right[:rows], 1).astype(F32) + hop(left[spill:], -1).astype(F32) + ends
+            hat, scale = row_norm(x)
+            grad = g1 + row_norm_back(attn_grad * feats[rows_of.ln_gain(layer, 0)], hat, scale)
+            norm_sums = jnp.sum(attn_grad * hat, axis=0), jnp.sum(attn_grad, axis=0)
+        middle = mlp_block.shape[1] // 2
+        w_fc1_grad[layer], w_fc2_grad[layer] = mlp_block[:, :middle], mlp_block[:, middle:].T
+        w_qkv_grad[layer], w_out_grad[layer] = attn_unshard(attn_block)
+        kept_sums[layer] = (*norm_sums, mlp_small, attn_small, up_grad.reshape(parts, width))
 
     token_grad = restore(grad, exact)
     row_grad = jnp.einsum("tg,td->gd", row_hot.astype(F32), grad, precision=HIGHEST)

time: 690 us -> 564 us (0.82)
  waiting for transfers between devices: 166 us -> 19.6 us
  Pallas kernels: 343 us -> 458 us
  starting transfers between devices: 55.8 us -> 11.8 us
  other arithmetic: 37 us -> 9.17 us
  local copies, waits for them, and re-layouts: 59.8 us -> 39.4 us
    pallas_call x6 -> x4, Pallas kernels: 79.3 us -> 205 us  [the longest x2 124 us: attend_back_scatter(): pl.pallas_call(functools.partial(attend_back_scatter_kernel, rows_of=rows...]
    ppermute x22 -> x10, waiting for transfers between devices: 113 us -> 19.6 us  [flip(): return lax.ppermute(array, axis, [(i, i ^ 1 << bit) for i in range(size)])]
    ppermute x20 -> x0, waiting for transfers between devices: 52.8 us -> none  [the longest x12 52.8 us: ring(): return lax.ppermute(array, 'tp', [(i, (i + 1) % size) for i in range(size)])]
    ppermute x20 -> x0, starting transfers between devices: 28.1 us -> none  [the longest x8 24.2 us: hop(): lax.ppermute(array, 'tp', [(i, i + distance) for i in range(size) if 0 <=...]
    convert_element_type x20 -> x0, other arithmetic: 18.9 us -> none  [add(): return (left.astype(F32) + right.astype(F32)).astype(kind)]
    ppermute x22 -> x10, starting transfers between devices: 27.7 us -> 11.8 us  [flip(): return lax.ppermute(array, axis, [(i, i ^ 1 << bit) for i in range(size)])]
    slice x11 -> x3, local copies, waits for them, and re-layouts: 13.5 us -> 1.66 us  [the longest x2 1.64 us: body(): norm_sums = (norm_sums[0], norm_sums[1])]
    pallas_call x2 -> x1, Pallas kernels: 20.9 us -> 10.4 us  [mlp_back(): pl.pallas_call(functools.partial(mlp_back_kernel, gain_row=gain_row), gri...]
  transfers between devices with their start and end apart: 42 -> 10, of which waited for: 23 -> 7; matrix products, arithmetic and copies ran while one was open for 13% -> 3% of each run, Pallas kernels for 15% -> 6%
where the time goes in v3:
time: 564 us; the launch traced here: 557 us
  Pallas kernels  458 us (81%)
  local copies, waits for them, and re-layouts  39.4 us (7%)
  waiting for transfers between devices  19.6 us (3%)
  matrix products  16.8 us (3%)
  starting transfers between devices  11.8 us (2%)
  other arithmetic  9.17 us (2%)
    pallas_call x2, Pallas kernels, attend_back_scatter(): pl.pallas_call(functools.partial(attend_back_scatter_kernel, rows_of=rows...  124 us
    pallas_call x2, Pallas kernels, attend(): pl.pallas_call(functools.partial(attend_kernel, rows_of=rows_of, layer=la...  113 us
    pallas_call x2, Pallas kernels, give_back(): pl.pallas_call(functools.partial(give_back_kernel, rows_of=rows_of, layer...  81.2 us
    pallas_call x2, Pallas kernels, mlp(): pl.pallas_call(functools.partial(mlp_kernel, rows_of=rows_of, layer=layer...  47.4 us
    pallas_call x2, Pallas kernels, halo(): pl.pallas_call(halo_kernel, grid=(1,), in_specs=[whole((rows, width))], o...  46.3 us
    pallas_call x1, Pallas kernels, gather_alone(): pl.pallas_call(gather_kernel, grid=(1,), in_specs=operands, out_specs=[AN...  35.2 us
    ppermute x10, waiting for transfers between devices, flip(): return lax.ppermute(array, axis, [(i, i ^ 1 << bit) for i in range(size)])  19.6 us
    ppermute x10, starting transfers between devices, flip(): return lax.ppermute(array, axis, [(i, i ^ 1 << bit) for i in range(size)])  11.8 us
  transfers between devices with their start and end apart: 10, of which 7 were waited for; matrix products, arithmetic and copies ran while one was open for 3% of the time, Pallas kernels for 6%

profile of v3, /device:TPU:0, one launch (start us, length us, event | category | flops | bytes accessed | tf_op | source)
XLA Modules:
  0.0 556.6 jit_solution(2809714528183580752)
XLA Ops:
  8.0 3.1 collective-permute-start
  11.9 1.0 slice_bitcast_fusion.6
  13.8 1.0 slice_bitcast_fusion.5
  14.8 1.0 slice_bitcast_fusion.4
  15.9 2.2 fusion.16.refs_0_
  18.1 0.9 pad_maximum_fusion.4
  19.0 2.7 collective-permute-start.1
  23.4 35.2 %gather_block.1 = (bf16[384,3072]{1,0:T(8,128)(2,1)}, bf16[384,3072]{1,0:T(8,128)(2,1)}) custom-call(bf16[96,768]{1,0:T(8,128)(2,1)} %concatenate.96.shard_ref), custom_call_target="tpu_custom_call" | custom-call | tf_op jit(solution)/shard_map/gather_block/pallas_call | solution.py:235
  58.5 1.0 copy.189.refs_6_
  62.6 3.8 collective-permute-done.3
  67.5 3.9 collective-permute-done.4
  71.4 1.0 concatenate.94
  75.3 0.9 add_convert_fusion.a_ref
  76.3 21.0 %halo.2.refs_0_ = bf16[1024,768]{1,0:T(8,128)(2,1)} custom-call(bf16[256,768]{1,0:T(8,128)(2,1)} %add_convert_fusion.a_ref), custom_call_target="tpu_custom_call" | custom-call | tf_op jit(solution)/shard_map/halo/pallas_call | solution.py:299
  98.5 1.5 fusion.2.refs_3_.heads_ref
  100.1 55.2 %attend.2 = (bf16[256,1024]{1,0:T(8,128)(2,1)}, bf16[1024,1536]{1,0:T(8,128)(2,1)}, bf16[256,1024]{1,0:T(8,128)(2,1)}, bf16[1024,1024]{1,0:T(8,128)(2,1)}, bf16[...) custom-call(bf16[1024,768]{1,0:T(8,128)(2,1)} %halo.2.refs_0_, ...), custom_call_target="tpu_custom_call" | custom-call | flops 8858370048 | bytes 15728640 | tf_op jit(solution)/shard_map/attend/pallas_call | solution.py:451
  155.3 37.5 %mlp.2 = (bf16[256,3072]{1,0:T(8,128)(2,1)}, bf16[256,3072]{1,0:T(8,128)(2,1)}, f32[256,768]{1,0:T(8,128)}, bf16[256,768]{1,0:T(8,128)(2,1)}, bf16[384,3072]{1,0:T(8,128)(2,1)}, /*index=5*/bf16[384,3072]{1,0:T(8,128)(2,1)}) custom-call(bf16[256,768]{1,0:T(8,128)(2,1)} %get-tuple-element.84.refs_0_.m_ref, f32[256,768]{1,0:T(8,128)} %get-tuple-element.85.refs_1_.refs_16_, ...), custom_call_target="tpu_custom_call" | custom-call | flops 2415919104 | bytes 9437184 | tf_op jit(solution)/shard_map/mlp/pallas_call | solution.py:524
  192.8 25.3 %halo.3.refs_0_ = bf16[1024,768]{1,0:T(8,128)(2,1)} custom-call(bf16[256,768]{1,0:T(8,128)(2,1)} %get-tuple-element.88.a_ref), custom_call_target="tpu_custom_call" | custom-call | tf_op jit(solution)/shard_map/halo/pallas_call | solution.py:299
  218.9 58.2 %attend.3 = (bf16[256,1024]{1,0:T(8,128)(2,1)}, bf16[1024,1536]{1,0:T(8,128)(2,1)}, bf16[256,1024]{1,0:T(8,128)(2,1)}, bf16[1024,1024]{1,0:T(8,128)(2,1)}, bf16[...) custom-call(bf16[1024,768]{1,0:T(8,128)(2,1)} %halo.3.refs_0_, ...), custom_call_target="tpu_custom_call" | custom-call | flops 8858370048 | bytes 15728640 | tf_op jit(solution)/shard_map/attend/pallas_call | solution.py:451
  277.1 10.0 %mlp.3 = (bf16[256,3072]{1,0:T(8,128)(2,1)}, bf16[256,3072]{1,0:T(8,128)(2,1)}, f32[256,768]{1,0:T(8,128)}, bf16[256,768]{1,0:T(8,128)(2,1)}) custom-call(bf16[256,768]{1,0:T(8,128)(2,1)} %get-tuple-element.92.refs_0_.m_ref, f32[256,768]{1,0:T(8,128)} %get-tuple-element.93.refs_1_.refs_6_, bf16[384,6144]{1,0:T(8,128)(2,1)} %get-tuple-element.94.refs_2_.refs_4_.refs_1_, ...), custom_call_target="tpu_custom_call" | custom-call | flops 2415919104 | bytes 9437184 | tf_op jit(solution)/shard_map/mlp/pallas_call | solution.py:524
  287.0 10.4 %mlp_back.1 = (bf16[256,768]{1,0:T(8,128)(2,1)}, bf16[256,3072]{1,0:T(8,128)(2,1)}, f32[1,3072]{1,0:T(1,128)}, f32[256,768]{1,0:T(8,128)}, bf16[256,768]{1,0:T(8,128)(2,1)}, /*index=5*/f32[8,768]{1,0:T(8,128)}) custom-call(f32[256,768]{1,0:T(8,128)} %fusion.16.refs_0_, bf16[384,6144]{1,0:T(8,128)(2,1)} %get-tuple-element.94.refs_2_.refs_4_.refs_1_, ...), custom_call_target="tpu_custom_call" | custom-call | flops 2415919104 | bytes 9437184 | tf_op jit(solution)/shard_map/mlp_back/pallas_call | solution.py:587
  297.5 62.8 %attend_back_scatter.2 = (bf16[256,1024]{1,0:T(8,128)(2,1)}, bf16[1024,1536]{1,0:T(8,128)(2,1)}, f32[256,768]{1,0:T(8,128)}, bf16[384,768]{1,0:T(8,128)(2,1)}, b...) custom-call(bf16[256,768]{1,0:T(8,128)(2,1)} %get-tuple-element.98.gr_ref.refs_3_, ...), custom_call_target="tpu_custom_call" | custom-call | flops 10468982784 | bytes 15728640 | tf_op jit(solution)/shard_map/attend_back_scatter/pallas_call | solution.py:965
  360.2 43.9 %give_back.2 = (f32[256,768]{1,0:T(8,128)}, f32[8,768]{1,0:T(8,128)}, f32[96,768]{1,0:T(8,128)}, bf16[256,768]{1,0:T(8,128)(2,1)}, bf16[256,3072]{1,0:T(8,128)(2...) custom-call(bf16[1024,768]{1,0:T(8,128)(2,1)} %halo.3.refs_0_, ...), custom_call_target="tpu_custom_call" | custom-call | flops 3019898880 | bytes 11796480 | tf_op jit(solution)/shard_map/give_back/pallas_call | solution.py:1122
  404.1 60.8 %attend_back_scatter.3 = (bf16[256,1024]{1,0:T(8,128)(2,1)}, bf16[1024,1536]{1,0:T(8,128)(2,1)}, f32[256,768]{1,0:T(8,128)}, bf16[384,768]{1,0:T(8,128)(2,1)}, b...) custom-call(bf16[256,768]{1,0:T(8,128)(2,1)} %get-tuple-element.117.gr_ref.refs_3_, ...), custom_call_target="tpu_custom_call" | custom-call | flops 10468982784 | bytes 15728640 | tf_op jit(solution)/shard_map/attend_back_scatter/pallas_call | solution.py:965
  464.9 37.3 %give_back.3 = (f32[256,768]{1,0:T(8,128)}, f32[8,768]{1,0:T(8,128)}, f32[96,768]{1,0:T(8,128)}) custom-call(bf16[1024,768]{1,0:T(8,128)(2,1)} %halo.2.refs_0_, bf16[256,1024]{1,0:T(8,128)(2,1)} %get-tuple-element.128.refs_1_, bf16[1024,1536]{1,0:T(8,128)(2,1)} %get-tuple-element.129.refs_2_, bf16[256,768]{1,0:T(8,128)(2,1)} %get-tuple-element.117.gr_ref.refs_3_, ...), custom_call_target="tpu_custom_call" | custom-call | flops 3019898880 | bytes 11796480 | tf_op jit(solution)/shard_map/give_back/pallas_call | solution.py:1122
  502.3 1.6 fusion.110
  503.9 1.7 fusion.111
  507.1 1.7 fusion.30
  509.4 2.2 fusion.10
  511.6 0.8 slice_bitcast_fusion.1
  512.4 0.8 slice_bitcast_fusion
  515.1 1.5 fusion.4
  516.6 2.1 fusion
  519.0 0.9 copy.197
  521.3 1.4 reduce.48
  522.7 1.4 reduce.47
  524.3 0.9 fusion.40
  525.4 2.9 collective-permute-start.5
  528.2 1.9 pad_maximum_fusion.2
  530.1 0.9 pad_maximum_fusion.1
  531.3 2.2 fusion.12
  533.6 0.9 collective-permute-start.6
  534.6 0.9 pad_maximum_fusion
  535.4 3.2 collective-permute-done.6
  538.7 1.2 collective-permute-done.7
  540.1 5.1 collective-permute-done.8
  545.2 1.1 collective-permute-start.9
  547.2 1.8 collective-permute-done.9
  (227 shorter events, 33.9 us)
Async XLA Ops:
  0.6 15.3 %copy-start = (f32[256,768]{1,0:T(8,128)S(1)}, f32[256,768]{1,0:T(8,128)}, u32[]{:S(2)}) copy-start(f32[256,768]{1,0:T(8,128)} %param.35) | copy-start | bytes 2359300
  0.7 15.1 %copy-start.32 = (s32[1,1024]{1,0:T(1,128)S(1)}, s32[1,1024]{1,0:T(1,128)}, u32[]{:S(2)}) copy-start(s32[1,1024]{1,0:T(1,128)} %param.19) | copy-start | bytes 12292
  8.0 11.0 %collective-permute-start = (bf16[1,3840]{1,0:T(2,128)(2,1)S(1)}, bf16[1,3840]{1,0:T(2,128)(2,1)S(1)}, u32[]{:S(2)}, u32[]{:S(2)}) collective-permute-start(bf16[1,3840]{1,0:T(2,128)(2,1)S(1)} %reshape.395), channel_id=1, source_target_pairs={{0,1},{1,0},{2,3},{3,2},{4,5},{5,4},{6,7},{7,6},{8,9},{9,8},{10,11... | collective-permute-start | bytes 23048 | tf_op jit(solution)/shard_map/ppermute | solution.py:1139
  11.2 503.9 %copy-start.30 = (s32[768]{0:T(1024)}, s32[768]{0:T(1024)S(1)}, u32[]{:S(2)}) copy-start(s32[768]{0:T(1024)S(1)} %get-tuple-element.308) | copy-start | bytes 9220
  18.9 78.5 %copy-start.35 = (s32[32]{0:T(128)}, s32[32]{0:T(128)S(1)}, u32[]{:S(2)}) copy-start(s32[32]{0:T(128)S(1)} %get-tuple-element.310) | copy-start | bytes 388
  18.9 78.5 %copy-start.36 = (s32[32]{0:T(128)}, s32[32]{0:T(128)S(1)}, u32[]{:S(2)}) copy-start(s32[32]{0:T(128)S(1)} %get-tuple-element.311) | copy-start | bytes 388
  19.0 41.6 %collective-permute-start.1 = (bf16[2,3840]{1,0:T(2,128)(2,1)S(1)}, bf16[2,3840]{1,0:T(2,128)(2,1)S(1)}, u32[]{:S(2)}, u32[]{:S(2)}) collective-permute-start(bf16[2,3840]{1,0:T(2,128)(2,1)S(1)} %pad_maximum_fusion.10), channel_id=1, source_target_pairs={{0,2},{1,3},{2,0},{3,1},{4,6},{5,7},{6,4},{7,5},{8,10},{9,11},{10,... | collective-permute-start | bytes 46088 | tf_op jit(solution)/shard_map/ppermute | solution.py:1139
  60.7 1.3 collective-permute-start.2
  62.0 4.3 collective-permute-start.3
  66.5 4.9 collective-permute-start.4
  72.8 1.5 copy-start.11
  73.7 1.6 copy-start.2
  75.0 23.5 %copy-start.3 = (f32[256,768]{1,0:T(8,128)}, f32[256,768]{1,0:T(8,128)S(1)}, u32[]{:S(2)}) copy-start(f32[256,768]{1,0:T(8,128)S(1)} %get-tuple-element.307.refs_5_) | copy-start | bytes 2359300
  464.9 40.7 %copy-start.10 = (f32[96,768]{1,0:T(8,128)S(1)}, f32[96,768]{1,0:T(8,128)}, u32[]{:S(2)}) copy-start(f32[96,768]{1,0:T(8,128)} %get-tuple-element.145) | copy-start | bytes 884740
  502.3 6.5 %copy-start.4 = (f32[256,768]{1,0:T(8,128)S(1)}, f32[256,768]{1,0:T(8,128)}, u32[]{:S(2)}) copy-start(f32[256,768]{1,0:T(8,128)} %get-tuple-element.135) | copy-start | bytes 2359300
  502.3 7.0 %copy-start.29 = (f32[8,1536]{1,0:T(8,128)S(1)}, f32[8,1536]{1,0:T(8,128)}, u32[]{:S(2)}) copy-start(f32[8,1536]{1,0:T(8,128)} %get-tuple-element.140) | copy-start | bytes 147460
  502.3 7.0 %copy-start.28 = (f32[8,1536]{1,0:T(8,128)S(1)}, f32[8,1536]{1,0:T(8,128)}, u32[]{:S(2)}) copy-start(f32[8,1536]{1,0:T(8,128)} %get-tuple-element.141) | copy-start | bytes 147460
  505.6 5.9 %copy-start.9 = (f32[96,1536]{1,0:T(8,128)S(1)}, f32[96,1536]{1,0:T(8,128)}, u32[]{:S(2)}) copy-start(f32[96,1536]{1,0:T(8,128)} %get-tuple-element.146) | copy-start | bytes 1769476
  507.1 5.4 copy-start.8
  509.2 4.9 copy-start.34
  509.2 5.7 %copy-start.33 = (f32[8,768]{1,0:T(8,128)S(1)}, f32[8,768]{1,0:T(8,128)}, u32[]{:S(2)}) copy-start(f32[8,768]{1,0:T(8,128)} %get-tuple-element.139) | copy-start | bytes 73732
  519.9 8.3 %copy-start.6 = (f32[1,768,96]{1,2,0:T(8,128)S(1)}, f32[1,768,96]{1,2,0:T(8,128)}, u32[]{:S(2)}) copy-start(f32[1,768,96]{1,2,0:T(8,128)} %get-tuple-element.254) | copy-start | bytes 884740
  519.9 10.2 %copy-start.5 = (f32[1,96,768]{2,1,0:T(8,128)S(1)}, f32[1,96,768]{2,1,0:T(8,128)}, u32[]{:S(2)}) copy-start(f32[1,96,768]{2,1,0:T(8,128)} %get-tuple-element.255) | copy-start | bytes 884740
  520.6 9.5 %copy-start.7 = (f32[1,96,768]{2,1,0:T(8,128)S(1)}, f32[1,96,768]{2,1,0:T(8,128)}, u32[]{:S(2)}) copy-start(f32[1,96,768]{2,1,0:T(8,128)} %get-tuple-element.257) | copy-start | bytes 884740
  520.6 10.3 %copy-start.19 = (f32[96,128]{1,0:T(8,128)S(1)}, f32[96,128]{1,0:T(8,128)}, u32[]{:S(2)}) copy-start(f32[96,128]{1,0:T(8,128)} %get-tuple-element.261) | copy-start | bytes 147460
  520.6 10.3 %copy-start.25 = (f32[96,64]{1,0:T(8,128)S(1)}, f32[96,64]{1,0:T(8,128)}, u32[]{:S(2)}) copy-start(f32[96,64]{1,0:T(8,128)} %get-tuple-element.265) | copy-start | bytes 73732
  520.7 10.3 %copy-start.17 = (f32[96,128]{1,0:T(8,128)S(1)}, f32[96,128]{1,0:T(8,128)}, u32[]{:S(2)}) copy-start(f32[96,128]{1,0:T(8,128)} %get-tuple-element.260) | copy-start | bytes 147460
  520.7 10.3 %copy-start.22 = (f32[96,64]{1,0:T(8,128)S(1)}, f32[96,64]{1,0:T(8,128)}, u32[]{:S(2)}) copy-start(f32[96,64]{1,0:T(8,128)} %get-tuple-element.264) | copy-start | bytes 73732
  520.7 10.4 %copy-start.16 = (f32[96,128]{1,0:T(8,128)S(1)}, f32[96,128]{1,0:T(8,128)}, u32[]{:S(2)}) copy-start(f32[96,128]{1,0:T(8,128)} %get-tuple-element.259) | copy-start | bytes 147460
  520.7 10.4 %copy-start.20 = (f32[96,64]{1,0:T(8,128)S(1)}, f32[96,64]{1,0:T(8,128)}, u32[]{:S(2)}) copy-start(f32[96,64]{1,0:T(8,128)} %get-tuple-element.263) | copy-start | bytes 73732
  520.7 10.4 %copy-start.23 = (f32[96,128]{1,0:T(8,128)S(1)}, f32[96,128]{1,0:T(8,128)}, u32[]{:S(2)}) copy-start(f32[96,128]{1,0:T(8,128)} %get-tuple-element.269) | copy-start | bytes 147460
  520.7 10.4 %copy-start.27 = (f32[96,64]{1,0:T(8,128)S(1)}, f32[96,64]{1,0:T(8,128)}, u32[]{:S(2)}) copy-start(f32[96,64]{1,0:T(8,128)} %get-tuple-element.273) | copy-start | bytes 73732
  520.7 10.4 %copy-start.21 = (f32[96,128]{1,0:T(8,128)S(1)}, f32[96,128]{1,0:T(8,128)}, u32[]{:S(2)}) copy-start(f32[96,128]{1,0:T(8,128)} %get-tuple-element.268) | copy-start | bytes 147460
  520.7 10.4 %copy-start.26 = (f32[96,64]{1,0:T(8,128)S(1)}, f32[96,64]{1,0:T(8,128)}, u32[]{:S(2)}) copy-start(f32[96,64]{1,0:T(8,128)} %get-tuple-element.272) | copy-start | bytes 73732
  520.7 10.4 %copy-start.18 = (f32[96,128]{1,0:T(8,128)S(1)}, f32[96,128]{1,0:T(8,128)}, u32[]{:S(2)}) copy-start(f32[96,128]{1,0:T(8,128)} %get-tuple-element.267) | copy-start | bytes 147460
  520.7 10.4 %copy-start.24 = (f32[96,64]{1,0:T(8,128)S(1)}, f32[96,64]{1,0:T(8,128)}, u32[]{:S(2)}) copy-start(f32[96,64]{1,0:T(8,128)} %get-tuple-element.271) | copy-start | bytes 73732
  525.4 8.2 %collective-permute-start.5 = (f32[16,3840]{1,0:T(8,128)S(1)}, f32[16,3840]{1,0:T(8,128)S(1)}, u32[]{:S(2)}, u32[]{:S(2)}) collective-permute-start(f32[16,3840]{1,0:T(8,128)S(1)} %pad_maximum_fusion.6), channel_id=1, source_target_pairs={{0,16},{4,20},{8,24},{12,28},{16,0},{20,4},{24,8},{28,12},{1,17},{... | collective-permute-start | bytes 737288 | tf_op jit(solution)/shard_map/ppermute | solution.py:1139
  528.2 3.0 copy-start.31
  528.2 3.0 copy-start.37
  531.3 7.4 %copy-start.14 = (f32[96,128]{1,0:T(8,128)S(1)}, f32[96,128]{1,0:T(8,128)}, u32[]{:S(2)}) copy-start(f32[96,128]{1,0:T(8,128)} %get-tuple-element.258) | copy-start | bytes 147460
  531.3 7.4 %copy-start.15 = (f32[96,64]{1,0:T(8,128)S(1)}, f32[96,64]{1,0:T(8,128)}, u32[]{:S(2)}) copy-start(f32[96,64]{1,0:T(8,128)} %get-tuple-element.262) | copy-start | bytes 73732
  531.3 8.8 %copy-start.12 = (f32[96,128]{1,0:T(8,128)S(1)}, f32[96,128]{1,0:T(8,128)}, u32[]{:S(2)}) copy-start(f32[96,128]{1,0:T(8,128)} %get-tuple-element.266) | copy-start | bytes 147460
  531.3 8.8 %copy-start.13 = (f32[96,64]{1,0:T(8,128)S(1)}, f32[96,64]{1,0:T(8,128)}, u32[]{:S(2)}) copy-start(f32[96,64]{1,0:T(8,128)} %get-tuple-element.270) | copy-start | bytes 73732
  531.3 24.8 %copy-start.1 = (f32[256,768]{1,0:T(8,128)S(1)}, f32[256,768]{1,0:T(8,128)}, u32[]{:S(2)}) copy-start(f32[256,768]{1,0:T(8,128)} %param.35) | copy-start | bytes 2359300
  533.6 4.9 collective-permute-start.6
  538.6 1.3 collective-permute-start.7
  540.0 5.2 collective-permute-start.8
  545.2 3.8 collective-permute-start.9

commit v4 on v3

v4 whole, which is shorter than its diff:
```python
import functools

import jax
import jax.numpy as jnp
from jax import lax
from jax.experimental import pallas as pl
from jax.experimental.pallas import tpu as pltpu
from jax.sharding import PartitionSpec as P

HD = 64
PAIR = 128
REACH = 384
EPS = 1e-06
FILL = -1e30
ROOT_HALF = 0.7071067811865476
INV_ROOT_TWO_PI = 0.3989422804014327
HIGHEST = lax.Precision.HIGHEST
F32 = jnp.float32
BF16 = jnp.bfloat16
MESH = pl.DeviceIdType.MESH
ANY = pl.BlockSpec(memory_space=pl.ANY)


def nn(left, right):
    return lax.dot_general(left, right, (((1,), (0,)), ((), ())), preferred_element_type=F32)


def nt(left, right):
    return lax.dot_general(left, right, (((1,), (1,)), ((), ())), preferred_element_type=F32)


def halves(array):
    middle = array.shape[1] // 2
    return array[:, :middle], array[:, middle:]


def row_norm(value):
    centered = value - jnp.mean(value, axis=-1, keepdims=True)
    scale = lax.rsqrt(jnp.mean(centered * centered, axis=-1, keepdims=True) + EPS)
    return centered * scale, scale


def row_norm_back(grad_hat, normed, scale):
    return scale * (
        grad_hat
        - jnp.mean(grad_hat, axis=-1, keepdims=True)
        - normed * jnp.mean(grad_hat * normed, axis=-1, keepdims=True)
    )


def head_mean(value, exact=False):
    wide = value.shape[1]
    rows = lax.broadcasted_iota(jnp.int32, (wide, wide), 0) // HD
    cols = lax.broadcasted_iota(jnp.int32, (wide, wide), 1) // HD
    spread = jnp.where(rows == cols, 1.0 / HD, 0.0).astype(BF16)
    high = value.astype(BF16)
    mean = nn(high, spread)
    if exact:
        mean += nn((value - high.astype(F32)).astype(BF16), spread)
    return mean


def head_norm(value):
    centered = value - head_mean(value, exact=True)
    scale = lax.rsqrt(head_mean(centered * centered) + EPS)
    return centered * scale, scale


def head_norm_back(grad_hat, normed, scale):
    return scale * (grad_hat - head_mean(grad_hat) - normed * head_mean(grad_hat * normed))


def only(array, part):
    return jnp.where(lax.broadcasted_iota(jnp.int32, (1, PAIR), 1) // HD == part, array, jnp.zeros_like(array))


def side(*parts):
    return jnp.concatenate(parts, axis=1)


def whole(shape):
    return pl.BlockSpec(shape, lambda step: (0,) * len(shape))


def column(height, wide, every=1, first=0):
    return pl.BlockSpec((height, wide), lambda step: (0, step * every + first))


def piece_of(layer, height, wide, first=0):
    return pl.BlockSpec((None, None, height, wide), lambda step: (layer, step, 0, first))


def slab(layer, height, wide):
    return pl.BlockSpec((None, height, wide), lambda step: (layer, 0, step))


def heads_of(layer):
    return pl.BlockSpec((None, None, HEADS, 3 * PAIR), lambda step: (step, layer, 0, 0))


def sheet(layer, height, wide):
    return pl.BlockSpec((None, height, wide), lambda step: (layer, 0, 0))


def shaped(shape, kind=BF16):
    return jax.ShapeDtypeStruct(shape, kind)


class Neighbours:
    def __init__(self):
        fsdp, tp = lax.axis_index("fsdp"), lax.axis_index("tp")
        self.size = lax.axis_size("tp")
        self.tp = tp
        self.x, self.y, self.core = ({"fsdp": jnp.bitwise_xor(fsdp, bit)} for bit in (2, 4, 1))

    def along(self, distance):
        return {"tp": lax.rem(self.tp + distance, self.size)}

    def greet(self):
        targets = [self.x, self.y, self.core] + [self.along(distance) for distance in range(1, self.size)]
        barrier = pltpu.get_barrier_semaphore()
        for target in targets:
            pl.semaphore_signal(barrier, inc=1, device_id=target, device_id_type=MESH)
        pl.semaphore_wait(barrier, len(targets))


class Plan:
    LINKS = {"x": (45.5e3, 1.5), "y": (45.5e3, 1.5), "z": (45.5e3, 2.2), "core": (600e3, 1.0)}

    def __init__(self, depth):
        self.depth, self.clock = depth, 0.0
        self.free, self.here, self.jobs, self.table = dict.fromkeys(self.LINKS, 0.0), {}, [], {}

    def add(self, rank, work, needs, copies, gives):
        self.jobs.append((rank, len(self.jobs), work, needs, copies, gives))
        self.jobs.sort(key=lambda job: job[:2])

    def carry(self, copies, gives):
        end = self.clock
        for link, size in copies:
            rate, latency = self.LINKS[link]
            self.free[link] = max(self.free[link], self.clock) + size / rate
            end = max(end, self.free[link] + latency)
        self.here[gives] = end

    def slot(self, *at):
        found = True
        while found:
            found = False
            for job in self.jobs:
                _, _, work, needs, copies, gives = job
                ready = all(self.here.get(need, float("inf")) <= self.clock for need in needs)
                if ready and all(self.free[link] - self.clock < self.depth for link, _ in copies):
                    self.carry(copies, gives)
                    self.table.setdefault(at, []).append(work)
                    self.jobs.remove(job)
                    found = True
                    break

    def wait(self, key, work, *at):
        self.slot(*at)
        while self.here.get(key, float("inf")) > self.clock:
            self.clock += 0.25
            self.slot(*at)
        self.table.setdefault(at, []).append(work)

    def spend(self, time):
        self.clock += time


def turn(index, pieces):
    if isinstance(index, int):
        return (index + 1) // 2 if index % 2 else (pieces - index // 2) % pieces
    return jnp.where(lax.rem(index, 2) == 1, (index + 1) // 2, lax.rem(pieces - index // 2, pieces))


class Gather:
    KINDS = 7

    def __init__(self, peers, shard, near, far, send, recv, local, near_out, far_out, stored):
        self.peers, self.shard, self.near, self.far = peers, shard, near, far
        self.send, self.recv, self.local = send, recv, local
        self.outs, self.stored = (near_out, far_out), stored
        self.chunk, self.wide = shard.shape
        self.pieces = near.shape[0]

    def at(self, piece, start, count, half=None):
        first, wide = (0, self.wide) if half is None else (half * (self.wide // 2), self.wide // 2)
        return self.near.at[piece, pl.ds(start * self.chunk, count * self.chunk), pl.ds(first, wide)]

    def copy(self, piece, kind, source, target, device):
        return pltpu.make_async_remote_copy(
            src_ref=source, dst_ref=target, send_sem=self.send.at[piece, kind], recv_sem=self.recv.at[piece, kind],
            device_id=device, device_id_type=MESH,
        )

    def copies(self, piece, stage):
        if stage == "z":
            return [self.copy(piece, 0, self.shard, self.at(piece, 0, 1), self.peers.along(piece))] if piece else []
        if stage == "first":
            half = self.wide // 2
            left = self.shard.at[:, pl.ds(0, half)] if piece == 0 else self.at(piece, 0, 1, 0)
            right = self.shard.at[:, pl.ds(half, half)] if piece == 0 else self.at(piece, 0, 1, 1)
            return [
                self.copy(piece, 1, left, self.at(piece, 1, 1, 0), self.peers.x),
                self.copy(piece, 2, right, self.at(piece, 2, 1, 1), self.peers.y),
            ]
        if stage == "second":
            return [
                self.copy(piece, 3, self.at(piece, 0, 2, 0), self.at(piece, 2, 2, 0), self.peers.y),
                self.copy(piece, 4, self.at(piece, 0, 1, 1), self.at(piece, 1, 1, 1), self.peers.x),
                self.copy(piece, 5, self.at(piece, 2, 1, 1), self.at(piece, 3, 1, 1), self.peers.x),
            ]
        return [self.copy(piece, 6, self.near.at[piece], self.far.at[piece], self.peers.core)]

    def start(self, piece, stage):
        for copy in self.copies(piece, stage):
            copy.start()

    def arrived(self, piece, stage):
        for copy in self.copies(piece, stage):
            copy.wait_recv()

    def store(self, piece):
        return [
            pltpu.make_async_copy(source.at[piece], target.at[piece], self.stored.at[piece, which])
            for which, (source, target) in enumerate(zip((self.near, self.far), self.outs))
        ]

    def own(self):
        return pltpu.make_async_copy(self.shard, self.at(0, 0, 1), self.local)

    def sent(self, piece):
        self.start(piece, "z")

    def landed(self, piece):
        self.arrived(piece, "z")
        self.start(piece, "first")

    def crossed(self, piece):
        self.arrived(piece, "first")
        self.start(piece, "second")

    def shared(self, piece):
        self.arrived(piece, "second")
        self.start(piece, "core")

    def need(self, piece):
        self.arrived(piece, "core")
        for copy in self.store(piece):
            copy.start()

    def jobs(self, plan, index):
        size = self.chunk * self.wide * 2
        for place in range(self.pieces):
            piece = turn(place, self.pieces)
            key = (index, piece)
            rank = index * self.pieces + place
            if piece:
                plan.add(rank, (self.sent, piece), [], [("z", size * self.pieces / (self.pieces - 1))], ("z", *key))
            both = lambda count: [("x", count * size), ("y", count * size)]
            plan.add(rank, (self.landed, piece), [("z", *key)] if piece else [], both(0.5), ("first", *key))
            plan.add(rank, (self.crossed, piece), [("first", *key)], both(1), ("second", *key))
            plan.add(rank, (self.shared, piece), [("second", *key)], [("core", 4 * size)], ("core", *key))

    def end(self):
        for piece in range(self.pieces):
            for stage in ("z", "first", "second", "core"):
                for copy in self.copies(piece, stage):
                    copy.wait_send()
            for copy in self.store(piece):
                copy.wait()


class Halo:
    def __init__(self, ref, rows, send, recv):
        self.ref, self.send, self.recv = ref, send, recv
        self.place, self.size = lax.axis_index("tp"), lax.axis_size("tp")
        spill = REACH - rows
        self.moves = [
            (1, pl.ds(REACH, rows), pl.ds(spill, rows)),
            (-1, pl.ds(REACH, rows), pl.ds(REACH + rows, rows)),
            (2, pl.ds(2 * rows, spill), pl.ds(0, spill)),
            (-2, pl.ds(REACH, spill), pl.ds(REACH + 2 * rows, spill)),
        ]

    def inside(self, distance):
        other = self.place + distance
        return jnp.logical_and(other >= 0, other < self.size)

    def copy(self, index):
        distance, source, target = self.moves[index]
        return pltpu.make_async_remote_copy(
            src_ref=self.ref.at[source, :], dst_ref=self.ref.at[target, :], send_sem=self.send.at[index],
            recv_sem=self.recv.at[index], device_id={"tp": self.place + distance}, device_id_type=MESH,
        )

    def begin(self):
        for index, (distance, _, target) in enumerate(self.moves):

            @pl.when(self.inside(distance))
            def _():
                self.copy(index).start()

            @pl.when(jnp.logical_not(self.inside(-distance)))
            def _():
                self.ref[target, :] = jnp.zeros((target.size, self.ref.shape[1]), BF16)

    def end(self, _=None):
        for index, (distance, _, _) in enumerate(self.moves):

            @pl.when(self.inside(distance))
            def _():
                self.copy(index).wait_send()

            @pl.when(self.inside(-distance))
            def _():
                self.copy(index).wait_recv()


def params(collective=None):
    if collective is None:
        return pltpu.CompilerParams()
    return pltpu.CompilerParams(collective_id=collective, has_side_effects=True)


LN_GAIN, LN_BIAS, OUT_BIAS, LAST_BIAS, FEATS = (0, 1), (2, 3), 4, 5, 6
PROJ_BIAS, HEAD_GAIN, HEAD_BIAS, HEADS = (0, 1, 2), (3, 4), 5, 6


def line(ref, row, start=0, wide=None):
    return ref[pl.ds(row, 1), pl.ds(start, wide or ref.shape[1] - start)]


def attend_work(
    a_ref, near_ref, far_ref, heads_ref, feats_ref, x_ref, q_ref, kv_ref, q_hat_ref, k_hat_ref, q_scale_ref, k_scale_ref,
    p_ref, o_ref, mid_ref, m_ref, mask_ref, acc_ref, opening, closing, hook,
):
    rows = q_ref.shape[0]
    half = near_ref.shape[0]

    @pl.when(opening)
    def _():
        acc_ref[...] = jnp.zeros_like(acc_ref)

    tile = lambda row, which: line(heads_ref, row, which * PAIR, PAIR)
    bias, (q_gain, k_gain), q_shift = PROJ_BIAS, HEAD_GAIN, HEAD_BIAS
    near, distant = halves(a_ref[...])
    own, own_far = halves(a_ref[REACH : REACH + rows, :])
    kv = nn(near, near_ref[:, PAIR : 4 * PAIR]) + nn(distant, far_ref[:, PAIR : 4 * PAIR])
    kv += side(tile(bias[1], 0), tile(bias[2], 0), tile(bias[1], 1) + tile(bias[2], 2))
    q = side(
        nn(own, near_ref[:, :PAIR]) + nn(own_far, far_ref[:, :PAIR]),
        nn(own, near_ref[:, 4 * PAIR : 5 * PAIR]) + nn(own_far, far_ref[:, 4 * PAIR : 5 * PAIR]),
    ) + line(heads_ref, bias[0], 0, 2 * PAIR)
    q_hat, q_scale = head_norm(q)
    k_hat, k_scale = head_norm(side(kv[:, :PAIR], kv[:, 2 * PAIR :]))
    qn = (q_hat * line(heads_ref, q_gain, 0, 2 * PAIR) + line(heads_ref, q_shift, 0, 2 * PAIR)).astype(BF16)
    qn = side(qn[:, :PAIR], only(qn[:, PAIR:], 0))
    kn = (k_hat * line(heads_ref, k_gain, 0, 2 * PAIR)).astype(BF16)
    v = kv[:, PAIR:].astype(BF16)
    low = lax.broadcasted_iota(jnp.int32, (1, PAIR), 1) < HD
    first, second = kn[:, :PAIR], jnp.where(low, kn[:, PAIR:], v[:, PAIR:])
    values = v[:, :PAIR]
    q_ref[...] = qn
    kv_ref[...] = side(first, values, second)
    q_hat_ref[...] = q_hat.astype(BF16)
    k_hat_ref[...] = k_hat.astype(BF16)
    q_scale_ref[...] = q_scale.astype(BF16)
    k_scale_ref[...] = k_scale.astype(BF16)
    hook(1)
    values_t, second_t = values.T, second.T
    mixed = []
    for head in range(3):
        if head:
            hook(head + 1)
        keys = (first, first, second)[head]
        query = only(qn[:, PAIR * (head // 2) : PAIR * (head // 2 + 1)] * HD ** (-0.5), head % 2).astype(BF16)
        scores = nt(keys, query) + mask_ref[...]
        weights = jnp.exp(scores - jnp.max(scores, axis=0, keepdims=True))
        total = jnp.sum(weights, axis=0, keepdims=True)
        probs = (weights * (1.0 / total)).astype(BF16)
        p_ref[head] = probs
        mixed.append(nn((values_t[:HD], values_t[HD:], second_t[HD:])[head], probs))
    o = jnp.concatenate([jnp.zeros_like(mixed[2]), mixed[2], mixed[0], mixed[1]], axis=0).T.astype(BF16)
    o_ref[...] = o
    acc_ref[:, :half] += nt(o, near_ref[:, 4 * PAIR :])
    acc_ref[:, half:] += nt(o, far_ref[:, 4 * PAIR :])

    @pl.when(closing)
    def _():
        mid = x_ref[...] + (acc_ref[...] + line(feats_ref, OUT_BIAS))
        mid_ref[...] = mid
        hat, _ = row_norm(mid)
        m_ref[...] = (hat * line(feats_ref, LN_GAIN[1]) + line(feats_ref, LN_BIAS[1])).astype(BF16)


def mlp_work(
    m_ref, mid_ref, near_ref, far_ref, up_shift, feats_ref, act_ref, slope_ref, x2_ref, acc_ref, opening, closing, hook,
):
    half = near_ref.shape[0]
    wide = act_ref.shape[1]

    @pl.when(opening)
    def _():
        acc_ref[...] = jnp.zeros_like(acc_ref)

    near, distant = halves(m_ref[...])
    hidden = nn(near, near_ref[:, :wide]) + nn(distant, far_ref[:, :wide]) + up_shift
    hook(1)
    phi = 0.5 * (1.0 + lax.erf(hidden * ROOT_HALF))
    act = (hidden * phi).astype(BF16)
    act_ref[...] = act
    slope_ref[...] = (phi + hidden * jnp.exp(-0.5 * hidden * hidden) * INV_ROOT_TWO_PI).astype(BF16)
    acc_ref[:, :half] += nt(act, near_ref[:, wide:])
    acc_ref[:, half:] += nt(act, far_ref[:, wide:])

    @pl.when(closing)
    def _():
        x2_ref[...] = mid_ref[...] + (acc_ref[...] + line(feats_ref, LAST_BIAS))


def norm_rows(x, feats_ref):
    hat, _ = row_norm(x)
    return (hat * line(feats_ref, LN_GAIN[0]) + line(feats_ref, LN_BIAS[0])).astype(BF16)


def quiet(slot):
    pass


def attend_kernel(
    a_ref, near_ref, far_ref, heads_ref, feats_ref, x_ref, seg_k_ref, seg_q_ref, *rest
):
    step = pl.program_id(0)
    mask_ref = rest[-2]

    @pl.when(step == 0)
    def _():
        mask_ref[...] = jnp.where(seg_k_ref[...] == seg_q_ref[...], 0.0, FILL)

    attend_work(
        a_ref, near_ref, far_ref, heads_ref, feats_ref, x_ref, *rest, step == 0, step == pl.num_programs(0) - 1, quiet
    )


def attend_shapes(rows, window):
    return [
        (rows, 2 * PAIR), (window, 3 * PAIR), (rows, 2 * PAIR), (window, 2 * PAIR), (rows, 2 * PAIR), (window, 2 * PAIR),
    ]


def attend(a_win, near, far, heads, feats, x, seg_k, seg_q, layer):
    window, width = a_win.shape
    rows = x.shape[0]
    half = width // 2
    pieces = near.shape[1]
    outs = attend_shapes(rows, window)
    return pl.pallas_call(
        attend_kernel,
        grid=(pieces,),
        in_specs=[
            whole((window, width)), piece_of(0, half, 6 * PAIR), piece_of(0, half, 6 * PAIR), heads_of(layer), sheet(layer, FEATS, width),
            whole((rows, width)), whole((window, 1)), whole((1, rows)),
        ],
        out_specs=[column(*shape) for shape in outs]
        + [pl.BlockSpec((3, window, rows), lambda step: (step, 0, 0)), column(rows, 2 * PAIR)] + [whole((rows, width))] * 2,
        out_shape=[shaped((height, pieces * wide)) for height, wide in outs]
        + [shaped((3 * pieces, window, rows)), shaped((rows, pieces * 2 * PAIR)), shaped((rows, width), F32), shaped((rows, width))],
        scratch_shapes=[pltpu.VMEM((window, rows), F32), pltpu.VMEM((rows, width), F32)],
        name="attend",
    )(a_win, near, far, heads, feats, x, seg_k, seg_q)


def mlp_kernel(m_ref, mid_ref, near_ref, far_ref, up_shift_ref, feats_ref, *rest):
    step = pl.program_id(0)
    mlp_work(
        m_ref, mid_ref, near_ref, far_ref, up_shift_ref[...], feats_ref, *rest, step == 0, step == pl.num_programs(0) - 1, quiet
    )


def mlp(m, mid, near, far, up_shift, feats, layer):
    rows, width = mid.shape
    half = width // 2
    _, pieces, _, wide = up_shift.shape
    hidden = pieces * wide
    full = whole((rows, width))
    return pl.pallas_call(
        mlp_kernel,
        grid=(pieces,),
        in_specs=[
            full, full, piece_of(0, half, 2 * wide), piece_of(0, half, 2 * wide), piece_of(layer, 1, wide), sheet(layer, FEATS, width),
        ],
        out_specs=[column(rows, wide), column(rows, wide), full],
        out_shape=[shaped((rows, hidden)), shaped((rows, hidden)), shaped((rows, width), F32)],
        scratch_shapes=[pltpu.VMEM((rows, width), F32)],
        name="mlp",
    )(m, mid, near, far, up_shift, feats)


def forward_kernel(
    a_ref, x_ref, heads_ref, feats_ref, up_shift_ref, seg_k_ref, seg_q_ref, attn_shard_ref, mlp_shard_ref,
    q_ref, kv_ref, q_hat_ref, k_hat_ref, q_scale_ref, k_scale_ref, p_ref, o_ref, act_ref, slope_ref, mid_ref, m_ref, x2_ref,
    a_win_out, attn_near_out, attn_far_out, mlp_near_out, mlp_far_out,
    mask_ref, acc_ref, now_ref, a_win_ref, kept, attn_near, attn_far, mlp_near, mlp_far, send, recv, local, stored, halo_send, halo_recv,
):
    layers, pieces, rows = attn_near.shape[0], attn_near.shape[1], a_ref.shape[0]
    step = pl.program_id(0)
    peers = Neighbours()
    halo = lambda layer: Halo(a_win_ref.at[layer], rows, halo_send.at[layer], halo_recv.at[layer])
    keep_window = lambda layer: pltpu.make_async_copy(a_win_ref.at[layer], a_win_out.at[layer], kept.at[layer])

    def window(layer):
        halo(layer).end()
        keep_window(layer).start()

    gathers = []
    for layer in range(layers):
        for which, (shard, near, far, near_out, far_out) in enumerate((
            (attn_shard_ref, attn_near, attn_far, attn_near_out, attn_far_out),
            (mlp_shard_ref, mlp_near, mlp_far, mlp_near_out, mlp_far_out),
        )):
            index = 2 * layer + which
            gathers.append(
                Gather(
                    peers, shard.at[layer], near.at[layer], far.at[layer], send.at[index], recv.at[index], local.at[index],
                    near_out.at[layer], far_out.at[layer], stored.at[index],
                )
            )

    plan = Plan(5.0)
    for index, gather in enumerate(gathers):
        gather.jobs(plan, index)
    halo_size = a_ref.shape[1] * 2 * 2 * rows
    plan.spend(2.5)
    plan.slot(0, 0)
    for layer in range(layers):
        plan.carry([("z", halo_size)], ("halo", layer))
        first = 1 + 2 * layer * pieces
        plan.wait(("halo", layer), (window, layer), *((first, 0) if layer else (0, 1)))
        for index in range(pieces):
            piece = turn(index, pieces)
            plan.wait(("core", 2 * layer, piece), (gathers[2 * layer].need, piece), first + index, 0)
            for slot, time in enumerate((2.0, 1.4, 1.4)):
                plan.spend(time)
                plan.slot(first + index, slot + 1)
            plan.spend(1.4)
        first += pieces
        for index in range(pieces):
            piece = turn(index, pieces)
            plan.wait(("core", 2 * layer + 1, piece), (gathers[2 * layer + 1].need, piece), first + index, 0)
            plan.spend(1.0)
            plan.slot(first + index, 1)
            plan.spend(1.5)
    table = plan.table

    def run(at, slot):
        if (at, slot) in table:

            @pl.when(step == at)
            def _():
                for work, piece in table[at, slot]:
                    work(piece)

    @pl.when(step == 0)
    def _():
        peers.greet()
        mask_ref[...] = jnp.where(seg_k_ref[...] == seg_q_ref[...], 0.0, FILL)
        now_ref[...] = x_ref[...]
        a_win_ref[0, REACH : REACH + rows, :] = a_ref[...]
        for gather in gathers:
            gather.own().start()
        for gather in gathers:
            gather.own().wait()

    run(0, 0)

    @pl.when(step == 0)
    def _():
        halo(0).begin()

    run(0, 1)

    count = jnp.maximum(step - 1, 0)
    layer = count // (2 * pieces)
    inner = lax.rem(count, 2 * pieces)
    index = lax.rem(inner, pieces)
    piece = turn(index, pieces)
    steps_of = lambda which: [
        1 + (2 * layer + which) * pieces + index for layer in range(layers) for index in range(pieces)
    ]

    @pl.when(jnp.logical_and(step > 0, inner < pieces))
    def _():
        def hook(slot):
            for at in steps_of(0):
                run(at, slot)

        hook(0)
        attend_work(
            a_win_ref.at[layer], attn_near.at[layer, piece], attn_far.at[layer, piece], heads_ref.at[piece, layer],
            feats_ref.at[layer], now_ref,
            q_ref, kv_ref, q_hat_ref, k_hat_ref, q_scale_ref, k_scale_ref, p_ref, o_ref, mid_ref.at[layer], m_ref.at[layer],
            mask_ref, acc_ref, index == 0, index == pieces - 1, hook,
        )

    @pl.when(inner >= pieces)
    def _():
        def hook(slot):
            for at in steps_of(1):
                run(at, slot)

        hook(0)
        mlp_work(
            m_ref.at[layer], mid_ref.at[layer], mlp_near.at[layer, piece], mlp_far.at[layer, piece],
            up_shift_ref[layer, piece], feats_ref.at[layer], act_ref, slope_ref, now_ref, acc_ref, index == 0,
            index == pieces - 1, hook,
        )

        @pl.when(index == pieces - 1)
        def _():
            x2_ref[layer] = now_ref[...]

            @pl.when(layer + 1 < layers)
            def _():
                a_win_ref[layer + 1, REACH : REACH + rows, :] = norm_rows(now_ref[...], feats_ref.at[layer + 1])
                halo(layer + 1).begin()

    @pl.when(step == pl.num_programs(0) - 1)
    def _():
        for gather in gathers:
            gather.end()
        for layer in range(layers):
            keep_window(layer).wait()


def forward(a_own, x, heads, feats, up_shift, seg_k, seg_q, attn_shards, mlp_shards):
    rows, width = x.shape
    layers, chunk, wide = mlp_shards.shape
    half = width // 2
    window = rows + 2 * REACH
    _, pieces, _, part = up_shift.shape
    hidden = pieces * part

    def attend_at(step):
        count = jnp.maximum(step - 1, 0)
        layer, inner = count // (2 * pieces), lax.rem(count, 2 * pieces)
        return layer, turn(jnp.minimum(inner, pieces - 1), pieces)

    def mlp_at(step):
        count = jnp.maximum(step - 1, 0)
        layer, inner = count // (2 * pieces), lax.rem(count, 2 * pieces)
        done = jnp.where(inner >= pieces, layer * pieces + inner - pieces, jnp.maximum(layer * pieces - 1, 0))
        return done // pieces, turn(lax.rem(done, pieces), pieces)

    def attend_block(height, wide):
        return pl.BlockSpec((None, height, wide), lambda step: (attend_at(step)[0], 0, attend_at(step)[1]))

    mlp_block = pl.BlockSpec((None, rows, part), lambda step: (mlp_at(step)[0], 0, mlp_at(step)[1]))
    heads_at = lambda step: attend_at(step)[0] * pieces + attend_at(step)[1]
    once = lambda shape: pl.BlockSpec(shape, lambda step: (0,) * len(shape), pipeline_mode=pl.Buffered(1))
    outs = attend_shapes(rows, window) + [(rows, 2 * PAIR)]
    specs = [attend_block(*shape) for shape in outs]
    shapes = [shaped((layers, height, pieces * wide)) for height, wide in outs]
    specs.insert(6, pl.BlockSpec((3, window, rows), lambda step: (heads_at(step), 0, 0)))
    shapes.insert(6, shaped((3 * layers * pieces, window, rows)))
    held = [((layers, rows, width), F32), ((layers, rows, width), BF16), ((layers, rows, width), F32)]
    weights = [(layers, pieces, half, 6 * PAIR)] * 2 + [(layers, pieces, half, wide)] * 2
    semaphores = pltpu.SemaphoreType.DMA((2 * layers, pieces, Gather.KINDS))
    inputs = (a_own, x, heads, feats, up_shift, seg_k, seg_q, attn_shards, mlp_shards)
    return pl.pallas_call(
        forward_kernel,
        grid=(1 + 2 * layers * pieces,),
        in_specs=[once(item.shape) for item in inputs],
        out_specs=specs + [mlp_block] * 2 + [once(shape) for shape, _ in held] + [ANY] * 5,
        out_shape=shapes + [shaped((layers, rows, hidden))] * 2 + [shaped(*item) for item in held]
        + [shaped(shape) for shape in [(layers, window, width)] + weights],
        scratch_shapes=[
            pltpu.VMEM((window, rows), F32), pltpu.VMEM((rows, width), F32), pltpu.VMEM((rows, width), F32),
            pltpu.VMEM((layers, window, width), BF16), pltpu.SemaphoreType.DMA((layers,)),
            *[pltpu.VMEM(shape, BF16) for shape in weights], semaphores, semaphores, pltpu.SemaphoreType.DMA((2 * layers,)),
            pltpu.SemaphoreType.DMA((2 * layers, pieces, 2)), pltpu.SemaphoreType.DMA((layers, 4)),
            pltpu.SemaphoreType.DMA((layers, 4)),
        ],
        compiler_params=params(20),
        name="forward",
    )(*inputs)


def mlp_back_kernel(*refs):
    step = pl.program_id(0)
    mlp_back_work(*refs, step == 0, step == pl.num_programs(0) - 1)


def mlp_back_work(
    g_ref, down_near_ref, down_far_ref, slope_ref, up_near_ref, up_far_ref, mid_ref, feats_ref,
    gz_ref, gh_ref, up_shift_grad_ref, g1_ref, gr_ref, small_ref, acc_ref, opening, closing,
):
    half = up_near_ref.shape[0]

    @pl.when(opening)
    def _():
        gz_ref[...] = g_ref[...].astype(BF16)
        acc_ref[...] = jnp.zeros_like(acc_ref)

    near, distant = halves(gz_ref[...])
    gh = ((nn(near, down_near_ref[...]) + nn(distant, down_far_ref[...])) * slope_ref[...].astype(F32)).astype(BF16)
    gh_ref[...] = gh
    up_shift_grad_ref[...] = jnp.sum(gh.astype(F32), axis=0, keepdims=True)
    acc_ref[:, :half] += nt(gh, up_near_ref[...])
    acc_ref[:, half:] += nt(gh, up_far_ref[...])

    @pl.when(closing)
    def _():
        gm = acc_ref[...]
        hat, scale = row_norm(mid_ref[...])
        g1 = g_ref[...] + row_norm_back(gm * line(feats_ref, LN_GAIN[1]), hat, scale)
        gr = g1.astype(BF16)
        g1_ref[...] = g1
        gr_ref[...] = gr
        small_ref[...] = jnp.zeros_like(small_ref)
        small_ref[0:1, :] = jnp.sum(gz_ref[...].astype(F32), axis=0, keepdims=True)
        small_ref[1:2, :] = jnp.sum(gr.astype(F32), axis=0, keepdims=True)
        small_ref[2:3, :] = jnp.sum(gm * hat, axis=0, keepdims=True)
        small_ref[3:4, :] = jnp.sum(gm, axis=0, keepdims=True)


def mlp_back(grad, near, far, slope, mid, feats, layer, index):
    rows, width = grad.shape
    half = width // 2
    hidden = slope.shape[2]
    pieces = near.shape[1]
    wide = hidden // pieces
    full = whole((rows, width))
    return pl.pallas_call(
        mlp_back_kernel,
        grid=(pieces,),
        in_specs=[
            full, piece_of(index, half, wide, 1), piece_of(index, half, wide, 1), slab(index, rows, wide),
            piece_of(index, half, wide), piece_of(index, half, wide), sheet(index, rows, width), sheet(layer, FEATS, width),
        ],
        out_specs=[full, column(rows, wide), column(1, wide), full, full, whole((8, width))],
        out_shape=[
            shaped((rows, width)), shaped((rows, hidden)), shaped((1, hidden), F32), shaped((rows, width), F32),
            shaped((rows, width)), shaped((8, width), F32),
        ],
        scratch_shapes=[pltpu.VMEM((rows, width), F32)],
        cost_estimate=pl.CostEstimate(
            flops=4 * rows * width * hidden, bytes_accessed=4 * width * hidden, transcendentals=0
        ),
        name="mlp_back",
    )(grad, near, far, slope, near, far, mid, feats)


def attend_back_kernel(*refs):
    attend_back_work(*refs, quiet)


def attend_back_work(
    gr_ref, q_ref, kv_ref, q_hat_ref, k_hat_ref, q_scale_ref, k_scale_ref, p_ref, near_ref, far_ref, heads_ref,
    gq_ref, gkv_ref, mine_ref, left_ref, right_ref, small_ref, acc_ref, hook,
):
    rows = gr_ref.shape[0]
    half = near_ref.shape[0]
    step = pl.program_id(0)

    @pl.when(step == 0)
    def _():
        acc_ref[...] = jnp.zeros_like(acc_ref)

    near, distant = halves(gr_ref[...])
    go = (nn(near, near_ref[:, 4 * PAIR :]) + nn(distant, far_ref[:, 4 * PAIR :])).astype(BF16)
    qn, kv = q_ref[...], kv_ref[...]
    first, values, second = kv[:, :PAIR], kv[:, PAIR : 2 * PAIR], kv[:, 2 * PAIR :]
    first_t, second_t = first.T, second.T
    grad_q, grad_k, grad_v = [], [], []
    for head in range(3):
        hook(head)
        go_head = only(go[:, PAIR:], head) if head < 2 else only(go[:, :PAIR], 1)
        query = only(qn[:, PAIR * (head // 2) : PAIR * (head // 2 + 1)] * HD ** (-0.5), head % 2).astype(BF16)
        stored = p_ref[head]
        probs = stored.astype(F32)
        grad_probs = nt((values, values, second)[head], go_head)
        delta = jnp.sum(probs * grad_probs, axis=0, keepdims=True)
        grad_scores = (probs * (grad_probs - delta)).astype(BF16)
        grad_v.append(nn(stored, go_head))
        grad_k.append(nn(grad_scores, query))
        grad_q.append(nn((first_t[:HD], first_t[HD:], second_t[:HD])[head], grad_scores))
    hook(3)
    zero = jnp.zeros_like(grad_q[2])
    grad_q = (jnp.concatenate(grad_q + [zero], axis=0) * HD ** (-0.5)).T
    grad_k = side(grad_k[0] + grad_k[1], grad_k[2])
    pair_v, last_v = grad_v[0] + grad_v[1], grad_v[2]
    q_hat = q_hat_ref[...].astype(F32)
    k_hat = k_hat_ref[...].astype(F32)
    gain = lambda which: line(heads_ref, HEAD_GAIN[which], 0, 2 * PAIR)
    gq = head_norm_back(grad_q * gain(0), q_hat, q_scale_ref[...].astype(F32)).astype(BF16)
    gk = head_norm_back(grad_k * gain(1), k_hat, k_scale_ref[...].astype(F32)).astype(BF16)
    gkv = side(gk[:, :PAIR], pair_v.astype(BF16), gk[:, PAIR:] + last_v.astype(BF16))
    gq_ref[...] = gq
    gkv_ref[...] = gkv
    total = lambda value: jnp.sum(value.astype(F32), axis=0, keepdims=True)
    small_ref[...] = jnp.zeros_like(small_ref)
    small_ref[0:1, : 2 * PAIR] = total(grad_q * q_hat)
    small_ref[1:2, : 2 * PAIR] = total(grad_k * k_hat)
    small_ref[2:3, : 2 * PAIR] = total(grad_q)
    small_ref[3:4, : 2 * PAIR] = total(gq)
    small_ref[4:5, : 2 * PAIR] = total(gk)
    small_ref[5:6, :PAIR] = total(pair_v.astype(BF16))
    small_ref[5:6, 2 * PAIR :] = total(last_v.astype(BF16))
    acc_ref[:, :half] += nt(gkv, near_ref[:, PAIR : 4 * PAIR])
    acc_ref[:, half:] += nt(gkv, far_ref[:, PAIR : 4 * PAIR])
    own = slice(REACH, REACH + rows)
    for ref, cols in ((near_ref, slice(0, half)), (far_ref, slice(half, 2 * half))):
        acc_ref[own, cols] += nt(gq[:, :PAIR], ref[:, :PAIR]) + nt(gq[:, PAIR:], ref[:, 4 * PAIR : 5 * PAIR])

    @pl.when(step == pl.num_programs(0) - 1)
    def _():
        left_ref[...] = acc_ref[:REACH, :].astype(BF16)
        mine_ref[...] = acc_ref[own, :]
        right_ref[...] = acc_ref[REACH + rows :, :].astype(BF16)


def attend_back_specs(rows, width, pieces, layer, index):
    half = width // 2
    window = rows + 2 * REACH
    full = whole((rows, width))
    in_specs = [
        full, *[slab(index, *shape) for shape in attend_shapes(rows, window)],
        pl.BlockSpec((3, window, rows), lambda step: (index * pieces + step, 0, 0)), piece_of(index, half, 6 * PAIR),
        piece_of(index, half, 6 * PAIR), heads_of(layer),
    ]
    out_specs = [
        column(rows, 2 * PAIR), column(window, 3 * PAIR), full, whole((REACH, width)), whole((REACH, width)), column(8, 3 * PAIR),
    ]
    out_shape = [
        shaped((rows, pieces * 2 * PAIR)), shaped((window, pieces * 3 * PAIR)), shaped((rows, width), F32),
        shaped((REACH, width)), shaped((REACH, width)), shaped((8, pieces * 3 * PAIR), F32),
    ]
    cost = pl.CostEstimate(
        flops=2 * window * width * width * 2 + 20 * window * rows * width * 2,
        bytes_accessed=20 * window * width,
        transcendentals=0,
    )
    return in_specs, out_specs, out_shape, [pltpu.VMEM((window, width), F32)], cost


def attend_back(gr, stored, near, far, heads, layer, index):
    rows, width = gr.shape
    pieces = near.shape[1]
    in_specs, out_specs, out_shape, scratch, cost = attend_back_specs(rows, width, pieces, layer, index)
    return pl.pallas_call(
        attend_back_kernel,
        grid=(pieces,),
        in_specs=in_specs,
        out_specs=out_specs,
        out_shape=out_shape,
        scratch_shapes=scratch,
        cost_estimate=cost,
        name="attend_back",
    )(gr, *stored, near, far, heads)


def attn_weight_kernel(a_ref, gq_ref, gkv_ref, gr_ref, o_ref, keep_ref, send_ref, a_t_ref, gr_t_ref):
    rows = gq_ref.shape[0]
    half = keep_ref.shape[0]

    @pl.when(pl.program_id(0) == 0)
    def _():
        a_t_ref[...] = a_ref[...].T
        gr_t_ref[...] = gr_ref[...].T

    for part, ref in ((slice(0, half), keep_ref), (slice(half, 2 * half), send_ref)):
        from_q = nn(a_t_ref[part, REACH : REACH + rows], gq_ref[...])
        from_o = nn(gr_t_ref[part, :], o_ref[...])
        ref[:, :PAIR] = from_q[:, :PAIR].astype(BF16)
        ref[:, PAIR : 4 * PAIR] = nn(a_t_ref[part, :], gkv_ref[...]).astype(BF16)
        ref[:, 4 * PAIR : 5 * PAIR] = (from_q[:, PAIR:] + from_o[:, :PAIR]).astype(BF16)
        ref[:, 5 * PAIR :] = from_o[:, PAIR:].astype(BF16)


def attn_weight_grads(a_win, gq, gkv, gr, o):
    _, window, width = a_win.shape
    rows = gr.shape[0]
    half = width // 2
    pieces = gq.shape[1] // (2 * PAIR)
    out = column(half, 6 * PAIR)
    return pl.pallas_call(
        attn_weight_kernel,
        grid=(pieces,),
        in_specs=[
            sheet(0, window, width), column(rows, 2 * PAIR), column(window, 3 * PAIR), whole((rows, width)),
            slab(0, rows, 2 * PAIR),
        ],
        out_specs=[out, out],
        out_shape=[shaped((half, pieces * 6 * PAIR))] * 2,
        scratch_shapes=[pltpu.VMEM((width, window), BF16), pltpu.VMEM((width, rows), BF16)],
        cost_estimate=pl.CostEstimate(
            flops=2 * width * width * (2 * window + 2 * rows), bytes_accessed=8 * width * width, transcendentals=0
        ),
        name="attn_weight_grads",
    )(a_win, gq, gkv, gr, o)


def mlp_weight_kernel(m_ref, gh_ref, gz_ref, act_ref, keep_ref, send_ref, m_t_ref, gz_t_ref):
    half = keep_ref.shape[0]
    wide = gh_ref.shape[1]

    @pl.when(pl.program_id(0) == 0)
    def _():
        m_t_ref[...] = m_ref[...].T
        gz_t_ref[...] = gz_ref[...].T

    for part, ref in ((slice(0, half), keep_ref), (slice(half, 2 * half), send_ref)):
        ref[:, :wide] = nn(m_t_ref[part, :], gh_ref[...]).astype(BF16)
        ref[:, wide:] = nn(gz_t_ref[part, :], act_ref[...]).astype(BF16)


def mlp_weight_grads(m, gh, gz, act):
    _, rows, width = m.shape
    half = width // 2
    hidden = gh.shape[1]
    pieces = lax.axis_size("tp")
    wide = hidden // pieces
    out = column(half, 2 * wide)
    return pl.pallas_call(
        mlp_weight_kernel,
        grid=(pieces,),
        in_specs=[sheet(0, rows, width), column(rows, wide), whole((rows, width)), slab(0, rows, wide)],
        out_specs=[out, out],
        out_shape=[shaped((half, 2 * hidden))] * 2,
        scratch_shapes=[pltpu.VMEM((width, rows), BF16), pltpu.VMEM((width, rows), BF16)],
        cost_estimate=pl.CostEstimate(
            flops=4 * width * hidden * rows, bytes_accessed=4 * width * hidden, transcendentals=0
        ),
        name="mlp_weight_grads",
    )(m, gh, gz, act)


class Scatter:
    KINDS = 7

    def __init__(self, out, away, keep, core, first, second, given, send, recv):
        self.out, self.away, self.keep, self.core_in = out, away, keep, core
        self.first_in, self.second_in, self.given, self.send, self.recv = first, second, given, send, recv
        self.chunk, self.wide = out.shape
        self.half = self.wide // 2
        self.pieces = keep.shape[0]
        self.near = Neighbours()

    def copy(self, piece, kind, source, target, device):
        return pltpu.make_async_remote_copy(
            src_ref=source, dst_ref=target, send_sem=self.send.at[piece, kind], recv_sem=self.recv.at[piece, kind],
            device_id=device, device_id_type=MESH,
        )

    def copies(self, piece, stage):
        c, left, right = self.chunk, pl.ds(0, self.half), pl.ds(self.half, self.half)
        rows = lambda start, count=1: pl.ds(start * c, count * c)
        if stage == "core":
            return [self.copy(piece, 0, self.away.at[piece], self.core_in.at[piece], self.near.core)]
        if stage == "first":
            source, target = self.keep.at[piece], self.first_in.at[piece]
            return [
                self.copy(piece, 1, source.at[rows(2, 2), left], target.at[:, left], self.near.y),
                self.copy(piece, 2, source.at[rows(1), right], target.at[rows(0), right], self.near.x),
                self.copy(piece, 3, source.at[rows(3), right], target.at[rows(1), right], self.near.x),
            ]
        if stage == "second":
            source, target = self.keep.at[piece], self.second_in.at[piece]
            return [
                self.copy(piece, 4, source.at[rows(1), left], target.at[:, left], self.near.x),
                self.copy(piece, 5, source.at[rows(2), right], target.at[:, right], self.near.y),
            ]
        owner = self.near.along(self.pieces - piece)
        return [self.copy(piece, 6, self.keep.at[piece, rows(0), :], self.given.at[piece], owner)]

    def start(self, piece, stage):
        for copy in self.copies(piece, stage):
            copy.start()

    def arrived(self, piece, stage):
        for copy in self.copies(piece, stage):
            copy.wait_recv()

    def add(self, piece, start, count, cols, source):
        step = 32

        @pl.loop(0, count * self.chunk // step)
        def _(index):
            row = pl.multiple_of(index * step, step)
            into = (piece, pl.ds(start * self.chunk + row, step), cols)
            self.keep[into] = self.keep[into] + source[pl.ds(row, step), cols]

    def place(self, index):
        return lax.rem(index + 1, self.pieces)

    def core(self, index):
        self.start(self.place(index), "core")

    def first(self, index):
        piece = self.place(index)
        self.arrived(piece, "core")
        self.add(piece, 0, 4, pl.ds(0, self.wide), self.core_in.at[piece])
        self.start(piece, "first")

    def second(self, index):
        piece = self.place(index)
        left, right = pl.ds(0, self.half), pl.ds(self.half, self.half)
        self.arrived(piece, "first")
        source = self.first_in.at[piece]
        self.add(piece, 0, 2, left, source)
        self.add(piece, 0, 1, right, source)
        self.add(piece, 2, 1, right, source.at[pl.ds(self.chunk, self.chunk)])
        self.start(piece, "second")

    def last(self, index):
        piece = (index + 1) % self.pieces
        self.arrived(piece, "second")
        kept = pl.ds(0, self.chunk)
        total = self.keep[piece, kept, :].astype(F32) + self.second_in[piece].astype(F32)
        if piece:
            self.keep[piece, kept, :] = total.astype(BF16)
            self.start(piece, "give")
        else:
            for other in range(1, self.pieces):
                self.arrived(other, "give")
                total += self.given[other].astype(F32)
            self.out[...] = total

    def done(self):
        for piece in range(self.pieces):
            for stage in ("core", "first", "second", "give"):
                if stage != "give" or piece:
                    for copy in self.copies(piece, stage):
                        copy.wait_send()


def scatter_specs(pieces, chunk, wide):
    buffer = lambda rows: pltpu.VMEM((pieces, rows * chunk, wide), BF16)
    semaphores = pltpu.SemaphoreType.DMA((pieces, Scatter.KINDS))
    return shaped((chunk, wide), F32), [buffer(4), buffer(4), buffer(4), buffer(2), buffer(1), buffer(1), semaphores, semaphores]


def at_step(index, work):
    @pl.when(pl.program_id(0) == index)
    def _():
        work()


def attend_back_scatter_kernel(
    gr_ref, q_ref, kv_ref, q_hat_ref, k_hat_ref, q_scale_ref, k_scale_ref, p_ref, near_ref, far_ref, heads_ref,
    m_ref, gh_ref, gz_ref, act_ref, gq_ref, gkv_ref, mine_ref, left_ref, right_ref, small_ref, out_ref,
    acc_ref, m_t_ref, gz_t_ref, *scratch,
):
    scatter = Scatter(out_ref, *scratch)
    pieces, half = scatter.pieces, near_ref.shape[0]
    wide = gh_ref.shape[1] // pieces
    step = pl.program_id(0)

    @pl.when(step == 0)
    def _():
        scatter.near.greet()
        m_t_ref[...] = m_ref[...].T
        gz_t_ref[...] = gz_ref[...].T

    @pl.loop(jnp.where(step == 0, 0, step + 1), jnp.minimum(step + 2, pieces))
    def _(index):
        piece = scatter.place(index)
        cols = pl.ds(pl.multiple_of(piece * wide, wide), wide)
        for part, ref in ((slice(0, half), scatter.keep), (slice(half, 2 * half), scatter.away)):
            ref[piece, :, :wide] = nn(m_t_ref[part, :], gh_ref[:, cols]).astype(BF16)
            ref[piece, :, wide:] = nn(gz_t_ref[part, :], act_ref[:, cols]).astype(BF16)
        scatter.core(index)

    table = {
        (0, 1): [(scatter.first, 0)],
        (0, 3): [(scatter.first, 1)],
        (1, 1): [(scatter.second, 0), (scatter.first, 2)],
        (2, 1): [(scatter.second, 1), (scatter.last, 0), (scatter.first, 3)],
        (3, 1): [(scatter.last, 1), (scatter.second, 2)],
    }

    def hook(slot):
        for (when, where), events in table.items():
            if where == slot:

                @pl.when(step == when)
                def _():
                    for work, index in events:
                        work(index)

    attend_back_work(
        gr_ref, q_ref, kv_ref, q_hat_ref, k_hat_ref, q_scale_ref, k_scale_ref, p_ref, near_ref, far_ref, heads_ref,
        gq_ref, gkv_ref, mine_ref, left_ref, right_ref, small_ref, acc_ref, hook,
    )

    @pl.when(step == pieces - 1)
    def _():
        scatter.last(pieces - 2)
        scatter.second(pieces - 1)
        scatter.last(pieces - 1)
        scatter.done()


def attend_back_scatter(gr, stored, near, far, heads, m, gh, gz, act, layer, collective):
    rows, width = gr.shape
    half = width // 2
    hidden = gh.shape[1]
    pieces = near.shape[1]
    wide = hidden // pieces
    in_specs, out_specs, out_shape, scratch, cost = attend_back_specs(rows, width, pieces, layer, layer)
    full, all_hidden = whole((rows, width)), whole((rows, hidden))
    result, extra = scatter_specs(pieces, half // 4, 2 * wide)
    return pl.pallas_call(
        attend_back_scatter_kernel,
        grid=(pieces,),
        in_specs=in_specs + [sheet(layer, rows, width), all_hidden, full, sheet(layer, rows, hidden)],
        out_specs=out_specs + [whole(result.shape)],
        out_shape=out_shape + [result],
        scratch_shapes=scratch + [pltpu.VMEM((width, rows), BF16)] * 2 + extra,
        compiler_params=params(collective),
        cost_estimate=cost,
        name="attend_back_scatter",
    )(gr, *stored, near, far, heads, m, gh, gz, act)


def give_back_kernel(*refs, layer, with_mlp):
    a_ref, gq_ref, gkv_ref, gr_ref, o_ref, x_ref, g1_ref, mine_ref, left_ref, right_ref, feats_ref = refs[:11]
    rest = refs[11:]
    if with_mlp:
        down_near_ref, down_far_ref, slope_ref, up_near_ref, up_far_ref, mid_ref = rest[:6]
        rest = rest[6:]
    g_ref, sums_ref, out_ref = rest[:3]
    rest = rest[3:]
    if with_mlp:
        mlp_outs, rest = rest[:6], rest[6:]
        acc_ref, rest = rest[0], rest[1:]
    a_t_ref, gr_t_ref, total_ref, landed_ref, halo_send, halo_recv, *scratch = rest
    scatter = Scatter(out_ref, *scratch)
    pieces, rows = scatter.pieces, gr_ref.shape[0]
    half = gr_ref.shape[1] // 2
    spill = REACH - rows
    step = pl.program_id(0)
    moves = [
        (1, right_ref, pl.ds(0, rows), pl.ds(0, rows), 0),
        (-1, left_ref, pl.ds(spill, rows), pl.ds(0, rows), 0),
        (2, right_ref, pl.ds(rows, spill), pl.ds(0, spill), 0),
        (-2, left_ref, pl.ds(0, spill), pl.ds(0, spill), rows - spill),
    ]
    place, size = lax.axis_index("tp"), lax.axis_size("tp")
    inside = lambda other: jnp.logical_and(other >= 0, other < size)

    def halo_copy(index):
        distance, ref, source, target, _ = moves[index]
        return pltpu.make_async_remote_copy(
            src_ref=ref.at[source, :], dst_ref=landed_ref.at[index, target, :], send_sem=halo_send.at[index],
            recv_sem=halo_recv.at[index], device_id={"tp": place + distance}, device_id_type=MESH,
        )

    @pl.when(step == 0)
    def _():
        scatter.near.greet()
        for index, (distance, *_) in enumerate(moves):

            @pl.when(inside(place + distance))
            def _():
                halo_copy(index).start()

        a_t_ref[...] = a_ref[...].T
        gr_t_ref[...] = gr_ref[...].T

    @pl.when(step < pieces)
    def _():
        piece = scatter.place(step)
        for part, ref in ((slice(0, half), scatter.keep), (slice(half, 2 * half), scatter.away)):
            from_q = nn(a_t_ref[part, REACH : REACH + rows], gq_ref[...])
            from_o = nn(gr_t_ref[part, :], o_ref[...])
            ref[piece, :, :PAIR] = from_q[:, :PAIR].astype(BF16)
            ref[piece, :, PAIR : 4 * PAIR] = nn(a_t_ref[part, :], gkv_ref[...]).astype(BF16)
            ref[piece, :, 4 * PAIR : 5 * PAIR] = (from_q[:, PAIR:] + from_o[:, :PAIR]).astype(BF16)
            ref[piece, :, 5 * PAIR :] = from_o[:, PAIR:].astype(BF16)
        scatter.core(step)

        @pl.when(step > 0)
        def _():
            scatter.first(step - 1)

        @pl.when(step > 1)
        def _():
            scatter.second(step - 2)

    @pl.when(step == pieces - 1)
    def _():
        scatter.first(pieces - 1)
        scatter.last(0)
        scatter.second(pieces - 2)
        total_ref[...] = mine_ref[...]
        for index, (distance, _, _, target, start) in enumerate(moves):

            @pl.when(inside(place + distance))
            def _():
                halo_copy(index).wait_send()

            @pl.when(inside(place - distance))
            def _():
                halo_copy(index).wait_recv()
                total_ref[pl.ds(start, target.size), :] += landed_ref[index, target, :].astype(F32)

        scatter.last(1)
        total = total_ref[...]
        hat, scale = row_norm(x_ref[...])
        g_ref[...] = g1_ref[...] + row_norm_back(total * line(feats_ref.at[layer], LN_GAIN[0]), hat, scale)
        sums_ref[...] = jnp.zeros_like(sums_ref)
        sums_ref[0:1, :] = jnp.sum(total * hat, axis=0, keepdims=True)
        sums_ref[1:2, :] = jnp.sum(total, axis=0, keepdims=True)
        scatter.second(pieces - 1)

    if with_mlp:

        @pl.when(step >= pieces)
        def _():
            mlp_back_work(
                g_ref, down_near_ref, down_far_ref, slope_ref, up_near_ref, up_far_ref, mid_ref,
                feats_ref.at[layer - 1], *mlp_outs, acc_ref, step == pieces, step == 2 * pieces - 1,
            )

    @pl.when(step == pl.num_programs(0) - 1)
    def _():
        scatter.last(pieces - 2)
        scatter.last(pieces - 1)
        scatter.done()


def give_back(a_win, gq, gkv, gr, o, x, g1, mine, left, right, feats, layer, collective, before=None):
    _, window, width = a_win.shape
    rows = gr.shape[0]
    half = width // 2
    pieces = gq.shape[1] // (2 * PAIR)
    full = whole((rows, width))
    turned_at = lambda step: lax.rem(jnp.minimum(step, pieces - 1) + 1, pieces)
    turned = lambda height, wide: pl.BlockSpec((height, wide), lambda step: (0, turned_at(step)))
    in_specs = [
        sheet(layer, window, width), turned(rows, 2 * PAIR), turned(window, 3 * PAIR), full,
        pl.BlockSpec((None, rows, 2 * PAIR), lambda step: (layer, 0, turned_at(step))),
        full if layer == 0 else sheet(layer - 1, rows, width), full, full, whole((REACH, width)), whole((REACH, width)),
        whole(feats.shape),
    ]
    operands = [a_win, gq, gkv, gr, o, x, g1, mine, left, right, feats]
    result, extra = scatter_specs(pieces, half // 4, 6 * PAIR)
    out_specs = [full, whole((8, width)), whole(result.shape)]
    out_shape = [shaped((rows, width), F32), shaped((8, width), F32), result]
    scratch = []
    if before is not None:
        near, far, slope, mid = before
        hidden = slope.shape[2]
        wide = hidden // pieces
        below = layer - 1
        late_at = lambda step: jnp.maximum(step - pieces, 0)
        late = lambda height: pl.BlockSpec((height, wide), lambda step: (0, late_at(step)))
        late_piece = lambda first: pl.BlockSpec((None, None, half, wide), lambda step: (below, late_at(step), 0, first))
        in_specs += [
            late_piece(1), late_piece(1), pl.BlockSpec((None, rows, wide), lambda step: (below, 0, late_at(step))),
            late_piece(0), late_piece(0), sheet(below, rows, width),
        ]
        operands += [near, far, slope, near, far, mid]
        out_specs += [full, late(rows), late(1), full, full, whole((8, width))]
        out_shape += [
            shaped((rows, width)), shaped((rows, hidden)), shaped((1, hidden), F32), shaped((rows, width), F32),
            shaped((rows, width)), shaped((8, width), F32),
        ]
        scratch = [pltpu.VMEM((rows, width), F32)]
    scratch += [
        pltpu.VMEM((width, window), BF16), pltpu.VMEM((width, rows), BF16), pltpu.VMEM((rows, width), F32),
        pltpu.VMEM((4, rows, width), BF16), pltpu.SemaphoreType.DMA((4,)), pltpu.SemaphoreType.DMA((4,)), *extra,
    ]
    return pl.pallas_call(
        functools.partial(give_back_kernel, layer=layer, with_mlp=before is not None),
        grid=(pieces if before is None else 2 * pieces,),
        in_specs=in_specs,
        out_specs=out_specs,
        out_shape=out_shape,
        scratch_shapes=scratch,
        compiler_params=params(collective),
        cost_estimate=pl.CostEstimate(
            flops=2 * width * width * (2 * window + 2 * rows), bytes_accessed=20 * width * width, transcendentals=0
        ),
        name="give_back",
    )(*operands)


def flip(array, bit, axis="fsdp"):
    size = lax.axis_size(axis)
    return lax.ppermute(array, axis, [(i, i ^ (1 << bit)) for i in range(size)])


def ring(array):
    size = lax.axis_size("tp")
    return lax.ppermute(array, "tp", [(i, (i + 1) % size) for i in range(size)])


def hop(array, distance):
    size = lax.axis_size("tp")
    return lax.ppermute(array, "tp", [(i, i + distance) for i in range(size) if 0 <= i + distance < size])


def bits_of(size):
    return size.bit_length() - 1


def row_bits(first_top):
    count = bits_of(lax.axis_size("fsdp"))
    tops = [count - 1, count - 2] if first_top else [count - 2, count - 1]
    return list(range(1, count - 2)), tops


def gather_by_permutes(block, first_top):
    pieces = [block]
    for _ in range(lax.axis_size("tp") - 1):
        pieces.append(ring(pieces[-1]))
    block = jnp.concatenate(pieces, axis=1)
    low, tops = row_bits(first_top)
    have = []
    for bit in low + tops:
        axis = sum(other > bit for other in have)
        block = jnp.stack([block, flip(block, bit)], axis=axis)
        have.append(bit)
    block = block.reshape((-1, len(pieces), pieces[0].shape[1])).transpose(1, 0, 2)[None]
    return block, flip(block, 0)


def add(left, right, kind=BF16):
    return (left.astype(F32) + right.astype(F32)).astype(kind)


def reduce_by_permutes(keep, send, first_top):
    low, tops = row_bits(first_top)
    block = add(keep, flip(send, 0))
    order = tops + low[::-1]
    have = sorted(order, reverse=True)
    block = block.reshape((2,) * len(have) + (-1, block.shape[-1]))
    for bit in order:
        axis = have.index(bit)
        mine = lax.index_in_dim(block, 0, axis, keepdims=False)
        other = lax.index_in_dim(block, 1, axis, keepdims=False)
        block = add(mine, flip(other, bit))
        have.remove(bit)
    pieces = jnp.split(block, lax.axis_size("tp"), axis=1)
    total = pieces[1]
    for piece in pieces[2:]:
        total = add(ring(total), piece)
    return add(ring(total), pieces[0], F32)


def attn_shard(w_qkv, w_out):
    q, k, v = (w_qkv[:, which] for which in range(3))
    o = w_out.T
    return side(q[:, :PAIR], k[:, :PAIR], v[:, :PAIR], k[:, PAIR:], v[:, PAIR:], q[:, PAIR:], o[:, PAIR:], o[:, :PAIR])


def attn_unshard(block):
    tile = lambda start, wide=PAIR: block[:, start : start + wide]
    q = side(tile(0), tile(4 * PAIR, HD))
    k = side(tile(PAIR), tile(3 * PAIR, HD))
    v = side(tile(2 * PAIR), tile(3 * PAIR + HD, HD))
    o = side(tile(5 * PAIR), tile(4 * PAIR + HD, HD))
    return jnp.stack([q, k, v], axis=1), o.T


def body(
    tokens, segment_ids, patch_pos, row_table, col_table, ln_gain, ln_bias, qkv_bias, qk_gain, query_bias, out_bias,
    fc1_bias, fc2_bias, w_qkv, w_out, w_fc1, w_fc2, cotangent,
):
    layers = w_qkv.shape[0]
    rows, width = tokens.shape
    half = width // 2
    fsdp, tp = lax.axis_size("fsdp"), lax.axis_size("tp")
    f_index, t_index = lax.axis_index("fsdp"), lax.axis_index("tp")
    hidden = fc1_bias.shape[1] * fsdp * tp
    grid = row_table.shape[0]
    fine = width // (fsdp * tp)
    parts = hidden // width
    in_kernel = fsdp == 8

    place = jnp.arange(width, dtype=jnp.int32)
    chunk = width // fsdp
    slot = place // chunk
    away = (slot % (fsdp // 2)) * 2 + slot // (fsdp // 2)
    feature_at = (f_index ^ away) * chunk + place % chunk
    head_cols = width // tp
    spot = jnp.arange(tp * 3 * PAIR, dtype=jnp.int32)
    tile, part = spot % (3 * PAIR) // PAIR, spot % PAIR // HD
    head = jnp.where(tile == 0, part, jnp.where(tile == part + 1, 2, -fsdp * tp))
    head_at = ((t_index - spot // (3 * PAIR)) % tp) * head_cols + head * HD + spot % HD
    far = place // fine
    arrived_at = ((f_index ^ (far // tp)) * tp + (t_index ^ (far % tp))) * fine + place % fine
    to_feature = (arrived_at[:, None] == feature_at[None, :]).astype(BF16)
    to_head = (arrived_at[:, None] == head_at[None, :]).astype(BF16)
    reorder = (place[:, None] == feature_at[None, :]).astype(BF16)
    device = jnp.arange(fsdp * tp, dtype=jnp.int32)
    device_at = (f_index ^ (device // tp)) * tp + (t_index ^ (device % tp))
    wanted = ((t_index - device // fsdp) % tp) * fsdp + device % fsdp
    to_hidden = (wanted[:, None] == device_at[None, :]).astype(BF16)

    by_layer = lambda *items: jnp.concatenate([item.reshape(layers, -1, fine) for item in items], axis=1).reshape(-1, fine)
    shares = [
        row_table, col_table, by_layer(ln_gain, ln_bias, out_bias, fc2_bias), by_layer(qkv_bias, qk_gain, query_bias),
        fc1_bias.reshape(layers * parts, fine),
    ]
    small = jnp.concatenate(shares, axis=0)
    count = small.shape[0]
    flat = small.reshape(1, -1)
    for bit in range(bits_of(tp)):
        flat = jnp.concatenate([flat, flip(flat, bit, "tp")], axis=0)
    for bit in range(bits_of(fsdp)):
        flat = jnp.concatenate([flat, flip(flat, bit)], axis=0)
    gathered = flat.reshape(fsdp * tp, count, fine)
    lined = gathered.transpose(1, 0, 2).reshape(count, width)
    wide = 2 * grid + 6 * layers
    feats = jnp.dot(lined[:wide], to_feature, preferred_element_type=F32)
    heads = jnp.dot(lined[wide : wide + 6 * layers], to_head, preferred_element_type=F32)
    up_shift = jnp.einsum(
        "or,rlsi->losi",
        to_hidden,
        gathered[:, wide + 6 * layers :].reshape(fsdp * tp, layers, parts, fine),
        preferred_element_type=F32,
    ).reshape(layers, tp, 1, hidden // tp)
    tables = feats[: 2 * grid].astype(BF16)
    feats = feats[2 * grid :].reshape(layers, FEATS, width)

    heads = heads.reshape(layers, HEADS, tp, 3 * PAIR).transpose(2, 0, 1, 3)
    attn_shards = jnp.stack([attn_shard(w_qkv[layer], w_out[layer]) for layer in range(layers)])
    mlp_shards = jnp.concatenate([w_fc1, w_fc2.transpose(0, 2, 1)], axis=2)

    grid_ids = jnp.arange(grid, dtype=jnp.int32)
    row_hot = patch_pos[0][:, None] == grid_ids[None, :]
    col_hot = patch_pos[1][:, None] == grid_ids[None, :]
    residual = (
        jnp.dot(tokens, reorder, preferred_element_type=F32)
        + jnp.dot(row_hot.astype(BF16), tables[:grid], preferred_element_type=F32)
        + jnp.dot(col_hot.astype(BF16), tables[grid:], preferred_element_type=F32)
    )
    segments = segment_ids[0]
    padded = jnp.pad(segments, (REACH, REACH), constant_values=-1)
    seg_k = lax.dynamic_slice_in_dim(padded, t_index * rows, rows + 2 * REACH).reshape(-1, 1)
    seg_q = lax.dynamic_slice_in_dim(segments, t_index * rows, rows).reshape(1, -1)
    spill = REACH - rows

    hat, _ = row_norm(residual)
    a_own = (hat * feats[0, LN_GAIN[0]] + feats[0, LN_BIAS[0]]).astype(BF16)
    if in_kernel:
        *stored, o, act, slope, mid, m, x2, a_win, attn_near, attn_far, mlp_near, mlp_far = forward(
            a_own, residual, heads, feats, up_shift, seg_k, seg_q, attn_shards, mlp_shards
        )
        start, residual = residual, x2[layers - 1]
        saved = [
            (x2 if layer else start, a_win, stored, o, mid, m, act, slope, attn_near, attn_far, mlp_near, mlp_far)
            for layer in range(layers)
        ]
    else:
        saved = []
        for layer in range(layers):
            a_win = jnp.concatenate(
                [hop(a_own[rows - spill :], 2), hop(a_own, 1), a_own, hop(a_own, -1), hop(a_own[:spill], -2)], axis=0
            )
            attn_near, attn_far = gather_by_permutes(attn_shards[layer], layer % 2 == 0)
            *stored, probs, o, mid, m = attend(
                a_win, attn_near, attn_far, heads, feats, residual, seg_k, seg_q, layer
            )
            mlp_near, mlp_far = gather_by_permutes(mlp_shards[layer], layer % 2 == 1)
            act, slope, x2 = mlp(m, mid, mlp_near, mlp_far, up_shift, feats, layer)
            stored = [item[None] for item in stored] + [probs]
            kept = [item[None] for item in (o, mid, m, act, slope)]
            saved.append((residual, a_win[None], stored, *kept, attn_near, attn_far, mlp_near, mlp_far))
            residual = x2
            if layer + 1 < layers:
                hat, _ = row_norm(residual)
                a_own = (
                    hat * feats[layer + 1, LN_GAIN[0]] + feats[layer + 1, LN_BIAS[0]]
                ).astype(BF16)

    restore = functools.partial(
        lax.dot_general, dimension_numbers=(((1,), (1,)), ((), ())), precision=HIGHEST, preferred_element_type=F32
    )
    exact = reorder.astype(F32)
    activations = restore(residual, exact)
    grad = jnp.dot(cotangent, exact, precision=HIGHEST, preferred_element_type=F32)
    kept_sums = [None] * layers
    w_qkv_grad, w_out_grad, w_fc1_grad, w_fc2_grad = ([None] * layers for _ in range(4))
    back = None
    for layer in reversed(range(layers)):
        x, a_win, stored, o, mid, m, act, slope, attn_near, attn_far, mlp_near, mlp_far = saved[layer]
        if back is None:
            index = layer if in_kernel else 0
            back = mlp_back(grad, mlp_near, mlp_far, slope, mid, feats, layer, index)
        gz, gh, up_grad, g1, gr, mlp_small = back
        back = None
        if in_kernel:
            gq, gkv, mine, left, right, attn_small, mlp_block = attend_back_scatter(
                gr, stored, attn_near, attn_far, heads, m, gh, gz, act, layer, 40 + layer
            )
            before = None
            if layer:
                before = mlp_near, mlp_far, slope, mid
            grad, norm_sums, attn_block, *back = give_back(
                a_win, gq, gkv, gr, o, x, g1, mine, left, right, feats, layer, 50 + layer, before
            )
            back = back or None
            norm_sums = norm_sums[0], norm_sums[1]
        else:
            mlp_block = reduce_by_permutes(*mlp_weight_grads(m, gh, gz, act), layer % 2 == 0)
            gq, gkv, mine, left, right, attn_small = attend_back(
                gr, stored, attn_near, attn_far, heads, layer, 0
            )
            attn_block = reduce_by_permutes(*attn_weight_grads(a_win, gq, gkv, gr, o), layer % 2 == 1)
            ends = jnp.concatenate([hop(right[rows:], 2), hop(left[:spill], -2)], axis=0).astype(F32)
            attn_grad = mine + hop(right[:rows], 1).astype(F32) + hop(left[spill:], -1).astype(F32) + ends
            hat, scale = row_norm(x)
            grad = g1 + row_norm_back(attn_grad * feats[layer, LN_GAIN[0]], hat, scale)
            norm_sums = jnp.sum(attn_grad * hat, axis=0), jnp.sum(attn_grad, axis=0)
        middle = mlp_block.shape[1] // 2
        w_fc1_grad[layer], w_fc2_grad[layer] = mlp_block[:, :middle], mlp_block[:, middle:].T
        w_qkv_grad[layer], w_out_grad[layer] = attn_unshard(attn_block)
        kept_sums[layer] = (*norm_sums, mlp_small, attn_small, up_grad.reshape(parts, width))

    token_grad = restore(grad, exact)
    row_grad = jnp.einsum("tg,td->gd", row_hot.astype(F32), grad, precision=HIGHEST)
    col_grad = jnp.einsum("tg,td->gd", col_hot.astype(F32), grad, precision=HIGHEST)
    featured = [row_grad, col_grad]
    headed = []
    for a_gain, a_shift, sums, head_sums, _ in kept_sums:
        featured.append(jnp.stack([a_gain, sums[2], a_shift, sums[3], sums[1], sums[0]]))
        headed += [head_sums[3:6], head_sums[0:2], head_sums[2:3]]
    headed = jnp.concatenate(headed)
    spread = jnp.concatenate(
        [restore(jnp.concatenate(featured), to_feature.astype(F32)), restore(headed, to_head.astype(F32))]
    )
    spread = spread.reshape(-1, fsdp * tp, fine).transpose(1, 0, 2)
    up_all = jnp.stack([item[4] for item in kept_sums]).reshape(layers, fsdp * tp, parts * fine)
    up_all = jnp.einsum("or,lok->rlk", to_hidden.astype(F32), up_all, precision=HIGHEST)
    flat = jnp.concatenate([spread.reshape(fsdp * tp, -1), up_all.reshape(fsdp * tp, -1)], axis=1)
    for bit in reversed(range(bits_of(fsdp))):
        middle = flat.shape[0] // 2
        flat = flat[:middle] + flip(flat[middle:], bit)
    for bit in reversed(range(bits_of(tp))):
        middle = flat.shape[0] // 2
        flat = flat[:middle] + flip(flat[middle:], bit, "tp")
    flat = flat.reshape(-1)
    found = flat.reshape(-1, fine)
    rows_g, cols_g, rest = found[:grid], found[grid : 2 * grid], found[2 * grid :]
    by_feature = rest[: layers * FEATS].reshape(layers, FEATS, fine)
    by_head = rest[layers * FEATS : layers * (FEATS + HEADS)].reshape(layers, HEADS, fine)
    up_g = rest[layers * (FEATS + HEADS) :].reshape(layers, parts * fine)
    gain_g, shift_g, out_g, last_g = by_feature[:, :2], by_feature[:, 2:4], by_feature[:, OUT_BIAS], by_feature[:, LAST_BIAS]
    proj_g, head_gain_g, head_shift_g = by_head[:, :3], by_head[:, 3:5], by_head[:, HEAD_BIAS]
    return (
        activations, token_grad, rows_g, cols_g, gain_g, shift_g, proj_g, head_gain_g, head_shift_g, out_g, up_g, last_g,
        jnp.stack(w_qkv_grad), jnp.stack(w_out_grad), jnp.stack(w_fc1_grad), jnp.stack(w_fc2_grad),
    )


def solution(mesh):
    both = ("fsdp", "tp")
    in_specs = (
        P(both, None), P("fsdp", None), P(None, both), P(None, both), P(None, both), P(None, None, both),
        P(None, None, both), P(None, None, both), P(None, None, both), P(None, both), P(None, both), P(None, both),
        P(None, both), P(None, "fsdp", None, "tp"), P(None, "tp", "fsdp"), P(None, "fsdp", "tp"), P(None, "tp", "fsdp"),
        P(both, None),
    )
    out_specs = (
        P(both, None), P(both, None), P(None, both), P(None, both), P(None, None, both), P(None, None, both),
        P(None, None, both), P(None, None, both), P(None, both), P(None, both), P(None, both), P(None, both),
        P(None, "fsdp", None, "tp"), P(None, "tp", "fsdp"), P(None, "fsdp", "tp"), P(None, "tp", "fsdp"),
    )
    return jax.shard_map(body, mesh=mesh, in_specs=in_specs, out_specs=out_specs, check_vma=False)
```

time: 564 us -> 475 us (0.84)
  Pallas kernels: 458 us -> 377 us
  local copies, waits for them, and re-layouts: 39.4 us -> 30.2 us
    pallas_call x12 -> x6, Pallas kernels: 458 us -> 377 us  [the longest x1 160 us: forward(): pl.pallas_call(forward_kernel, grid=(1 + 2 * layers * pieces,), in_specs=...]
  transfers between devices with their start and end apart: 10 -> 10, of which waited for: 7 -> 8; matrix products, arithmetic and copies ran while one was open for 3% -> 3% of each run, Pallas kernels for 6% -> 0%
where the time goes in v4:
time: 475 us; the launch traced here: 468 us
  Pallas kernels  377 us (79%)
  local copies, waits for them, and re-layouts  30.2 us (6%)
  waiting for transfers between devices  17.5 us (4%)
  matrix products  16.9 us (4%)
  starting transfers between devices  12.5 us (3%)
  other arithmetic  11.4 us (2%)
    pallas_call x1, Pallas kernels, forward(): pl.pallas_call(forward_kernel, grid=(1 + 2 * layers * pieces,), in_specs=...  160 us
    pallas_call x2, Pallas kernels, attend_back_scatter(): pl.pallas_call(attend_back_scatter_kernel, grid=(pieces,), in_specs=in_sp...  123 us
    pallas_call x2, Pallas kernels, give_back(): pl.pallas_call(functools.partial(give_back_kernel, layer=layer, with_mlp=...  84.3 us
    ppermute x10, waiting for transfers between devices, flip(): return lax.ppermute(array, axis, [(i, i ^ 1 << bit) for i in range(size)])  17.5 us
    ppermute x10, starting transfers between devices, flip(): return lax.ppermute(array, axis, [(i, i ^ 1 << bit) for i in range(size)])  12.5 us
    pallas_call x1, Pallas kernels, mlp_back(): pl.pallas_call(mlp_back_kernel, grid=(pieces,), in_specs=[full, piece_of(...  10.3 us
  transfers between devices with their start and end apart: 10, of which 8 were waited for; matrix products, arithmetic and copies ran while one was open for 3% of the time, Pallas kernels for 0%

profile of v4, /device:TPU:0, one launch (start us, length us, event | category | flops | bytes accessed | tf_op | source)
XLA Modules:
  0.0 468.1 jit_solution(14013034182890060517)
XLA Ops:
  5.3 0.8 concatenate.90
  6.4 3.1 collective-permute-start
  9.4 1.0 slice_bitcast_fusion.5
  10.5 0.8 fusion.149
  12.9 0.9 pad_maximum_fusion.mlp_shard_ref
  13.8 2.1 fusion.17.refs_0_
  16.0 2.7 collective-permute-start.1
  19.2 1.0 copy.181.seg_k_ref
  21.1 1.0 collective-permute-done.2
  22.1 1.6 collective-permute-start.3
  24.1 2.3 collective-permute-done.3
  26.5 1.6 collective-permute-start.4
  28.8 2.6 collective-permute-done.4
  31.4 1.0 concatenate.100
  36.4 0.8 reshape.403.up_shift_ref
  37.2 1.5 fusion.29.heads_ref
  38.7 0.9 add_convert_fusion.a_ref
  39.6 159.9 %forward.1 = (bf16[2,256,1024]{2,1,0:T(8,128)(2,1)}, bf16[2,1024,1536]{2,1,0:T(8,128)(2,1)}, bf16[2,256,1024]{2,1,0:T(8,128)(2,1)}, bf16[2,1024,1024]{2,1,0:T(8,...) custom-call(bf16[256,768]{1,0:T(8,128)(2,1)} %add_convert_fusion.a_r, ...), custom_call_target="tpu_custom_call" | custom-call | tf_op jit(solution)/shard_map/forward/pallas_call | solution.py:671
  199.6 10.3 %mlp_back.1 = (bf16[256,768]{1,0:T(8,128)(2,1)}, bf16[256,3072]{1,0:T(8,128)(2,1)}, f32[1,3072]{1,0:T(1,128)}, f32[256,768]{1,0:T(8,128)}, bf16[256,768]{1,0:T(8,128)(2,1)}, /*index=5*/f32[8,768]{1,0:T(8,128)}) custom-call(f32[256,768]{1,0:T(8,128)} %fusion.17.refs_0_, bf16[2,4,384,1536]{3,2,1,0:T(8,128)(2,1)} %get-tuple-element.67.refs_1_.refs_4_.refs_11_.refs_14_, ...), custom_call_target="tpu_custom_call" | custom-call | flops 2415919104 | bytes 9437184 | tf_op jit(solution)/shard_map/mlp_back/pallas_call | solution.py:735
  209.9 61.8 %attend_back_scatter.2 = (bf16[256,1024]{1,0:T(8,128)(2,1)}, bf16[1024,1536]{1,0:T(8,128)(2,1)}, f32[256,768]{1,0:T(8,128)}, bf16[384,768]{1,0:T(8,128)(2,1)}, b...) custom-call(bf16[256,768]{1,0:T(8,128)(2,1)} %get-tuple-element.71.gr_ref.refs_3_, ...), custom_call_target="tpu_custom_call" | custom-call | flops 10468982784 | bytes 15728640 | tf_op jit(solution)/shard_map/attend_back_scatter/pallas_call | solution.py:1115
  271.7 45.9 %give_back.2 = (f32[256,768]{1,0:T(8,128)}, f32[8,768]{1,0:T(8,128)}, f32[96,768]{1,0:T(8,128)}, bf16[256,768]{1,0:T(8,128)(2,1)}, bf16[256,3072]{1,0:T(8,128)(2...) custom-call(bf16[2,1024,768]{2,1,0:T(8,128)(2,1)} %get-tuple-element.66.refs_0_, ...), custom_call_target="tpu_custom_call" | custom-call | flops 3019898880 | bytes 11796480 | tf_op jit(solution)/shard_map/give_back/pallas_call | solution.py:1277
  317.5 61.1 %attend_back_scatter.3 = (bf16[256,1024]{1,0:T(8,128)(2,1)}, bf16[1024,1536]{1,0:T(8,128)(2,1)}, f32[256,768]{1,0:T(8,128)}, bf16[384,768]{1,0:T(8,128)(2,1)}, b...) custom-call(bf16[256,768]{1,0:T(8,128)(2,1)} %get-tuple-element.92.gr_ref.refs_3_, ...), custom_call_target="tpu_custom_call" | custom-call | flops 10468982784 | bytes 15728640 | tf_op jit(solution)/shard_map/attend_back_scatter/pallas_call | solution.py:1115
  378.6 38.4 %give_back.3 = (f32[256,768]{1,0:T(8,128)}, f32[8,768]{1,0:T(8,128)}, f32[96,768]{1,0:T(8,128)}) custom-call(bf16[2,1024,768]{2,1,0:T(8,128)(2,1)} %get-tuple-element.66.refs_0_, bf16[256,1024]{1,0:T(8,128)(2,1)} %get-tuple-element.95.refs_1_, bf16[1024,1536]{1,0:T(8,128)(2,1)} %get-tuple-element.96.refs_2_, ...), custom_call_target="tpu_custom_call" | custom-call | flops 3019898880 | bytes 11796480 | tf_op jit(solution)/shard_map/give_back/pallas_call | solution.py:1277
  417.0 1.6 fusion.145
  418.7 1.6 fusion.146
  421.7 1.7 fusion.36
  423.9 2.2 fusion.12
  426.1 0.8 slice_bitcast_fusion.1
  427.0 0.8 slice_bitcast_fusion
  427.8 0.8 fusion.155
  428.7 0.8 fusion.153
  429.6 1.5 fusion.5
  431.1 2.1 fusion.3
  433.6 0.9 copy.184
  435.8 1.4 reduce.24
  437.3 1.4 reduce.23
  438.9 1.0 fusion.53
  439.9 1.7 collective-permute-start.5
  441.7 1.9 pad_maximum_fusion.3
  443.6 0.9 pad_maximum_fusion.2
  444.8 2.2 fusion.14
  447.1 0.9 collective-permute-start.6
  448.0 0.9 pad_maximum_fusion.1
  448.9 3.2 collective-permute-done.6
  452.2 1.2 collective-permute-done.7
  454.2 4.2 collective-permute-done.8
  458.5 0.8 copy.190
  459.3 2.9 collective-permute-done.9
  (222 shorter events, 23.3 us)
Async XLA Ops:
  0.6 13.1 %copy-start = (f32[256,768]{1,0:T(8,128)S(1)}, f32[256,768]{1,0:T(8,128)}, u32[]{:S(2)}) copy-start(f32[256,768]{1,0:T(8,128)} %param.35) | copy-start | bytes 2359300
  0.7 11.2 %copy-start.40 = (s32[2,256]{1,0:T(2,128)S(1)}, s32[2,256]{1,0:T(2,128)}, u32[]{:S(2)}) copy-start(s32[2,256]{1,0:T(2,128)} %param.20) | copy-start | bytes 6148
  0.7 12.2 %copy-start.35 = (s32[1,1024]{1,0:T(1,128)S(1)}, s32[1,1024]{1,0:T(1,128)}, u32[]{:S(2)}) copy-start(s32[1,1024]{1,0:T(1,128)} %param.19) | copy-start | bytes 12292
  0.7 12.2 %copy-start.13 = (bf16[2,768,96]{1,2,0:T(8,128)(2,1)S(1)}, bf16[2,768,96]{1,2,0:T(8,128)(2,1)}, u32[]{:S(2)}) copy-start(bf16[2,768,96]{1,2,0:T(8,128)(2,1)} %param.34) | copy-start | bytes 884740
  0.7 12.2 %copy-start.14 = (bf16[2,96,768]{2,1,0:T(8,128)(2,1)S(1)}, bf16[2,96,768]{2,1,0:T(8,128)(2,1)}, u32[]{:S(2)}) copy-start(bf16[2,96,768]{2,1,0:T(8,128)(2,1)} %param.33) | copy-start | bytes 884740
  6.4 9.6 %collective-permute-start = (bf16[1,3840]{1,0:T(2,128)(2,1)S(1)}, bf16[1,3840]{1,0:T(2,128)(2,1)S(1)}, u32[]{:S(2)}, u32[]{:S(2)}) collective-permute-start(bf16[1,3840]{1,0:T(2,128)(2,1)S(1)} %reshape.389), channel_id=1, source_target_pairs={{0,1},{1,0},{2,3},{3,2},{4,5},{5,4},{6,7},{7,6},{8,9},{9,8},{10,11... | collective-permute-start | bytes 23048 | tf_op jit(solution)/shard_map/ppermute | solution.py:1294
  11.8 417.8 %copy-start.33 = (s32[768]{0:T(1024)}, s32[768]{0:T(1024)S(1)}, u32[]{:S(2)}) copy-start(s32[768]{0:T(1024)S(1)} %get-tuple-element.272) | copy-start | bytes 9220
  15.9 20.1 %copy-start.39 = (s32[32]{0:T(128)}, s32[32]{0:T(128)S(1)}, u32[]{:S(2)}) copy-start(s32[32]{0:T(128)S(1)} %get-tuple-element.275) | copy-start | bytes 388
  15.9 21.2 %copy-start.38 = (s32[32]{0:T(128)}, s32[32]{0:T(128)S(1)}, u32[]{:S(2)}) copy-start(s32[32]{0:T(128)S(1)} %get-tuple-element.274) | copy-start | bytes 388
  16.0 4.7 %collective-permute-start.1 = (bf16[2,3840]{1,0:T(2,128)(2,1)S(1)}, bf16[2,3840]{1,0:T(2,128)(2,1)S(1)}, u32[]{:S(2)}, u32[]{:S(2)}) collective-permute-start(bf16[2,3840]{1,0:T(2,128)(2,1)S(1)} %pad_maximum_fusion.10), channel_id=1, source_target_pairs={{0,2},{1,3},{2,0},{3,1},{4,6},{5,7},{6,4},{7,5},{8,10},{9,11},{10,... | collective-permute-start | bytes 46088 | tf_op jit(solution)/shard_map/ppermute | solution.py:1294
  20.8 1.3 collective-permute-start.2
  22.1 4.3 collective-permute-start.3
  26.5 4.9 %collective-permute-start.4 = (bf16[16,3840]{1,0:T(8,128)(2,1)S(1)}, bf16[16,3840]{1,0:T(8,128)(2,1)S(1)}, u32[]{:S(2)}, u32[]{:S(2)}) collective-permute-start(bf16[16,3840]{1,0:T(8,128)(2,1)S(1)} %concatenate.99), channel_id=1, source_target_pairs={{0,16},{4,20},{8,24},{12,28},{16,0},{20,4},{24,8},{28,12},{1,17},{... | collective-permute-start | bytes 368648 | tf_op jit(solution)/shard_map/ppermute | solution.py:1294
  35.0 4.6 copy-start.2
  35.3 4.3 copy-start.5
  378.6 41.7 %copy-start.11 = (f32[96,768]{1,0:T(8,128)S(1)}, f32[96,768]{1,0:T(8,128)}, u32[]{:S(2)}) copy-start(f32[96,768]{1,0:T(8,128)} %get-tuple-element.111) | copy-start | bytes 884740
  417.0 6.4 %copy-start.3 = (f32[256,768]{1,0:T(8,128)S(1)}, f32[256,768]{1,0:T(8,128)}, u32[]{:S(2)}) copy-start(f32[256,768]{1,0:T(8,128)} %get-tuple-element.101) | copy-start | bytes 2359300
  420.3 5.8 %copy-start.10 = (f32[96,1536]{1,0:T(8,128)S(1)}, f32[96,1536]{1,0:T(8,128)}, u32[]{:S(2)}) copy-start(f32[96,1536]{1,0:T(8,128)} %get-tuple-element.112) | copy-start | bytes 1769476
  421.7 5.3 %copy-start.9 = (f32[96,1536]{1,0:T(8,128)S(1)}, f32[96,1536]{1,0:T(8,128)}, u32[]{:S(2)}) copy-start(f32[96,1536]{1,0:T(8,128)} %get-tuple-element.113) | copy-start | bytes 1769476
  423.9 4.8 %copy-start.37 = (f32[8,768]{1,0:T(8,128)S(1)}, f32[8,768]{1,0:T(8,128)}, u32[]{:S(2)}) copy-start(f32[8,768]{1,0:T(8,128)} %get-tuple-element.103) | copy-start | bytes 73732
  423.9 5.6 %copy-start.36 = (f32[8,768]{1,0:T(8,128)S(1)}, f32[8,768]{1,0:T(8,128)}, u32[]{:S(2)}) copy-start(f32[8,768]{1,0:T(8,128)} %get-tuple-element.105) | copy-start | bytes 73732
  426.1 5.0 %copy-start.32 = (f32[8,1536]{1,0:T(8,128)S(1)}, f32[8,1536]{1,0:T(8,128)}, u32[]{:S(2)}) copy-start(f32[8,1536]{1,0:T(8,128)} %get-tuple-element.106) | copy-start | bytes 147460
  426.1 5.0 %copy-start.31 = (f32[8,1536]{1,0:T(8,128)S(1)}, f32[8,1536]{1,0:T(8,128)}, u32[]{:S(2)}) copy-start(f32[8,1536]{1,0:T(8,128)} %get-tuple-element.107) | copy-start | bytes 147460
  434.5 7.2 %copy-start.7 = (f32[1,768,96]{1,2,0:T(8,128)S(1)}, f32[1,768,96]{1,2,0:T(8,128)}, u32[]{:S(2)}) copy-start(f32[1,768,96]{1,2,0:T(8,128)} %get-tuple-element.216) | copy-start | bytes 884740
  434.5 9.1 %copy-start.6 = (f32[1,96,768]{2,1,0:T(8,128)S(1)}, f32[1,96,768]{2,1,0:T(8,128)}, u32[]{:S(2)}) copy-start(f32[1,96,768]{2,1,0:T(8,128)} %get-tuple-element.217) | copy-start | bytes 884740
  435.2 8.4 %copy-start.8 = (f32[1,96,768]{2,1,0:T(8,128)S(1)}, f32[1,96,768]{2,1,0:T(8,128)}, u32[]{:S(2)}) copy-start(f32[1,96,768]{2,1,0:T(8,128)} %get-tuple-element.219) | copy-start | bytes 884740
  435.2 9.2 %copy-start.22 = (f32[96,128]{1,0:T(8,128)S(1)}, f32[96,128]{1,0:T(8,128)}, u32[]{:S(2)}) copy-start(f32[96,128]{1,0:T(8,128)} %get-tuple-element.223) | copy-start | bytes 147460
  435.2 9.2 %copy-start.28 = (f32[96,64]{1,0:T(8,128)S(1)}, f32[96,64]{1,0:T(8,128)}, u32[]{:S(2)}) copy-start(f32[96,64]{1,0:T(8,128)} %get-tuple-element.227) | copy-start | bytes 73732
  435.2 9.2 %copy-start.20 = (f32[96,128]{1,0:T(8,128)S(1)}, f32[96,128]{1,0:T(8,128)}, u32[]{:S(2)}) copy-start(f32[96,128]{1,0:T(8,128)} %get-tuple-element.222) | copy-start | bytes 147460
  435.3 9.2 %copy-start.25 = (f32[96,64]{1,0:T(8,128)S(1)}, f32[96,64]{1,0:T(8,128)}, u32[]{:S(2)}) copy-start(f32[96,64]{1,0:T(8,128)} %get-tuple-element.226) | copy-start | bytes 73732
  435.3 9.3 %copy-start.19 = (f32[96,128]{1,0:T(8,128)S(1)}, f32[96,128]{1,0:T(8,128)}, u32[]{:S(2)}) copy-start(f32[96,128]{1,0:T(8,128)} %get-tuple-element.221) | copy-start | bytes 147460
  435.3 9.3 %copy-start.23 = (f32[96,64]{1,0:T(8,128)S(1)}, f32[96,64]{1,0:T(8,128)}, u32[]{:S(2)}) copy-start(f32[96,64]{1,0:T(8,128)} %get-tuple-element.225) | copy-start | bytes 73732
  435.3 9.3 %copy-start.26 = (f32[96,128]{1,0:T(8,128)S(1)}, f32[96,128]{1,0:T(8,128)}, u32[]{:S(2)}) copy-start(f32[96,128]{1,0:T(8,128)} %get-tuple-element.231) | copy-start | bytes 147460
  435.3 9.3 %copy-start.24 = (f32[96,128]{1,0:T(8,128)S(1)}, f32[96,128]{1,0:T(8,128)}, u32[]{:S(2)}) copy-start(f32[96,128]{1,0:T(8,128)} %get-tuple-element.230) | copy-start | bytes 147460
  435.3 9.3 %copy-start.21 = (f32[96,128]{1,0:T(8,128)S(1)}, f32[96,128]{1,0:T(8,128)}, u32[]{:S(2)}) copy-start(f32[96,128]{1,0:T(8,128)} %get-tuple-element.229) | copy-start | bytes 147460
  435.3 9.3 %copy-start.27 = (f32[96,64]{1,0:T(8,128)S(1)}, f32[96,64]{1,0:T(8,128)}, u32[]{:S(2)}) copy-start(f32[96,64]{1,0:T(8,128)} %get-tuple-element.233) | copy-start | bytes 73732
  438.9 5.7 %copy-start.30 = (f32[96,64]{1,0:T(8,128)S(1)}, f32[96,64]{1,0:T(8,128)}, u32[]{:S(2)}) copy-start(f32[96,64]{1,0:T(8,128)} %get-tuple-element.235) | copy-start | bytes 73732
  438.9 5.7 %copy-start.29 = (f32[96,64]{1,0:T(8,128)S(1)}, f32[96,64]{1,0:T(8,128)}, u32[]{:S(2)}) copy-start(f32[96,64]{1,0:T(8,128)} %get-tuple-element.234) | copy-start | bytes 73732
  439.9 7.1 %collective-permute-start.5 = (f32[16,3840]{1,0:T(8,128)S(1)}, f32[16,3840]{1,0:T(8,128)S(1)}, u32[]{:S(2)}, u32[]{:S(2)}) collective-permute-start(f32[16,3840]{1,0:T(8,128)S(1)} %pad_maximum_fusion.6), channel_id=1, source_target_pairs={{0,16},{4,20},{8,24},{12,28},{16,0},{20,4},{24,8},{28,12},{1,17},{... | collective-permute-start | bytes 737288 | tf_op jit(solution)/shard_map/ppermute | solution.py:1294
  444.8 7.4 %copy-start.17 = (f32[96,128]{1,0:T(8,128)S(1)}, f32[96,128]{1,0:T(8,128)}, u32[]{:S(2)}) copy-start(f32[96,128]{1,0:T(8,128)} %get-tuple-element.220) | copy-start | bytes 147460
  444.8 7.4 %copy-start.18 = (f32[96,64]{1,0:T(8,128)S(1)}, f32[96,64]{1,0:T(8,128)}, u32[]{:S(2)}) copy-start(f32[96,64]{1,0:T(8,128)} %get-tuple-element.224) | copy-start | bytes 73732
  444.8 9.4 %copy-start.15 = (f32[96,128]{1,0:T(8,128)S(1)}, f32[96,128]{1,0:T(8,128)}, u32[]{:S(2)}) copy-start(f32[96,128]{1,0:T(8,128)} %get-tuple-element.228) | copy-start | bytes 147460
  444.8 9.4 %copy-start.16 = (f32[96,64]{1,0:T(8,128)S(1)}, f32[96,64]{1,0:T(8,128)}, u32[]{:S(2)}) copy-start(f32[96,64]{1,0:T(8,128)} %get-tuple-element.232) | copy-start | bytes 73732
  444.8 22.8 %copy-start.1 = (f32[256,768]{1,0:T(8,128)S(1)}, f32[256,768]{1,0:T(8,128)}, u32[]{:S(2)}) copy-start(f32[256,768]{1,0:T(8,128)} %param.35) | copy-start | bytes 2359300
  447.1 4.9 %collective-permute-start.6 = (f32[8,3840]{1,0:T(8,128)S(1)}, f32[8,3840]{1,0:T(8,128)S(1)}, u32[]{:S(2)}, u32[]{:S(2)}) collective-permute-start(f32[8,3840]{1,0:T(8,128)S(1)} %slice.442), channel_id=1, source_target_pairs={{0,8},{4,12},{8,0},{12,4},{16,24},{20,28},{24,16},{28,20},{1,9},{5... | collective-permute-start | bytes 368648 | tf_op jit(solution)/shard_map/ppermute | solution.py:1294
  452.1 1.3 collective-permute-start.7
  453.5 4.9 %collective-permute-start.8 = (f32[2,3840]{1,0:T(2,128)S(1)}, f32[2,3840]{1,0:T(2,128)S(1)}, u32[]{:S(2)}, u32[]{:S(2)}) collective-permute-start(f32[2,3840]{1,0:T(2,128)S(1)} %slice.446), channel_id=1, source_target_pairs={{0,2},{1,3},{2,0},{3,1},{4,6},{5,7},{6,4},{7,5},{8,10},{9,11},{10,... | collective-permute-start | bytes 92168 | tf_op jit(solution)/shard_map/ppermute | solution.py:1294
  458.4 3.8 collective-permute-start.9
  (3 other events, 7.7 us)
